TPU v7x, 32 devices: a whole 2x2x4 slice. The times are simulated.
32 devices in a mesh: grp: 4 (over z), tok: 8 (over y, x, core).
Axes of the slice: x: 2, y: 2, z: 4, core: 2. Of those that a mesh axis runs over, the one named last changes fastest.
Arguments:
- tokens: bfloat16 [8192, 2048], P(('grp', 'tok')), may hold values from -6 to 6
- cotangent: bfloat16 [8192, 2048], P(('grp', 'tok')), may hold values from -6 to 6
- norm_gain: bfloat16 [2048], P(('grp', 'tok')), may hold values from 0.099609375 to 1.8984375
- norm_bias: bfloat16 [2048], P(('grp', 'tok')), may hold values from -3 to 3
- joint_weight: bfloat16 [2048, 6144], P(('grp', 'tok')), may hold values from -0.125 to 0.125
- out_weight: bfloat16 [2048, 2048], P(('grp', 'tok')), may hold values from -2 to 2
- gate_weight: bfloat16 [2048, 5632], P(('grp', 'tok')), may hold values from -0.125 to 0.125
- up_weight: bfloat16 [2048, 5632], P(('grp', 'tok')), may hold values from -0.125 to 0.125
- down_weight: bfloat16 [5632, 2048], P(('grp', 'tok')), may hold values from -0.078125 to 0.078125
- block_table: int32 [4, 16], P('grp'), may hold values from 0 to 15, each once within a row
Outputs:
- result: bfloat16 [8192, 2048], P(('grp', 'tok'))
- input_grad: bfloat16 [8192, 2048], P(('grp', 'tok'))
- gain_grad: float32 [2048], P(('grp', 'tok'))
- bias_grad: float32 [2048], P(('grp', 'tok'))
- joint_grad: float32 [2048, 6144], P(('grp', 'tok'))
- out_grad: float32 [2048, 2048], P(('grp', 'tok'))
- gate_grad: float32 [2048, 5632], P(('grp', 'tok'))
- up_grad: float32 [2048, 5632], P(('grp', 'tok'))
- down_grad: float32 [5632, 2048], P(('grp', 'tok'))
Inputs may be any that keep to these rules, and one draw needn't show every extreme that they name: Each row of block_table is a permutation; value v in a slot of grp index r places there block v % 16 of group v // 16 of that index: a prompt block if v % 16 < 8, else one continuation.
All inputs are finite; a program needn't handle non-finite values.
Results may differ from a plain program's by a relative error of at most 0.012.
Values may be sent and summed in bfloat16 or wider, within the bound.
No kernel may reach another device: no remote copies, remote signals or barrier semaphores. Data moves between devices by JAX's collectives and lax.ppermute only.
A program may use at most 640 MiB of HBM per device.

v0:
```python
import jax
import jax.numpy as jnp
from jax import lax
from jax.sharding import PartitionSpec as P

HD = 64
ROT = 16
FF = 5632
BT = 128
PB = 8
BLK_GROUP = 16
PROMPT = 1024
KEY_BLK = 256


eps = 1e-05
neg_big = -1e30


def spread_blocks(values):
    return jnp.repeat(values, BT, axis=-1)


def token_tables(slots):
    part_of = slots % BLK_GROUP
    group_of = slots // BLK_GROUP
    is_prompt = part_of < PB
    begins = jnp.where(is_prompt, part_of * BT, PROMPT)
    offsets = jnp.arange(BT, dtype=jnp.int32)
    position = (begins[:, None] + offsets[None, :]).reshape(-1)
    return (position, spread_blocks(group_of), spread_blocks(part_of), spread_blocks(is_prompt))


def permitted(query_info, key_info):
    q_pos, q_grp, q_part = query_info
    k_pos, k_grp, k_part, k_prompt = key_info
    same = q_grp[:, None] == k_grp[None, :]
    causal = k_pos[None, :] <= q_pos[:, None]
    either = k_prompt[None, :] | (k_part[None, :] == q_part[:, None])
    return same & causal & either


def frequencies():
    return 10000.0 ** (-jnp.arange(0, ROT, 2, dtype=jnp.float32) / ROT)


def turn(values, cosine, sine):
    half = ROT // 2
    first = values[..., :half]
    second = values[..., half:ROT]
    return jnp.concatenate(
        [first * cosine - second * sine, second * cosine + first * sine, values[..., ROT:]], axis=-1
    )


def inner(left, right):
    return lax.dot_general(
        left, right, (((0,), (0,)), ((), ())), preferred_element_type=jnp.float32
    )


def body(
    tokens,
    cotangent,
    norm_gain,
    norm_bias,
    joint_weight,
    out_weight,
    gate_weight,
    up_weight,
    down_weight,
    block_table,
):
    rows = tokens.shape[0]
    width = tokens.shape[1]
    heads = width // HD
    scale = HD ** (-0.5)
    gathered = (
        lax.all_gather(norm_gain, ("grp", "tok"), axis=0, tiled=True),
        lax.all_gather(norm_bias, ("grp", "tok"), axis=0, tiled=True),
        lax.all_gather(joint_weight, ("grp", "tok"), axis=0, tiled=True),
        lax.all_gather(out_weight, ("grp", "tok"), axis=0, tiled=True),
        lax.all_gather(gate_weight, ("grp", "tok"), axis=0, tiled=True),
        lax.all_gather(up_weight, ("grp", "tok"), axis=0, tiled=True),
        lax.all_gather(down_weight, ("grp", "tok"), axis=0, tiled=True),
    )
    gain_full = gathered[0].astype(jnp.float32)
    bias_full = gathered[1].astype(jnp.float32)
    joint_full, out_full, gate_full, up_full, down_full = gathered[2:]
    position, group_tok, part_tok, prompt_tok = token_tables(block_table[0])
    first_row = lax.axis_index("tok") * rows

    def mine(values):
        return lax.dynamic_slice_in_dim(values, first_row, rows)

    query_info = (mine(position), mine(group_tok), mine(part_tok))
    inputs = tokens.astype(jnp.float32)
    mean = jnp.mean(inputs, axis=-1, keepdims=True)
    centred = inputs - mean
    inv_std = lax.rsqrt(jnp.mean(centred * centred, axis=-1, keepdims=True) + eps)
    normed = centred * inv_std
    hidden_in = (normed * gain_full + bias_full).astype(jnp.bfloat16)
    joint = jnp.dot(hidden_in, joint_full, preferred_element_type=jnp.float32)
    angles = query_info[0].astype(jnp.float32)[:, None] * frequencies()[None, :]
    cosine = jnp.cos(angles)[:, None, :]
    sine = jnp.sin(angles)[:, None, :]
    query = turn(joint[:, :width].reshape(rows, heads, HD), cosine, sine).astype(jnp.bfloat16)
    key_mine = (
        turn(joint[:, width : 2 * width].reshape(rows, heads, HD), cosine, sine)
        .astype(jnp.bfloat16)
        .reshape(rows, width)
    )
    value_mine = joint[:, 2 * width :].astype(jnp.bfloat16)
    key_all, value_all = (
        lax.all_gather(key_mine, "tok", axis=0, tiled=True),
        lax.all_gather(value_mine, "tok", axis=0, tiled=True),
    )
    blocks = key_all.shape[0] // KEY_BLK
    key_blocks = key_all.reshape(blocks, KEY_BLK, heads, HD)
    value_blocks = value_all.reshape(blocks, KEY_BLK, heads, HD)
    key_info = (
        position.reshape(blocks, KEY_BLK),
        group_tok.reshape(blocks, KEY_BLK),
        part_tok.reshape(blocks, KEY_BLK),
        prompt_tok.reshape(blocks, KEY_BLK),
    )

    def scores(key_block):
        return (
            jnp.einsum("qhd,khd->hqk", query, key_block, preferred_element_type=jnp.float32) * scale
        )

    def lse_step(carry, item):
        key_block = item[0]
        allowed = permitted(query_info, item[1:])
        masked = jnp.where(allowed[None], scores(key_block), neg_big)
        top = jnp.maximum(carry[0], jnp.max(masked, axis=2))
        terms = jnp.where(allowed[None], jnp.exp(masked - top[:, :, None]), 0.0)
        return ((top, carry[1] * jnp.exp(carry[0] - top) + jnp.sum(terms, axis=2)), None)

    start = (jnp.full((heads, rows), neg_big, jnp.float32), jnp.zeros((heads, rows), jnp.float32))
    (top_all, total_all), _ = lax.scan(lse_step, start, (key_blocks,) + key_info)
    log_total = top_all + jnp.log(total_all)

    def probabilities(raw, allowed):
        masked = jnp.where(allowed[None], raw, neg_big)
        return jnp.where(allowed[None], jnp.exp(masked - log_total[:, :, None]), 0.0)

    def out_step(carry, item):
        key_block, value_block = (item[0], item[1])
        allowed = permitted(query_info, item[2:])
        weights = probabilities(scores(key_block), allowed).astype(jnp.bfloat16)
        return (
            carry
            + jnp.einsum("hqk,khd->qhd", weights, value_block, preferred_element_type=jnp.float32),
            None,
        )

    attended, _ = lax.scan(
        out_step, jnp.zeros((rows, heads, HD), jnp.float32), (key_blocks, value_blocks) + key_info
    )
    attended = attended.reshape(rows, width)
    attended_low = attended.astype(jnp.bfloat16)
    branch_attn = jnp.dot(attended_low, out_full, preferred_element_type=jnp.float32)
    gate = jnp.dot(hidden_in, gate_full, preferred_element_type=jnp.float32)
    up = jnp.dot(hidden_in, up_full, preferred_element_type=jnp.float32)
    sigma = jax.nn.sigmoid(gate)
    swish = gate * sigma
    activated = (swish * up).astype(jnp.bfloat16)
    branch_ff = jnp.dot(activated, down_full, preferred_element_type=jnp.float32)
    result = (inputs + branch_attn + branch_ff).astype(jnp.bfloat16)
    again = (
        lax.all_gather(norm_gain, ("grp", "tok"), axis=0, tiled=True),
        lax.all_gather(joint_weight, ("grp", "tok"), axis=0, tiled=True),
        lax.all_gather(out_weight, ("grp", "tok"), axis=0, tiled=True),
        lax.all_gather(gate_weight, ("grp", "tok"), axis=0, tiled=True),
        lax.all_gather(up_weight, ("grp", "tok"), axis=0, tiled=True),
        lax.all_gather(down_weight, ("grp", "tok"), axis=0, tiled=True),
    )
    gain_back = again[0].astype(jnp.float32)
    joint_back, out_back, gate_back, up_back, down_back = again[1:]
    d_act = jnp.dot(cotangent, down_back.T, preferred_element_type=jnp.float32)
    d_gate = (d_act * up * sigma * (1.0 + gate * (1.0 - sigma))).astype(jnp.bfloat16)
    d_up = (d_act * swish).astype(jnp.bfloat16)
    d_attended = jnp.dot(cotangent, out_back.T, preferred_element_type=jnp.float32).astype(
        jnp.bfloat16
    )
    d_heads = d_attended.reshape(rows, heads, HD)
    delta = jnp.einsum(
        "qhd,qhd->hq", d_heads.astype(jnp.float32), attended.reshape(rows, heads, HD)
    )

    def back_step(carry, item):
        key_block, value_block = (item[0], item[1])
        allowed = permitted(query_info, item[2:])
        weights = probabilities(scores(key_block), allowed)
        d_value = jnp.einsum(
            "hqk,qhd->khd",
            weights.astype(jnp.bfloat16),
            d_heads,
            preferred_element_type=jnp.float32,
        )
        d_weights = jnp.einsum(
            "qhd,khd->hqk", d_heads, value_block, preferred_element_type=jnp.float32
        )
        d_scores = (weights * (d_weights - delta[:, :, None])).astype(jnp.bfloat16)
        d_query = (
            carry
            + jnp.einsum("hqk,khd->qhd", d_scores, key_block, preferred_element_type=jnp.float32)
            * scale
        )
        d_key = (
            jnp.einsum("hqk,qhd->khd", d_scores, query, preferred_element_type=jnp.float32) * scale
        )
        return (d_query, (d_key, d_value))

    d_query, (d_keys, d_values) = lax.scan(
        back_step, jnp.zeros((rows, heads, HD), jnp.float32), (key_blocks, value_blocks) + key_info
    )
    d_key_mine, d_value_mine = (
        lax.psum_scatter(
            d_keys.reshape(-1, width).astype(jnp.bfloat16), "tok", scatter_dimension=0, tiled=True
        ).astype(jnp.float32),
        lax.psum_scatter(
            d_values.reshape(-1, width).astype(jnp.bfloat16), "tok", scatter_dimension=0, tiled=True
        ).astype(jnp.float32),
    )
    d_query_turned = turn(d_query, cosine, -sine).reshape(rows, width)
    d_key_turned = turn(d_key_mine.reshape(rows, heads, HD), cosine, -sine).reshape(rows, width)
    d_joint = jnp.concatenate([d_query_turned, d_key_turned, d_value_mine], axis=1).astype(
        jnp.bfloat16
    )
    d_hidden = jnp.dot(d_joint, joint_back.T, preferred_element_type=jnp.float32)
    d_hidden = d_hidden + jnp.dot(d_gate, gate_back.T, preferred_element_type=jnp.float32)
    d_hidden = d_hidden + jnp.dot(d_up, up_back.T, preferred_element_type=jnp.float32)
    d_normed = d_hidden * gain_back
    d_inputs = inv_std * (
        d_normed
        - jnp.mean(d_normed, axis=-1, keepdims=True)
        - normed * jnp.mean(d_normed * normed, axis=-1, keepdims=True)
    )
    input_grad = (cotangent.astype(jnp.float32) + d_inputs).astype(jnp.bfloat16)
    down_term = inner(activated, cotangent)
    gain_term = jnp.sum(d_hidden * normed, axis=0)
    bias_term = jnp.sum(d_hidden, axis=0)
    joined = lax.psum_scatter(
        jnp.concatenate(
            [
                inner(hidden_in, d_joint),
                inner(attended_low, cotangent),
                inner(hidden_in, d_gate),
                inner(hidden_in, d_up),
            ],
            axis=1,
        ),
        ("grp", "tok"),
        scatter_dimension=0,
        tiled=True,
    )
    down_grad, gain_grad, bias_grad = (
        lax.psum_scatter(down_term, ("grp", "tok"), scatter_dimension=0, tiled=True),
        lax.psum_scatter(gain_term, ("grp", "tok"), scatter_dimension=0, tiled=True),
        lax.psum_scatter(bias_term, ("grp", "tok"), scatter_dimension=0, tiled=True),
    )
    joint_grad = joined[:, : 3 * width]
    out_grad = joined[:, 3 * width : 4 * width]
    gate_grad = joined[:, 4 * width : 4 * width + FF]
    up_grad = joined[:, 4 * width + FF :]
    return (
        result,
        input_grad,
        gain_grad,
        bias_grad,
        joint_grad,
        out_grad,
        gate_grad,
        up_grad,
        down_grad,
    )


def solution(mesh):
    placed = (
        P(("grp", "tok"), None),
        P(("grp", "tok"), None),
        P(("grp", "tok")),
        P(("grp", "tok")),
        P(("grp", "tok"), None),
        P(("grp", "tok"), None),
        P(("grp", "tok"), None),
        P(("grp", "tok"), None),
        P(("grp", "tok"), None),
        P("grp", None),
    )
    return jax.shard_map(
        body,
        mesh=mesh,
        in_specs=placed,
        out_specs=(
            P(("grp", "tok"), None),
            P(("grp", "tok"), None),
            P(("grp", "tok")),
            P(("grp", "tok")),
            P(("grp", "tok"), None),
            P(("grp", "tok"), None),
            P(("grp", "tok"), None),
            P(("grp", "tok"), None),
            P(("grp", "tok"), None),
        ),
        check_vma=False,
    )
```

profile of v0, /device:TPU:0, one launch (start us, length us, event | category | flops | bytes accessed | tf_op | source)
XLA Modules:
  0.0 3235.3 jit_solution(7060317920040438360)
XLA Ops:
  10.4 43.5 %all-reduce.5 = (bf16[2048]{0:T(1024)(128)(2,1)S(1)}, bf16[2048]{0:T(1024)(128)(2,1)S(1)}) all-reduce(bf16[2048]{0:T(1024)(128)(2,1)S(1)} %dynamic-update-slice.1, bf16[2048]{0:T(1024)(128)(2,1)S(1)} %dynamic-update-slice), channel_id=1, replica_groups=mesh['grp'=4,'tok'=8] {'grp','tok'}, use_global_device_ids=true, to_apply=%add.1 | all-reduce | flops 4096 | bytes 16384
  58.6 111.0 %all-gather.8.cloned.1.call-done = bf16[2048,6144]{1,0:T(8,128)(2,1)} async-done(((bf16[64,6144]{1,0:T(8,128)(2,1)}), bf16[2048,6144]{1,0:T(8,128)(2,1)}) %all-gather.8.cloned.1.call-update) | async-done | bytes 25165840 | tf_op jit(solution)/shard_map/all_gather | solution.py:81
  200.4 47.7 %all-gather.14.cloned.1.call-done = bf16[2048,2048]{1,0:T(8,128)(2,1)} async-done(((bf16[64,2048]{1,0:T(8,128)(2,1)}), bf16[2048,2048]{1,0:T(8,128)(2,1)}) %all-gather.14.cloned.1.call-update) | async-done | bytes 8388624 | tf_op jit(solution)/shard_map/all_gather | solution.py:82
  259.3 45.9 %all-gather.12.cloned.1.call-done = bf16[2048,2048]{0,1:T(8,128)(2,1)} async-done(((bf16[256,2048]{0,1:T(8,128)(2,1)}), bf16[2048,2048]{0,1:T(8,128)(2,1)}) %all-gather.12.cloned.1.call-update) | async-done | bytes 8388624 | tf_op jit(solution)/shard_map/all_gather | solution.py:115
  324.8 41.3 %while.39 = (s32[]{:T(128)}, f32[32,256]{1,0:T(8,128)S(1)}, f32[32,256]{1,0:T(8,128)S(1)}, s32[256]{0:T(256)S(1)}, s32[8,256]{1,0:T(8,128)S(1)}, /*index=5*/s32[...) while((s32[]{:T(128)}, f32[32,256]{1,0:T(8,128)S(1)}, ...), condition=%wide.region_5.6_spmd.clone, body=%wide.region_2.5_spmd.clone.sunk | while | flops 285646848 | bytes 19510184 | solution.py:142
  366.1 24.5 reshape.533
  390.6 19.5 copy.71
  410.1 52.5 %while.40 = (s32[]{:T(128)}, f32[256,32,64]{0,2,1:T(8,128)}, bf16[8,256,32,64]{1,3,2,0:T(8,128)(2,1)}, s32[256]{0:T(256)S(1)}, s32[8,256]{1,0:T(8,128)S(1)}, /*i...) while((s32[]{:T(128)}, f32[256,32,64]{0,2,1:T(8,128)}, ...), condition=%wide.region_7.8_spmd.clone, body=%wide.region_6.7_spmd.clone.sunk | while | flops 548798464 | bytes 7518634 | solution.py:159
  465.0 121.3 %while.41 = (s32[]{:T(128)}, f32[256,32,64]{0,2,1:T(8,128)S(1)}, bf16[8,256,32,64]{1,3,2,0:T(8,128)(2,1)}, bf16[8,256,32,64]{1,3,2,0:T(8,128)(2,1)}, bf16[8,256,...) while((s32[]{:T(128)}, f32[256,32,64]{0,2,1:T(8,128)S(1)}, ...), condition=%wide.region_9.10_spmd.clone, body=%wide.region_8.9_spmd.clone.sunk | while | flops 1369833472 | bytes 57979896 | solution.py:217
  586.3 15.7 copy.76
  612.8 15.3 copy.77
  640.4 13.7 fusion.81
  668.1 132.4 %all-gather.20.cloned.1.call-done = bf16[5632,2048]{1,0:T(8,128)(2,1)} async-done(((bf16[176,2048]{1,0:T(8,128)(2,1)}), bf16[5632,2048]{1,0:T(8,128)(2,1)}) %all-gather.20.cloned.1.call-update) | async-done | bytes 23068688 | tf_op jit(solution)/shard_map/all_gather | solution.py:85
  800.5 20.5 multiply_convert_fusion
  821.0 21.5 fusion.76
  842.5 20.8 fusion.78
  877.8 70.9 %reduce-scatter.7.cloned.1.call-done = bf16[256,2048]{0,1:T(8,128)(2,1)} async-done(((bf16[2048,2048]{0,1:T(8,128)(2,1)}), bf16[256,2048]{0,1:T(8,128)(2,1)}) %reduce-scatter.7.cloned.1.call-update) | async-done | bytes 1048592 | tf_op jit(solution)/shard_map/reduce_scatter | solution.py:224
  948.7 19.0 fusion.69
  967.7 102.9 %pad_maximum_fusion = f32[2048,19456]{1,0:T(8,128)} fusion(f32[2048,5632]{1,0:T(8,128)} %fusion.76, f32[2048,5632]{1,0:T(8,128)} %fusion.78, f32[2048,2048]{1,0:T(8,128)} %fusion.90, f32[2048,6144]{1,0:T(8,128)} %fusion.69), kind=kLoop, calls=%fused_computation.67 | loop fusion | flops 119537664 | bytes 318767104 | tf_op jit(solution)/shard_map/concatenate | solution.py:247
  1071.8 20.6 fusion.91
  1125.7 13.5 convolution_add_fusion.1
  1152.6 45.2 %all-reduce.4 = (f32[2048]{0:T(1024)S(1)}, f32[2048]{0:T(1024)S(1)}) all-reduce(f32[2048]{0:T(1024)S(1)} %get-tuple-element.483, f32[2048]{0:T(1024)S(1)} %get-tuple-element.486), channel_id=4, replica_groups=mesh['grp'=4,'tok'=8] {'grp','tok'}, use_global_device_ids=true, to_apply=%region_15.16.clone | all-reduce | flops 4096 | bytes 32768
  1202.5 1529.1 %reduce-scatter.9.cloned.1.call-done = f32[64,19456]{1,0:T(8,128)} async-done(((f32[2048,19456]{1,0:T(8,128)}), f32[64,19456]{1,0:T(8,128)}) %reduce-scatter.9.cloned.1.call-update) | async-done | bytes 4980752 | tf_op jit(solution)/shard_map/reduce_scatter | solution.py:246
  2739.7 488.9 %reduce-scatter.11.cloned.1.call-done = f32[176,2048]{1,0:T(8,128)} async-done(((f32[5632,2048]{1,0:T(8,128)}), f32[176,2048]{1,0:T(8,128)}) %reduce-scatter.11.cloned.1.call-update) | async-done | bytes 1441808 | tf_op jit(solution)/shard_map/reduce_scatter | solution.py:261
  (361 shorter events, 397.3 us)
Async XLA Ops:
  7.2 162.4 %copy-start = (bf16[256,2048]{1,0:T(8,128)(2,1)S(1)}, bf16[256,2048]{1,0:T(8,128)(2,1)}, u32[]{:S(2)}) copy-start(bf16[256,2048]{1,0:T(8,128)(2,1)} %param.16) | copy-start | bytes 3145732
  7.2 162.4 %all-gather.8.cloned.1.call-start = ((), (), s32[]{:S(2)}) async-start(), calls=%async_computation.4 | async-start | bytes 25952256 | tf_op jit(solution)/shard_map/all_gather | solution.py:81
  7.9 240.3 %all-gather.14.cloned.1.call-start = ((), (), s32[]{:S(2)}) async-start(), calls=%async_computation.7 | async-start | bytes 8650752 | tf_op jit(solution)/shard_map/all_gather | solution.py:82
  8.7 296.5 %all-gather.12.cloned.1.call-start = ((), (), s32[]{:S(2)}) async-start(), calls=%async_computation.6 | async-start | bytes 9437184 | tf_op jit(solution)/shard_map/all_gather | solution.py:115
  53.9 115.7 %copy-start.18 = (f32[2048]{0:T(1024)}, f32[2048]{0:T(1024)S(1)}, u32[]{:S(2)}) copy-start(f32[2048]{0:T(1024)S(1)} %convert_element_type.77) | copy-start | bytes 24580
  53.9 115.7 %copy-start.15 = (f32[2048]{0:T(1024)}, f32[2048]{0:T(1024)S(1)}, u32[]{:S(2)}) copy-start(f32[2048]{0:T(1024)S(1)} %convert_element_type.76) | copy-start | bytes 24580
  56.2 113.4 %copy-start.20 = (f32[256]{0:T(256)}, f32[256]{0:T(256)S(1)}, u32[]{:S(2)}) copy-start(f32[256]{0:T(256)S(1)} %broadcast_multiply_fusion.2) | copy-start | bytes 3076
  57.9 111.7 %copy-start.23 = (f32[256]{0:T(256)}, f32[256]{0:T(256)S(1)}, u32[]{:S(2)}) copy-start(f32[256]{0:T(256)S(1)} %add_rsqrt_fusion) | copy-start | bytes 3076
  58.6 132.4 %copy-start.26 = (f32[256,8]{0,1:T(8,128)}, f32[256,8]{0,1:T(8,128)S(1)}, u32[]{:S(2)}) copy-start(f32[256,8]{0,1:T(8,128)S(1)} %get-tuple-element.610) | copy-start | bytes 24580
  193.5 54.7 %copy-start.5 = (bf16[256,2048]{1,0:T(8,128)(2,1)S(1)}, bf16[256,2048]{1,0:T(8,128)(2,1)}, u32[]{:S(2)}) copy-start(bf16[256,2048]{1,0:T(8,128)(2,1)} %param.17) | copy-start | bytes 3145732
  193.5 172.6 %all-gather.10.cloned.1.call-start = ((), (), s32[]{:S(2)}) async-start(), calls=%async_computation.5 | async-start | bytes 9437184 | tf_op jit(solution)/shard_map/all_gather | solution.py:116
  196.4 442.9 %all-gather.18.cloned.1.call-start = ((), (), s32[]{:S(2)}) async-start(), calls=%async_computation.9 | async-start | bytes 23789568 | tf_op jit(solution)/shard_map/all_gather | solution.py:84
  197.0 457.9 %all-gather.16.cloned.1.call-start = ((), (), s32[]{:S(2)}) async-start(), calls=%async_computation.8 | async-start | bytes 23789568 | tf_op jit(solution)/shard_map/all_gather | solution.py:83
  197.5 603.0 %all-gather.20.cloned.1.call-start = ((), (), s32[]{:S(2)}) async-start(), calls=%async_computation.10 | async-start | bytes 23789568 | tf_op jit(solution)/shard_map/all_gather | solution.py:85
  198.3 676.3 %reduce-scatter.5.cloned.1.call-start = ((), (), s32[]{:S(2)}) async-start(), calls=%async_computation.11 | async-start | bytes 9437184 | tf_op jit(solution)/shard_map/reduce_scatter | solution.py:221
  612.8 335.9 %reduce-scatter.7.cloned.1.call-start = ((), (), s32[]{:S(2)}) async-start(), calls=%async_computation.12 | async-start | bytes 9437184 | tf_op jit(solution)/shard_map/reduce_scatter | solution.py:224
  639.2 2092.4 %reduce-scatter.9.cloned.1.call-start = ((), (), s32[]{:S(2)}) async-start(), calls=%async_computation.13 | async-start | bytes 164364288 | tf_op jit(solution)/shard_map/reduce_scatter | solution.py:246
  877.6 90.0 %copy-start.11 = (bf16[256,32,64]{0,2,1:T(8,128)(2,1)}, bf16[256,32,64]{0,2,1:T(8,128)(2,1)S(1)}, u32[]{:S(2)}) copy-start(bf16[256,32,64]{0,2,1:T(8,128)(2,1)S(1)} %pad_maximum_fusion.6) | copy-start | bytes 3145732
  877.8 89.9 %copy-start.13 = (bf16[256,32,64]{0,2,1:T(8,128)(2,1)}, bf16[256,32,64]{0,2,1:T(8,128)(2,1)S(1)}, u32[]{:S(2)}) copy-start(bf16[256,32,64]{0,2,1:T(8,128)(2,1)S(1)} %pad_maximum_fusion.7) | copy-start | bytes 3145732
  1070.6 2158.0 %reduce-scatter.11.cloned.1.call-start = ((), (), s32[]{:S(2)}) async-start(), calls=%async_computation.14 | async-start | bytes 47579136 | tf_op jit(solution)/shard_map/reduce_scatter | solution.py:261
  1100.0 12.2 copy-start.12
  1125.7 13.5 copy-start.17
  1125.7 13.5 copy-start.22
  1125.7 13.5 copy-start.25
  (24 other events, 58.7 us)
Sparse Core Ops, SparseCore 0:
  10.9 158.6 all-gather.7
  172.5 75.6 all-gather.13
  250.6 54.5 all-gather.11
  307.5 54.4 all-gather.9
  364.7 144.6 all-gather.17
  512.1 142.7 all-gather.15
  657.7 142.7 all-gather.19
  804.0 69.4 reduce-scatter.4
  877.3 71.2 reduce-scatter.6
  1070.7 1660.8 reduce-scatter.8
  2734.6 493.9 reduce-scatter.10
where the time goes:
time: 3250 us; the launch traced here: 3240 us
  waiting for transfers between devices  2430 us (75%)
  matrix products  405 us (12%)
  local copies, waits for them, and re-layouts  153 us (5%)
  other arithmetic  142 us (4%)
  blocking collectives  88.7 us (3%)
    reduce_scatter x1, waiting for transfers between devices, body(): lax.psum_scatter(jnp.concatenate([inner(hidden_in, d_joint), inner(attend...  1530 us
    reduce_scatter x1, waiting for transfers between devices, body(): lax.psum_scatter(down_term, ('grp', 'tok'), scatter_dimension=0, tiled=True)  489 us
    all_gather x1, waiting for transfers between devices, body(): lax.all_gather(down_weight, ('grp', 'tok'), axis=0, tiled=True)  132 us
    all_gather x1, waiting for transfers between devices, body(): lax.all_gather(joint_weight, ('grp', 'tok'), axis=0, tiled=True)  111 us
    concatenate x1, other arithmetic, body(): jnp.concatenate([inner(hidden_in, d_joint), inner(attended_low, cotangent...  103 us
    dot_general x5, matrix products, inner(): lax.dot_general(left, right, (((0,), (0,)), ((), ())), preferred_element_...  90.1 us
    unnamed x2, blocking collectives  88.7 us
    reduce_scatter x1, waiting for transfers between devices, body(): lax.psum_scatter(d_values.reshape(-1, width).astype(jnp.bfloat16), 'tok',...  70.9 us
  transfers between devices with their start and end apart: 11, of which 8 were waited for; matrix products, arithmetic and copies ran while one was open for 18% of the time, Pallas kernels for 0%

commit v1 on v0

v1 whole, which is shorter than its diff:
```python
import functools

import jax
import jax.numpy as jnp
from jax import lax
from jax.experimental import pallas as pl
from jax.experimental.pallas import tpu as pltpu
from jax.sharding import PartitionSpec as P

HD = 64
ROT = 16
BT = 128
PB = 8
BLK_GROUP = 16
LANES = 128
QT = 2 * BT

eps = 1e-05
neg_big = -1e30
bf16 = jnp.bfloat16
f32 = jnp.float32
both = ("grp", "tok")
no_cost = pl.CostEstimate(flops=0, transcendentals=0, bytes_accessed=0)


def matmul(left, right):
    return jnp.dot(left, right, preferred_element_type=f32)


def matmul_nt(left, right):
    return lax.dot_general(left, right, (((1,), (1,)), ((), ())), preferred_element_type=f32)


def matmul_tn(left, right):
    return lax.dot_general(left, right, (((0,), (0,)), ((), ())), preferred_element_type=f32)


def rotary_tables():
    positions = (PB + 1) * BT
    freq = 10000.0 ** (-jnp.arange(0, ROT, 2, dtype=f32) / ROT)
    angles = jnp.arange(positions, dtype=jnp.int32).astype(f32)[:, None] * freq[None, :]
    cosine, sine = jnp.cos(angles), jnp.sin(angles)
    rest = jnp.zeros((positions, HD - ROT), f32)
    none = jnp.zeros_like(sine)

    def widen(parts):
        one = jnp.concatenate(parts, axis=1)
        return jnp.concatenate([one] * (LANES // HD), axis=1)

    keep = widen([cosine, cosine, rest + 1.0])
    below = widen([-sine, none, rest])
    above = widen([none, sine, rest])
    return keep, below, above


def attention_kernel(
    place, joint, d_out, keep, below, above, out, d_joint, qs, ks, vs, ds, d_key, d_value
):
    head = pl.program_id(0)
    half = head % 2
    lane_block = head // 2
    span = d_out.shape[1]
    lanes = [pl.ds(pl.multiple_of(c * span + lane_block * LANES, LANES), LANES) for c in range(3)]
    mine = lax.broadcasted_iota(jnp.int32, (BT, LANES), 1) // HD == half

    def turned(values, part, sign):
        row = min(part, PB) * BT
        c, b, a = (t[row : row + BT, :] for t in (keep, below, above))
        up = pltpu.roll(values, LANES - ROT // 2, 1)
        down = pltpu.roll(values, ROT // 2, 1)
        return values * c + sign * (up * b + down * a)

    def rows_of(part):
        return pl.ds(pl.multiple_of(place[part] * BT, BT), BT)

    for part in range(BLK_GROUP):
        rows = rows_of(part)
        here = pl.ds(part * BT, BT)
        query = turned(joint[rows, lanes[0]], part, 1.0).astype(bf16) * HD ** (-0.5)
        key = turned(joint[rows, lanes[1]], part, 1.0).astype(bf16)
        qs[here, :] = jnp.where(mine, query, 0).astype(bf16)
        ks[here, :] = jnp.where(mine, key, 0).astype(bf16)
        vs[here, :] = jnp.where(mine, joint[rows, lanes[2]].astype(bf16), 0).astype(bf16)
        ds[here, :] = jnp.where(mine, d_out[rows, lanes[0]], 0).astype(bf16)
    d_key[...] = jnp.zeros_like(d_key)
    d_value[...] = jnp.zeros_like(d_value)

    def put(ref, rows, where, values):
        @pl.when(half == 0)
        def _():
            ref[rows, where] = values

        @pl.when(half != 0)
        def _():
            ref[rows, where] = jnp.where(mine, values, ref[rows, where]).astype(ref.dtype)

    row_id = lax.broadcasted_iota(jnp.int32, (QT, QT), 0)
    col_id = lax.broadcasted_iota(jnp.int32, (QT, QT), 1)
    causal = row_id >= col_id
    alone = causal & (row_id // BT == col_id // BT)

    def tile(index, shared, allowed):
        start = index * QT
        own = pl.ds(start, QT)
        query, d_o = qs[own, :], ds[own, :]
        spans = [own] + ([pl.ds(0, shared)] if shared else [])
        raw = [matmul_nt(query, ks[s, :]) for s in spans]
        raw[0] = jnp.where(allowed, raw[0], neg_big)
        top = functools.reduce(jnp.maximum, [jnp.max(r, axis=1, keepdims=True) for r in raw])
        terms = [jnp.exp(r - top) for r in raw]
        total = functools.reduce(jnp.add, [jnp.sum(t, axis=1, keepdims=True) for t in terms])
        inverse = 1.0 / total
        weights = [t * inverse for t in terms]
        low = [w.astype(bf16) for w in weights]
        attended = functools.reduce(jnp.add, [matmul(w, vs[s, :]) for w, s in zip(low, spans)])
        delta = jnp.sum(attended * d_o.astype(f32), axis=1, keepdims=True)
        d_scores = [
            (w * (matmul_nt(d_o, vs[s, :]) - delta)).astype(bf16) for w, s in zip(weights, spans)
        ]
        d_query = functools.reduce(jnp.add, [matmul(d, ks[s, :]) for d, s in zip(d_scores, spans)])
        d_query = d_query * HD ** (-0.5)
        for s, d, w in zip(spans, d_scores, low):
            d_key[s, :] += matmul_tn(d, query)
            d_value[s, :] += matmul_tn(w, d_o)
        for k in range(QT // BT):
            part = index * (QT // BT) + k
            rows = rows_of(part)
            piece = slice(k * BT, (k + 1) * BT)
            put(out, rows, lanes[0], attended[piece, :].astype(bf16))
            put(d_joint, rows, lanes[0], turned(d_query[piece, :], part, -1.0).astype(bf16))

    prompt_tiles = PB * BT // QT
    for index in range(BLK_GROUP * BT // QT):
        if index < prompt_tiles:
            tile(index, index * QT, causal)
        else:
            tile(index, PB * BT, alone)
    for part in range(BLK_GROUP):
        here = pl.ds(part * BT, BT)
        rows = rows_of(part)
        put(d_joint, rows, lanes[1], turned(d_key[here, :], part, -1.0).astype(bf16))
        put(d_joint, rows, lanes[2], d_value[here, :].astype(bf16))


def attention(place, joint, d_out, tables):
    count, span = d_out.shape
    full = lambda shape: pl.BlockSpec(shape, lambda h, p: (0,) * len(shape))
    scratch = [pltpu.VMEM((count, LANES), bf16)] * 4 + [pltpu.VMEM((count, LANES), f32)] * 2
    return pl.pallas_call(
        attention_kernel,
        grid_spec=pltpu.PrefetchScalarGridSpec(
            num_scalar_prefetch=1,
            grid=(span // HD,),
            in_specs=[full(joint.shape), full(d_out.shape)] + [full(t.shape) for t in tables],
            out_specs=[full((count, span)), full((count, 3 * span))],
            scratch_shapes=scratch,
        ),
        out_shape=[
            jax.ShapeDtypeStruct((count, span), bf16),
            jax.ShapeDtypeStruct((count, 3 * span), bf16),
        ],
        compiler_params=pltpu.CompilerParams(vmem_limit_bytes=48 * 2**20),
        cost_estimate=no_cost,
    )(place, joint, d_out, *tables)


def after(values, *earlier):
    return lax.optimization_barrier((values, earlier))[0]


def gather_pieces(values):
    toks = lax.axis_size("tok")
    bits = toks.bit_length() - 1
    paths = values.shape[0] // BT
    orders = [list(range(1, bits)) + [0], list(range(bits - 1, 0, -1)) + [0]]
    held = list(jnp.split(values, paths))
    found = []
    for step in range(bits):
        swaps = [[(i, i ^ (1 << orders[p % 2][step])) for i in range(toks)] for p in range(paths)]
        got = [lax.ppermute(h, "tok", s) for h, s in zip(held, swaps)]
        if step == bits - 1:
            found = [piece for pair in zip(held, got) for piece in pair]
        else:
            held = [jnp.concatenate(pair) for pair in zip(held, got)]
    return found, orders[:paths]


def order_of(orders):
    found = []
    for half, order in enumerate(orders):
        for q in range(1 << len(order)):
            found.append((sum(1 << b for k, b in enumerate(order) if q >> k & 1), half))
    return found


def assemble_kernel(count, norm, *refs):
    pieces, refs = refs[:count], refs[count:]
    step = pl.program_id(0)
    each = pl.num_programs(0) // count
    for k, piece in enumerate(pieces):

        @pl.when(step // each == k)
        def _():
            if norm:
                gain, bias, out = refs
                values = piece[...].astype(f32)
                centred = values - jnp.mean(values, axis=-1, keepdims=True)
                spread = jnp.mean(centred * centred, axis=-1, keepdims=True)
                out[...] = (centred * lax.rsqrt(spread + eps) * gain[...] + bias[...]).astype(bf16)
            else:
                refs[-1][...] = piece[...]


def assemble(pieces, *norm):
    tall, width = pieces[0].shape
    block = min(tall, QT)
    each = tall // block
    total = tall * len(pieces)

    def piece_block(k):
        return pl.BlockSpec((block, width), lambda i: (jnp.clip(i - k * each, 0, each - 1), 0))

    return pl.pallas_call(
        functools.partial(assemble_kernel, len(pieces), bool(norm)),
        grid=(total // block,),
        in_specs=[piece_block(k) for k in range(len(pieces))]
        + [pl.BlockSpec((1, width), lambda i: (0, 0)) for _ in norm],
        out_specs=pl.BlockSpec((block, width), lambda i: (i, 0)),
        out_shape=jax.ShapeDtypeStruct((total, width), bf16),
        compiler_params=pltpu.CompilerParams(vmem_limit_bytes=48 * 2**20),
        cost_estimate=no_cost,
    )(*pieces, *norm)


def sum_kernel(count, transposed, *refs):
    product = matmul_nt if transposed else matmul
    terms = [product(refs[k][...], refs[count + k][...]) for k in range(count)]
    refs[-1][...] = functools.reduce(jnp.add, terms).astype(bf16)


def sum_of_products(lefts, rights, transposed):
    rows = lefts[0].shape[0]
    cols = rights[0].shape[0 if transposed else 1]
    inner = sum(v.shape[1] for v in lefts)
    block = QT
    return pl.pallas_call(
        functools.partial(sum_kernel, len(lefts), transposed),
        grid=(rows // block,),
        in_specs=[pl.BlockSpec((block, v.shape[1]), lambda i: (i, 0)) for v in lefts]
        + [pl.BlockSpec(v.shape, lambda i: (0, 0), pipeline_mode=pl.Buffered(1)) for v in rights],
        out_specs=pl.BlockSpec((block, cols), lambda i: (i, 0)),
        out_shape=jax.ShapeDtypeStruct((rows, cols), bf16),
        compiler_params=pltpu.CompilerParams(vmem_limit_bytes=48 * 2**20),
        cost_estimate=no_cost,
    )(*lefts, *rights)


def feed_kernel(hidden, d_result, up_weight, down_weight, act, d_both):
    wide = act.shape[1]
    both_here = matmul(hidden[...], up_weight[...])
    d_act = matmul_nt(d_result[...], down_weight[...])
    gate, up = both_here[:, :wide], both_here[:, wide:]
    sigma = jax.nn.sigmoid(gate)
    swish = gate * sigma
    act[...] = (swish * up).astype(bf16)
    d_gate = d_act * up * sigma * (1.0 + gate * (1.0 - sigma))
    d_both[...] = jnp.concatenate([d_gate, d_act * swish], axis=1).astype(bf16)


def feed_forward(hidden, d_result, up_weight, down_weight):
    rows, width = hidden.shape
    wide = down_weight.shape[0]
    fixed = lambda w: pl.BlockSpec(w.shape, lambda i: (0, 0), pipeline_mode=pl.Buffered(1))
    return pl.pallas_call(
        feed_kernel,
        grid=(rows // QT,),
        in_specs=[pl.BlockSpec((QT, width), lambda i: (i, 0))] * 2
        + [fixed(up_weight), fixed(down_weight)],
        out_specs=[
            pl.BlockSpec((QT, wide), lambda i: (i, 0)),
            pl.BlockSpec((QT, 2 * wide), lambda i: (i, 0)),
        ],
        out_shape=[
            jax.ShapeDtypeStruct((rows, wide), bf16),
            jax.ShapeDtypeStruct((rows, 2 * wide), bf16),
        ],
        compiler_params=pltpu.CompilerParams(vmem_limit_bytes=48 * 2**20),
        cost_estimate=no_cost,
    )(hidden, d_result, up_weight, down_weight)


def outer_kernel(left, right, out):
    out[...] = matmul_tn(left[...], right[...]).astype(bf16)


def outer_product(left, right):
    rows, tall = left.shape
    wide = right.shape[1]
    return pl.pallas_call(
        outer_kernel,
        grid=(tall // QT,),
        in_specs=[
            pl.BlockSpec((rows, QT), lambda i: (0, i)),
            pl.BlockSpec((rows, wide), lambda i: (0, 0), pipeline_mode=pl.Buffered(1)),
        ],
        out_specs=pl.BlockSpec((QT, wide), lambda i: (i, 0)),
        out_shape=jax.ShapeDtypeStruct((tall, wide), bf16),
        compiler_params=pltpu.CompilerParams(vmem_limit_bytes=48 * 2**20),
        cost_estimate=no_cost,
    )(left, right)


def scatter_pieces(values, orders):
    toks = lax.axis_size("tok")
    bits = toks.bit_length() - 1
    held = list(jnp.split(values, len(orders)))
    for step in range(bits - 1, -1, -1):
        sent = [h[h.shape[0] // 2 :] for h in held]
        swaps = [[(i, i ^ (1 << order[step])) for i in range(toks)] for order in orders]
        got = [lax.ppermute(v, "tok", w) for v, w in zip(sent, swaps)]
        held = [
            h[: h.shape[0] // 2].astype(f32) + g.astype(f32) for h, g in zip(held, got)
        ]
        if step:
            held = [h.astype(bf16) for h in held]
    return jnp.concatenate(held)


def gather_grp(values):
    return lax.all_gather(values, "grp", axis=0, tiled=True)


def scatter_grp(values):
    return lax.psum_scatter(values.astype(bf16), "grp", scatter_dimension=0, tiled=True)


def swap_tok(values):
    return lax.all_to_all(values, "tok", 0, 0)


def split_kernel(outer, *refs):
    sources, out = refs[:-1], refs[-1]
    toks = out.shape[0]
    for tok in range(toks):
        pieces = []
        for source in sources:
            inner = source.shape[1] // (outer * toks)
            values = source[...]
            for k in range(outer):
                start = (k * toks + tok) * inner
                pieces.append(values[:, start : start + inner])
        out[tok] = jnp.concatenate(pieces, axis=1)


def split_columns(weights, outer, toks):
    rows = weights[0].shape[0]
    cols = sum(w.shape[1] for w in weights) // toks
    return pl.pallas_call(
        functools.partial(split_kernel, outer),
        out_shape=jax.ShapeDtypeStruct((toks, rows, cols), weights[0].dtype),
        compiler_params=pltpu.CompilerParams(vmem_limit_bytes=32 * 2**20),
    )(*weights)


def join_kernel(outer, source, *outs):
    toks = source.shape[0]
    offset = 0
    for out in outs:
        inner = out.shape[1] // (outer * toks)
        pieces = []
        for k in range(outer):
            for tok in range(toks):
                start = offset + k * inner
                pieces.append(source[tok, :, start : start + inner].astype(f32))
        out[...] = jnp.concatenate(pieces, axis=1)
        offset += outer * inner


def join_columns(parts, outer, count):
    toks, rows, cols = parts.shape
    shape = jax.ShapeDtypeStruct((rows, toks * cols // count), f32)
    return pl.pallas_call(
        functools.partial(join_kernel, outer),
        out_shape=[shape] * count,
        compiler_params=pltpu.CompilerParams(vmem_limit_bytes=32 * 2**20),
    )(parts)


def body(
    tokens,
    cotangent,
    norm_gain,
    norm_bias,
    joint_weight,
    out_weight,
    gate_weight,
    up_weight,
    down_weight,
    block_table,
):
    grps, toks = lax.axis_size("grp"), lax.axis_size("tok")
    devices = grps * toks
    rows, width = tokens.shape
    own_heads = width // HD // toks
    span = own_heads * HD
    wide = gate_weight.shape[1] // toks
    tok = lax.axis_index("tok")

    pair = jnp.stack([norm_gain, norm_bias])
    pair = lax.all_to_all(jnp.broadcast_to(pair[None], (devices,) + pair.shape), both, 0, 0)
    gain = pair[:, 0].reshape(width).astype(f32)
    bias = pair[:, 1].reshape(width).astype(f32)

    whole_heads = out_weight.shape[0] == HD
    if whole_heads:
        first = gather_grp(jnp.concatenate([down_weight, out_weight]))
        first = first.reshape(grps, -1, width)
        down_w = first[:, : down_weight.shape[0]].reshape(-1, width)
        out_w = first[:, down_weight.shape[0] :].reshape(-1, width)
    else:
        down_w = first = gather_grp(down_weight)
        out_w = lax.all_gather(out_weight, both, axis=0, tiled=True)
        out_w = lax.dynamic_index_in_dim(
            out_w.reshape(own_heads, toks, HD, width), tok, 1, keepdims=False
        ).reshape(span, width)
    gate_up_own = swap_tok(split_columns([gate_weight, up_weight], grps, toks))
    gate_up_w = gather_grp(after(gate_up_own.reshape(-1, 2 * wide), first))
    pieces, orders = gather_pieces(after(tokens, gate_up_own))
    hidden = assemble(pieces, gain[None], bias[None])
    d_pieces, _ = gather_pieces(after(cotangent, *pieces))
    dy = assemble(d_pieces)
    slots = jnp.argsort(block_table[0] % BLK_GROUP).astype(jnp.int32)
    halves = len(orders)
    spots = [(tok ^ apart) * halves + half for apart, half in order_of(orders)]
    place = jnp.argsort(jnp.stack(spots))[slots].astype(jnp.int32)
    tables = rotary_tables()
    d_attended = matmul_nt(dy, out_w).astype(bf16)
    joint_own = split_columns(
        [after(joint_weight, hidden, dy, d_attended, place, *tables)], 3 * own_heads, toks
    )
    joint_own = swap_tok(joint_own).reshape(-1, 3 * span)
    joint_w = gather_grp(after(joint_own, gate_up_w))

    activated, d_gate_up = feed_forward(hidden, dy, gate_up_w, down_w)
    gate_up_term = outer_product(hidden, d_gate_up)
    gate_up_grad = scatter_grp(after(gate_up_term, joint_w))
    down_term = matmul_tn(after(activated, joint_w), dy).astype(bf16)

    joint = matmul(after(hidden, gate_up_term), joint_w)
    attended, d_joint = attention(place, joint, after(d_attended, down_term), tables)
    down_grad = scatter_grp(after(down_term, gate_up_grad, d_joint))
    joint_term = matmul_tn(hidden, d_joint).astype(bf16)
    out_term = matmul_tn(attended, dy).astype(bf16)
    if whole_heads:
        tall = width // grps
        out_term = out_term.reshape(grps, -1, width).reshape(grps * tall, -1)
        joined = jnp.concatenate([joint_term, out_term], axis=1)
        joined = scatter_grp(after(joined, down_grad))
        joint_grad = joined[:, : 3 * span]
        out_grad = joined[:, 3 * span :].reshape(-1, width).astype(f32)
    else:
        joint_grad = scatter_grp(after(joint_term, down_grad))
        spread = jnp.zeros((own_heads, toks, HD, width), bf16)
        spread = lax.dynamic_update_index_in_dim(
            spread, out_term.reshape(own_heads, 1, HD, width), tok, 1
        )
        out_grad = lax.psum_scatter(
            spread.reshape(width, width), both, scatter_dimension=0, tiled=True
        ).astype(f32)
    d_hidden = sum_of_products(
        [after(d_joint, gate_up_grad, joint_term, out_term), d_gate_up], [joint_w, gate_up_w], True
    )
    branch = sum_of_products([after(attended, d_hidden), activated], [out_w, down_w], False)
    d_hidden = scatter_pieces(d_hidden, orders)
    result = (tokens.astype(f32) + scatter_pieces(branch, orders)).astype(bf16)
    tokens_wide = tokens.astype(f32)
    centred = tokens_wide - jnp.mean(tokens_wide, axis=-1, keepdims=True)
    inv_std = lax.rsqrt(jnp.mean(centred * centred, axis=-1, keepdims=True) + eps)
    normed = centred * inv_std
    d_normed = d_hidden * gain
    d_inputs = inv_std * (
        d_normed
        - jnp.mean(d_normed, axis=-1, keepdims=True)
        - normed * jnp.mean(d_normed * normed, axis=-1, keepdims=True)
    )
    input_grad = (cotangent.astype(f32) + d_inputs).astype(bf16)
    sums = jnp.stack([jnp.sum(d_hidden * normed, axis=0), jnp.sum(d_hidden, axis=0)])
    sums = lax.all_to_all(sums.reshape(2, devices, -1).transpose(1, 0, 2), both, 0, 0)
    sums = jnp.sum(sums, axis=0)

    def owned(grad, outer, count):
        return join_columns(swap_tok(grad.reshape(toks, -1, grad.shape[1])), outer, count)

    return (
        result,
        input_grad,
        sums[0],
        sums[1],
        *owned(joint_grad, 3 * own_heads, 1),
        out_grad,
        *owned(gate_up_grad, grps, 2),
        down_grad.astype(f32),
    )


def solution(mesh):
    sharded = P(("grp", "tok"), None)
    vector = P(("grp", "tok"))
    return jax.shard_map(
        body,
        mesh=mesh,
        in_specs=(sharded, sharded, vector, vector) + (sharded,) * 5 + (P("grp", None),),
        out_specs=(sharded, sharded, vector, vector) + (sharded,) * 5,
        check_vma=False,
    )
```

time: 3250 us -> 590 us (0.18)
  waiting for transfers between devices: 2430 us -> 172 us
  matrix products: 405 us -> 46.6 us
  Pallas kernels: 0 us -> 176 us
  local copies, waits for them, and re-layouts: 153 us -> 53.5 us
  other arithmetic: 142 us -> 47.5 us
  blocking collectives: 88.7 us -> 41.2 us
  starting transfers between devices: 0.44 us -> 33.3 us
    reduce_scatter x4 -> x3, waiting for transfers between devices: 2090 us -> 18.4 us  [scatter_grp(): lax.psum_scatter(values.astype(bf16), 'grp', scatter_dimension=0, tiled=T...]
    dot_general x71 -> x5, matrix products: 405 us -> 46.6 us  [the longest x3 28 us: matmul_tn(): lax.dot_general(left, right, (((0,), (0,)), ((), ())), preferred_element_...]
    all_gather x7 -> x3, waiting for transfers between devices: 338 us -> 26.4 us  [gather_grp(): return lax.all_gather(values, 'grp', axis=0, tiled=True)]
    pallas_call x0 -> x11, Pallas kernels: none -> 176 us  [the longest x1 67.6 us: attention(): pl.pallas_call(attention_kernel, grid_spec=pltpu.PrefetchScalarGridSpec(n...]
    ppermute x0 -> x24, waiting for transfers between devices: none -> 120 us  [the longest x12 71.2 us: gather_pieces(): got = [lax.ppermute(h, 'tok', s) for h, s in zip(held, swaps)]]
    concatenate x5 -> x10, other arithmetic: 104 us -> 11.2 us  [the longest x8 6.59 us: gather_pieces(): held = [jnp.concatenate(pair) for pair in zip(held, got)]]
    unnamed x2 -> x0, blocking collectives: 88.7 us -> none
    unnamed x70, local copies, waits for them, and re-layouts: 69.7 us -> 12.1 us
  transfers between devices with their start and end apart: 11 -> 34, of which waited for: 8 -> 17; matrix products, arithmetic and copies ran while one was open for 18% -> 23% of each run, Pallas kernels for 0% -> 30%
where the time goes in v1:
time: 590 us; the launch traced here: 585 us
  Pallas kernels  176 us (30%)
  waiting for transfers between devices  172 us (29%)
  local copies, waits for them, and re-layouts  53.5 us (9%)
  other arithmetic  47.5 us (8%)
  matrix products  46.6 us (8%)
  blocking collectives  41.2 us (7%)
  starting transfers between devices  33.3 us (6%)
  between operations  15.2 us (3%)
    ppermute x12, waiting for transfers between devices, gather_pieces(): got = [lax.ppermute(h, 'tok', s) for h, s in zip(held, swaps)]  71.2 us
    pallas_call x1, Pallas kernels, attention(): pl.pallas_call(attention_kernel, grid_spec=pltpu.PrefetchScalarGridSpec(n...  67.6 us
    ppermute x12, waiting for transfers between devices, scatter_pieces(): got = [lax.ppermute(v, 'tok', w) for v, w in zip(sent, swaps)]  48.5 us
    all_to_all x2, blocking collectives, swap_tok(): return lax.all_to_all(values, 'tok', 0, 0)  41.2 us
    pallas_call x2, Pallas kernels, sum_of_products(): pl.pallas_call(functools.partial(sum_kernel, len(lefts), transposed), gri...  38.3 us
    dot_general x3, matrix products, matmul_tn(): lax.dot_general(left, right, (((0,), (0,)), ((), ())), preferred_element_...  28 us
    pallas_call x1, Pallas kernels, feed_forward(): pl.pallas_call(feed_kernel, grid=(rows // QT,), in_specs=[pl.BlockSpec((Q...  26.7 us
    all_gather x3, waiting for transfers between devices, gather_grp(): return lax.all_gather(values, 'grp', axis=0, tiled=True)  26.4 us
  transfers between devices with their start and end apart: 34, of which 17 were waited for; matrix products, arithmetic and copies ran while one was open for 23% of the time, Pallas kernels for 30%

profile of v1, /device:TPU:0, one launch (start us, length us, event | category | flops | bytes accessed | tf_op | source)
XLA Modules:
  0.0 585.4 jit_solution(17564787200100265934)
XLA Ops:
  10.3 24.8 %all_to_all.30 = bf16[8,64,1408]{2,1,0:T(8,128)(2,1)} all-to-all(bf16[8,64,1408]{2,1,0:T(8,128)(2,1)S(1)} %shard_map.169), channel_id=1, replica_groups=mesh['grp'=4,'tok'=8] {'tok'}, dimensions={0} | all-to-all | bytes 2883584 | tf_op jit(solution)/shard_map/all_to_all | solution.py:338
  36.4 12.5 %collective-permute-done.3 = bf16[128,2048]{1,0:T(8,128)(2,1)S(1)} collective-permute-done((bf16[128,2048]{1,0:T(8,128)(2,1)S(1)}, bf16[128,2048]{1,0:T(8,128)(2,1)S(1)}, u32[]{:S(2)}, u32[]{:S(2)}) %collective-permute-start.3) | collective-permute-done | bytes 524320 | tf_op jit(solution)/shard_map/ppermute | solution.py:180
  50.7 22.3 %collective-permute-done.4 = bf16[256,2048]{1,0:T(8,128)(2,1)S(1)} collective-permute-done((bf16[256,2048]{1,0:T(8,128)(2,1)S(1)}, bf16[256,2048]{1,0:T(8,128)(2,1)S(1)}, u32[]{:S(2)}, u32[]{:S(2)}) %collective-permute-start.4) | collective-permute-done | bytes 1048608 | tf_op jit(solution)/shard_map/ppermute | solution.py:180
  74.6 14.7 %all-gather.4.cloned.1.call-done = bf16[960,2048]{1,0:T(8,128)(2,1)} async-done(((bf16[240,2048]{1,0:T(8,128)(2,1)}), bf16[960,2048]{1,0:T(8,128)(2,1)}) %all-gather.4.cloned.1.call-update) | async-done | bytes 3932176 | tf_op jit(solution)/shard_map/all_gather | solution.py:330
  99.7 11.0 %collective-permute-done.9 = bf16[128,2048]{1,0:T(8,128)(2,1)S(1)} collective-permute-done((bf16[128,2048]{1,0:T(8,128)(2,1)S(1)}, bf16[128,2048]{1,0:T(8,128)(2,1)S(1)}, u32[]{:S(2)}, u32[]{:S(2)}) %collective-permute-start.9) | collective-permute-done | bytes 524320 | tf_op jit(solution)/shard_map/ppermute | solution.py:180
  113.9 21.3 %collective-permute-done.10 = bf16[256,2048]{1,0:T(8,128)(2,1)S(1)} collective-permute-done((bf16[256,2048]{1,0:T(8,128)(2,1)S(1)}, bf16[256,2048]{1,0:T(8,128)(2,1)S(1)}, u32[]{:S(2)}, u32[]{:S(2)}) %collective-permute-start.10) | collective-permute-done | bytes 1048608 | tf_op jit(solution)/shard_map/ppermute | solution.py:180
  163.6 10.7 %shard_map.170.hidden.left = bf16[2048,2048]{1,0:T(8,128)(2,1)} custom-call(bf16[512,2048]{1,0:T(8,128)(2,1)S(1)} %pad_maximum_fusion.1.refs_0_, bf16[512,2048]{1,0:T(8,128)(2,1)S(1)} %copy-done.10, bf16[512,2048]{1,0:T(8,128)(2,1)} %pad_maximum_fusion.2.refs_2_, bf16[512,2048]{1,0:T(8,128)(2,1)} %collective-permute-done.5.refs_3_, ...), custom_call_target="tpu_custom_call" | custom-call | tf_op jit(solution)/shard_map/pallas_call | solution.py:223
  175.6 10.4 %shard_map.171.d_result = bf16[2048,2048]{1,0:T(8,128)(2,1)} custom-call(bf16[512,2048]{1,0:T(8,128)(2,1)} %pad_maximum_fusion.3.refs_0_, bf16[512,2048]{1,0:T(8,128)(2,1)} %collective-permute-done.8.refs_1_, bf16[512,2048]{1,0:T(8,128)(2,1)} %pad_maximum_fusion.4.refs_2_, bf16[512,2048]{1,0:T(8,128)(2,1)} %collective-permute-done.11.refs_3_), custom_call_target="tpu_custom_call" | custom-call | tf_op jit(solution)/shard_map/pallas_call | solution.py:223
  193.1 16.4 %all_to_all.31 = bf16[8,64,768]{2,1,0:T(8,128)(2,1)} all-to-all(bf16[8,64,768]{2,1,0:T(8,128)(2,1)S(1)} %shard_map.174), channel_id=1, replica_groups=mesh['grp'=4,'tok'=8] {'tok'}, dimensions={0} | all-to-all | bytes 1572864 | tf_op jit(solution)/shard_map/all_to_all | solution.py:338
  212.1 26.7 %shard_map.172 = (bf16[2048,704]{1,0:T(8,128)(2,1)S(1)}, bf16[2048,1408]{1,0:T(8,128)(2,1)}) custom-call(bf16[2048,2048]{1,0:T(8,128)(2,1)} %shard_map.170.hidden.left, bf16[2048,2048]{1,0:T(8,128)(2,1)} %shard_map.171.d_result, bf16[2048,1408]{1,0:T(8,128)(2,1)} %all-gather.6.cloned.1.call-done.up_weight.refs_3_, bf16[704,2048]{1,0:T(8,128)(2,1)S(1)} %bitcast.44), custom_call_target="tpu_custom_call" | custom-call | tf_op jit(solution)/shard_map/pallas_call | solution.py:274
  240.6 17.7 %shard_map.173 = bf16[2048,1408]{1,0:T(8,128)(2,1)S(1)} custom-call(bf16[2048,2048]{1,0:T(8,128)(2,1)} %shard_map.170.hidden.left, bf16[2048,1408]{1,0:T(8,128)(2,1)} %get-tuple-element.35.right.refs_1_), custom_call_target="tpu_custom_call" | custom-call | tf_op jit(solution)/shard_map/pallas_call | solution.py:299
  260.7 11.7 %all-gather.8.cloned.1.call-done.refs_2_ = bf16[2048,768]{1,0:T(8,128)(2,1)} async-done(((bf16[512,768]{1,0:T(8,128)(2,1)}), bf16[2048,768]{1,0:T(8,128)(2,1)}) %all-gather.8.cloned.1.call-update) | async-done | bytes 3145744 | tf_op jit(solution)/shard_map/all_gather | solution.py:330
  272.4 10.7 %convolution_convert_fusion.1 = bf16[704,2048]{1,0:T(8,128)(2,1)} fusion(bf16[2048,704]{1,0:T(8,128)(2,1)} %copy-done.6, bf16[2048,2048]{1,0:T(8,128)(2,1)} %shard_map.171.d_result), kind=kOutput, calls=%fused_computation.7 | convolution fusion | flops 5907021824 | bytes 14155776 | tf_op jit(solution)/shard_map/dot_general | solution.py:35
  283.1 11.8 %fusion.23.joint = f32[2048,768]{1,0:T(8,128)} fusion(bf16[2048,2048]{1,0:T(8,128)(2,1)} %shard_map.170.hidden.left, bf16[2048,768]{1,0:T(8,128)(2,1)} %all-gather.8.cloned.1.call-done.refs_2_), kind=kOutput, calls=%fused_computation.75 | convolution fusion | flops 6442450944 | bytes 17825792 | tf_op jit(solution)/shard_map/dot_general | solution.py:27
  295.0 67.6 %shard_map.175 = (bf16[2048,256]{1,0:T(8,128)(2,1)S(1)}, bf16[2048,768]{1,0:T(8,128)(2,1)}) custom-call(s32[16]{0:T(128)S(1)} %gather_fusion, f32[2048,768]{1,0:T(8,128)} %fusion.23.joint, bf16[2048,256]{1,0:T(8,128)(2,1)S(1)} %copy-done.11, f32[1152,128]{1,0:T(8,128)S(1)} %copy-done.8, f32[1152,128]{1,0:T(8,128)S(1)} %concatenate.66.below, ...), custom_call_target="tpu_custom_call" | custom-call | tf_op jit(solution)/shard_map/pallas_call | solution.py:149
  363.6 11.8 %reduce-scatter.4.cloned.1.call-done = bf16[512,1408]{1,0:T(8,128)(2,1)} async-done(((bf16[2048,1408]{1,0:T(8,128)(2,1)}), bf16[512,1408]{1,0:T(8,128)(2,1)}) %reduce-scatter.4.cloned.1.call-update) | async-done | bytes 1441808 | tf_op jit(solution)/shard_map/reduce_scatter | solution.py:334
  375.5 7.0 %convolution_convert_fusion.2 = bf16[256,2048]{1,0:T(8,128)(2,1)} fusion(bf16[2048,256]{1,0:T(8,128)(2,1)} %copy-done.1, bf16[2048,2048]{1,0:T(8,128)(2,1)} %shard_map.171.d_result), kind=kOutput, calls=%fused_computation.11 | convolution fusion | flops 2148007936 | bytes 10485760 | tf_op jit(solution)/shard_map/dot_general | solution.py:35
  387.1 10.2 %convolution_convert_fusion = bf16[2048,768]{0,1:T(8,128)(2,1)S(1)} fusion(bf16[2048,2048]{1,0:T(8,128)(2,1)} %shard_map.170.hidden.left, bf16[2048,768]{1,0:T(8,128)(2,1)} %get-tuple-element.45.refs_0_), kind=kOutput, calls=%fused_computation.6 | convolution fusion | flops 6444023808 | bytes 14680064 | tf_op jit(solution)/shard_map/dot_general | solution.py:35
  401.5 26.2 %shard_map.176 = bf16[2048,2048]{1,0:T(8,128)(2,1)} custom-call(bf16[2048,768]{1,0:T(8,128)(2,1)S(1)} %copy-done.5, bf16[2048,1408]{1,0:T(8,128)(2,1)} %get-tuple-element.35.right.refs_1_, bf16[2048,768]{1,0:T(8,128)(2,1)} %all-gather.8.cloned.1.call-done.refs_2_, bf16[2048,1408]{1,0:T(8,128)(2,1)} %all-gather.6.cloned.1.call-done.up_weight.refs_3_), custom_call_target="tpu_custom_call" | custom-call | tf_op jit(solution)/shard_map/pallas_call | solution.py:246
  439.9 12.1 %shard_map.177 = bf16[2048,2048]{1,0:T(8,128)(2,1)} custom-call(bf16[2048,256]{1,0:T(8,128)(2,1)S(1)} %copy-done.2, bf16[2048,704]{1,0:T(8,128)(2,1)} %copy-done.6, bf16[256,2048]{1,0:T(8,128)(2,1)S(1)} %bitcast.47, bf16[704,2048]{1,0:T(8,128)(2,1)S(1)} %bitcast.45), custom_call_target="tpu_custom_call" | custom-call | tf_op jit(solution)/shard_map/pallas_call | solution.py:246
  462.1 7.2 %add_convert_fusion.1 = (bf16[512,2048]{1,0:T(8,128)(2,1)S(1)}, bf16[512,2048]{1,0:T(8,128)(2,1)}) fusion(bf16[512,2048]{1,0:T(8,128)(2,1)} %collective-permute-done.18, bf16[2048,2048]{1,0:T(8,128)(2,1)} %shard_map.176, bf16[512,2048]{1,0:T(8,128)(2,1)} %collective-permute-done.21), kind=kLoop, calls=%fused_computation.3 | loop fusion | flops 8388608 | bytes 12582912 | tf_op jit(solution)/shard_map/convert_element_type | solution.py:325
  493.5 9.7 %collective-permute-done.19 = bf16[256,2048]{1,0:T(8,128)(2,1)S(1)} collective-permute-done((bf16[256,2048]{1,0:T(8,128)(2,1)}, bf16[256,2048]{1,0:T(8,128)(2,1)S(1)}, u32[]{:S(2)}, u32[]{:S(2)}) %collective-permute-start.19) | collective-permute-done | bytes 1048608 | tf_op jit(solution)/shard_map/ppermute | solution.py:320
  512.1 13.7 %collective-permute-done.13 = bf16[256,2048]{1,0:T(8,128)(2,1)S(1)} collective-permute-done((bf16[256,2048]{1,0:T(8,128)(2,1)S(1)}, bf16[256,2048]{1,0:T(8,128)(2,1)S(1)}, u32[]{:S(2)}, u32[]{:S(2)}) %collective-permute-start.13) | collective-permute-done | bytes 1048608 | tf_op jit(solution)/shard_map/ppermute | solution.py:320
  535.3 9.3 %collective-permute-done.20 = bf16[128,2048]{1,0:T(8,128)(2,1)S(1)} collective-permute-done((bf16[128,2048]{1,0:T(8,128)(2,1)S(1)}, bf16[128,2048]{1,0:T(8,128)(2,1)S(1)}, u32[]{:S(2)}, u32[]{:S(2)}) %collective-permute-start.20) | collective-permute-done | bytes 524320 | tf_op jit(solution)/shard_map/ppermute | solution.py:320
  (221 shorter events, 172.6 us)
Async XLA Ops:
  7.2 82.2 %all-gather.4.cloned.1.call-start = ((), (), s32[]{:S(2)}) async-start(), calls=%async_computation.9 | async-start | bytes 4915200 | tf_op jit(solution)/shard_map/all_gather | solution.py:330
  9.6 199.9 %all-gather.6.cloned.1.call-start = ((), (), s32[]{:S(2)}) async-start(), calls=%async_computation.10 | async-start | bytes 7208960 | tf_op jit(solution)/shard_map/all_gather | solution.py:330
  48.9 24.1 %collective-permute-start.4 = (bf16[256,2048]{1,0:T(8,128)(2,1)S(1)}, bf16[256,2048]{1,0:T(8,128)(2,1)S(1)}, u32[]{:S(2)}, u32[]{:S(2)}) collective-permute-start(bf16[256,2048]{1,0:T(8,128)(2,1)S(1)} %pad_maximum_fusion.7), channel_id=1, source_target_pairs={{0,2},{1,3},{2,0},{3,1},{4,6},{5,7},{6,4},{7,5},{8,10},{9,11},{10,... | collective-permute-start | bytes 3145736 | tf_op jit(solution)/shard_map/ppermute | solution.py:180
  49.6 39.8 %collective-permute-start.1 = (bf16[256,2048]{1,0:T(8,128)(2,1)S(1)}, bf16[256,2048]{1,0:T(8,128)(2,1)}, u32[]{:S(2)}, u32[]{:S(2)}) collective-permute-start(bf16[256,2048]{1,0:T(8,128)(2,1)S(1)} %pad_maximum_fusion.6), channel_id=1, source_target_pairs={{0,4},{1,5},{2,6},{3,7},{4,0},{5,1},{6,2},{7,3},{8,12},{9,13},{10,... | collective-permute-start | bytes 3145736 | tf_op jit(solution)/shard_map/ppermute | solution.py:180
  110.7 24.5 %collective-permute-start.10 = (bf16[256,2048]{1,0:T(8,128)(2,1)S(1)}, bf16[256,2048]{1,0:T(8,128)(2,1)S(1)}, u32[]{:S(2)}, u32[]{:S(2)}) collective-permute-start(bf16[256,2048]{1,0:T(8,128)(2,1)S(1)} %pad_maximum_fusion.9), channel_id=1, source_target_pairs={{0,2},{1,3},{2,0},{3,1},{4,6},{5,7},{6,4},{7,5},{8,10},{9,11},{10,... | collective-permute-start | bytes 3145736 | tf_op jit(solution)/shard_map/ppermute | solution.py:180
  112.4 24.5 %collective-permute-start.7 = (bf16[256,2048]{1,0:T(8,128)(2,1)S(1)}, bf16[256,2048]{1,0:T(8,128)(2,1)S(1)}, u32[]{:S(2)}, u32[]{:S(2)}) collective-permute-start(bf16[256,2048]{1,0:T(8,128)(2,1)S(1)} %pad_maximum_fusion.8), channel_id=1, source_target_pairs={{0,4},{1,5},{2,6},{3,7},{4,0},{5,1},{6,2},{7,3},{8,12},{9,13},{10,... | collective-permute-start | bytes 3145736 | tf_op jit(solution)/shard_map/ppermute | solution.py:180
  136.8 38.7 %collective-permute-start.11 = (bf16[512,2048]{1,0:T(8,128)(2,1)}, bf16[512,2048]{1,0:T(8,128)(2,1)}, u32[]{:S(2)}, u32[]{:S(2)}) collective-permute-start(bf16[512,2048]{1,0:T(8,128)(2,1)} %pad_maximum_fusion.4.refs_2_), channel_id=1, source_target_pairs={{0,1},{1,0},{2,3},{3,2},{4,5},{5,4},{6,7},{7,6},{8,9},{9,8},{10,11... | collective-permute-start | bytes 6291464 | tf_op jit(solution)/shard_map/ppermute | solution.py:180
  138.5 37.1 %collective-permute-start.8 = (bf16[512,2048]{1,0:T(8,128)(2,1)}, bf16[512,2048]{1,0:T(8,128)(2,1)}, u32[]{:S(2)}, u32[]{:S(2)}) collective-permute-start(bf16[512,2048]{1,0:T(8,128)(2,1)} %pad_maximum_fusion.3.refs_0_), channel_id=1, source_target_pairs={{0,1},{1,0},{2,3},{3,2},{4,5},{5,4},{6,7},{7,6},{8,9},{9,8},{10,11... | collective-permute-start | bytes 6291464 | tf_op jit(solution)/shard_map/ppermute | solution.py:180
  142.8 129.6 %all-gather.8.cloned.1.call-start = ((), (), s32[]{:S(2)}) async-start(), calls=%async_computation.11 | async-start | bytes 3932160 | tf_op jit(solution)/shard_map/all_gather | solution.py:330
  209.5 165.9 %reduce-scatter.4.cloned.1.call-start = ((), (), s32[]{:S(2)}) async-start(), calls=%async_computation.12 | async-start | bytes 7208960 | tf_op jit(solution)/shard_map/reduce_scatter | solution.py:334
  272.4 162.0 %reduce-scatter.6.cloned.1.call-start = ((), (), s32[]{:S(2)}) async-start(), calls=%async_computation.13 | async-start | bytes 3604480 | tf_op jit(solution)/shard_map/reduce_scatter | solution.py:334
  375.4 182.9 %reduce-scatter.8.cloned.1.call-start = ((), (), s32[]{:S(2)}) async-start(), calls=%async_computation.14 | async-start | bytes 5242880 | tf_op jit(solution)/shard_map/reduce_scatter | solution.py:334
  439.4 22.7 %collective-permute-start.18 = (bf16[512,2048]{1,0:T(8,128)(2,1)}, bf16[512,2048]{1,0:T(8,128)(2,1)}, u32[]{:S(2)}, u32[]{:S(2)}) collective-permute-start(bf16[512,2048]{1,0:T(8,128)(2,1)} %get-tuple-element.58), channel_id=1, source_target_pairs={{0,1},{1,0},{2,3},{3,2},{4,5},{5,4},{6,7},{7,6},{8,9},{9,8},{10,11... | collective-permute-start | bytes 6291464 | tf_op jit(solution)/shard_map/ppermute | solution.py:320
  439.4 22.7 %collective-permute-start.21 = (bf16[512,2048]{1,0:T(8,128)(2,1)}, bf16[512,2048]{1,0:T(8,128)(2,1)}, u32[]{:S(2)}, u32[]{:S(2)}) collective-permute-start(bf16[512,2048]{1,0:T(8,128)(2,1)} %get-tuple-element.59), channel_id=1, source_target_pairs={{0,1},{1,0},{2,3},{3,2},{4,5},{5,4},{6,7},{7,6},{8,9},{9,8},{10,11... | collective-permute-start | bytes 6291464 | tf_op jit(solution)/shard_map/ppermute | solution.py:320
  456.9 28.4 %collective-permute-start.12 = (bf16[512,2048]{1,0:T(8,128)(2,1)}, bf16[512,2048]{1,0:T(8,128)(2,1)}, u32[]{:S(2)}, u32[]{:S(2)}) collective-permute-start(bf16[512,2048]{1,0:T(8,128)(2,1)} %get-tuple-element.62), channel_id=1, source_target_pairs={{0,1},{1,0},{2,3},{3,2},{4,5},{5,4},{6,7},{7,6},{8,9},{9,8},{10,11... | collective-permute-start | bytes 6291464 | tf_op jit(solution)/shard_map/ppermute | solution.py:320
  457.0 28.4 %collective-permute-start.15 = (bf16[512,2048]{1,0:T(8,128)(2,1)}, bf16[512,2048]{1,0:T(8,128)(2,1)}, u32[]{:S(2)}, u32[]{:S(2)}) collective-permute-start(bf16[512,2048]{1,0:T(8,128)(2,1)} %get-tuple-element.63), channel_id=1, source_target_pairs={{0,1},{1,0},{2,3},{3,2},{4,5},{5,4},{6,7},{7,6},{8,9},{9,8},{10,11... | collective-permute-start | bytes 6291464 | tf_op jit(solution)/shard_map/ppermute | solution.py:320
  457.7 23.6 %all-to-all-start.5 = ((bf16[8,64,1408]{2,1,0:T(8,128)(2,1)}), bf16[8,64,1408]{2,1,0:T(8,128)(2,1)S(1)}, u32[]{:S(2)}, u32[]{:S(2)}) async-start(bf16[8,64,1408]{2,1,0:T(8,128)(2,1)} %bitcast.53), calls=%async_computation.8 | async-start | bytes 2883584 | tf_op jit(solution)/shard_map/all_to_all | solution.py:338
  471.6 31.6 %collective-permute-start.19 = (bf16[256,2048]{1,0:T(8,128)(2,1)}, bf16[256,2048]{1,0:T(8,128)(2,1)S(1)}, u32[]{:S(2)}, u32[]{:S(2)}) collective-permute-start(bf16[256,2048]{1,0:T(8,128)(2,1)} %slice.157), channel_id=1, source_target_pairs={{0,4},{1,5},{2,6},{3,7},{4,0},{5,1},{6,2},{7,3},{8,12},{9,13},{10,... | collective-permute-start | bytes 3145736 | tf_op jit(solution)/shard_map/ppermute | solution.py:320
  484.8 26.2 %collective-permute-start.22 = (bf16[256,2048]{1,0:T(8,128)(2,1)S(1)}, bf16[256,2048]{1,0:T(8,128)(2,1)S(1)}, u32[]{:S(2)}, u32[]{:S(2)}) collective-permute-start(bf16[256,2048]{1,0:T(8,128)(2,1)S(1)} %slice.163), channel_id=1, source_target_pairs={{0,2},{1,3},{2,0},{3,1},{4,6},{5,7},{6,4},{7,5},{8,10},{9,11},{10,... | collective-permute-start | bytes 3145736 | tf_op jit(solution)/shard_map/ppermute | solution.py:320
  491.3 34.4 %collective-permute-start.13 = (bf16[256,2048]{1,0:T(8,128)(2,1)S(1)}, bf16[256,2048]{1,0:T(8,128)(2,1)S(1)}, u32[]{:S(2)}, u32[]{:S(2)}) collective-permute-start(bf16[256,2048]{1,0:T(8,128)(2,1)S(1)} %slice.145), channel_id=1, source_target_pairs={{0,4},{1,5},{2,6},{3,7},{4,0},{5,1},{6,2},{7,3},{8,12},{9,13},{10,... | collective-permute-start | bytes 3145736 | tf_op jit(solution)/shard_map/ppermute | solution.py:320
  491.9 41.5 %collective-permute-start.16 = (bf16[256,2048]{1,0:T(8,128)(2,1)S(1)}, bf16[256,2048]{1,0:T(8,128)(2,1)S(1)}, u32[]{:S(2)}, u32[]{:S(2)}) collective-permute-start(bf16[256,2048]{1,0:T(8,128)(2,1)S(1)} %slice.151), channel_id=1, source_target_pairs={{0,2},{1,3},{2,0},{3,1},{4,6},{5,7},{6,4},{7,5},{8,10},{9,11},{10,... | collective-permute-start | bytes 3145736 | tf_op jit(solution)/shard_map/ppermute | solution.py:320
  503.7 41.0 %collective-permute-start.20 = (bf16[128,2048]{1,0:T(8,128)(2,1)S(1)}, bf16[128,2048]{1,0:T(8,128)(2,1)S(1)}, u32[]{:S(2)}, u32[]{:S(2)}) collective-permute-start(bf16[128,2048]{1,0:T(8,128)(2,1)S(1)} %slice.159), channel_id=1, source_target_pairs={{0,2},{1,3},{2,0},{3,1},{4,6},{5,7},{6,4},{7,5},{8,10},{9,11},{10,... | collective-permute-start | bytes 1572872 | tf_op jit(solution)/shard_map/ppermute | solution.py:320
  511.4 33.4 %collective-permute-start.23 = (bf16[128,2048]{1,0:T(8,128)(2,1)S(1)}, bf16[128,2048]{1,0:T(8,128)(2,1)S(1)}, u32[]{:S(2)}, u32[]{:S(2)}) collective-permute-start(bf16[128,2048]{1,0:T(8,128)(2,1)S(1)} %slice.165), channel_id=1, source_target_pairs={{0,4},{1,5},{2,6},{3,7},{4,0},{5,1},{6,2},{7,3},{8,12},{9,13},{10,... | collective-permute-start | bytes 1572872 | tf_op jit(solution)/shard_map/ppermute | solution.py:320
  527.0 26.8 %collective-permute-start.14 = (bf16[128,2048]{1,0:T(8,128)(2,1)}, bf16[128,2048]{1,0:T(8,128)(2,1)}, u32[]{:S(2)}, u32[]{:S(2)}) collective-permute-start(bf16[128,2048]{1,0:T(8,128)(2,1)} %slice.147), channel_id=1, source_target_pairs={{0,2},{1,3},{2,0},{3,1},{4,6},{5,7},{6,4},{7,5},{8,10},{9,11},{10,... | collective-permute-start | bytes 1572872 | tf_op jit(solution)/shard_map/ppermute | solution.py:320
  (45 other events, 397.5 us)
Sparse Core Ops, SparseCore 0:
  10.2 79.1 all-gather.3
  90.9 105.5 all-gather.5
  209.7 62.6 all-gather.7
  274.5 100.8 reduce-scatter.3
  377.6 56.7 reduce-scatter.5
  436.5 76.6 reduce-scatter.7

commit v2 on v1

--- a/solution.py
+++ b/solution.py
@@ -56,12 +56,9 @@
 def attention_kernel(
     place, joint, d_out, keep, below, above, out, d_joint, qs, ks, vs, ds, d_key, d_value
 ):
-    head = pl.program_id(0)
-    half = head % 2
-    lane_block = head // 2
     span = d_out.shape[1]
-    lanes = [pl.ds(pl.multiple_of(c * span + lane_block * LANES, LANES), LANES) for c in range(3)]
-    mine = lax.broadcasted_iota(jnp.int32, (BT, LANES), 1) // HD == half
+    first = pl.program_id(0) * LANES
+    lanes = [pl.ds(pl.multiple_of(c * span + first, LANES), LANES) for c in range(3)]
 
     def turned(values, part, sign):
         row = min(part, PB) * BT
@@ -76,33 +73,21 @@
     for part in range(BLK_GROUP):
         rows = rows_of(part)
         here = pl.ds(part * BT, BT)
-        query = turned(joint[rows, lanes[0]], part, 1.0).astype(bf16) * HD ** (-0.5)
-        key = turned(joint[rows, lanes[1]], part, 1.0).astype(bf16)
-        qs[here, :] = jnp.where(mine, query, 0).astype(bf16)
-        ks[here, :] = jnp.where(mine, key, 0).astype(bf16)
-        vs[here, :] = jnp.where(mine, joint[rows, lanes[2]].astype(bf16), 0).astype(bf16)
-        ds[here, :] = jnp.where(mine, d_out[rows, lanes[0]], 0).astype(bf16)
-    d_key[...] = jnp.zeros_like(d_key)
-    d_value[...] = jnp.zeros_like(d_value)
-
-    def put(ref, rows, where, values):
-        @pl.when(half == 0)
-        def _():
-            ref[rows, where] = values
-
-        @pl.when(half != 0)
-        def _():
-            ref[rows, where] = jnp.where(mine, values, ref[rows, where]).astype(ref.dtype)
+        qs[here, :] = turned(joint[rows, lanes[0]], part, 1.0).astype(bf16) * HD ** (-0.5)
+        ks[here, :] = turned(joint[rows, lanes[1]], part, 1.0).astype(bf16)
+        vs[here, :] = joint[rows, lanes[2]].astype(bf16)
+        ds[here, :] = d_out[rows, lanes[0]]
 
     row_id = lax.broadcasted_iota(jnp.int32, (QT, QT), 0)
     col_id = lax.broadcasted_iota(jnp.int32, (QT, QT), 1)
     causal = row_id >= col_id
     alone = causal & (row_id // BT == col_id // BT)
-
-    def tile(index, shared, allowed):
-        start = index * QT
-        own = pl.ds(start, QT)
-        query, d_o = qs[own, :], ds[own, :]
+    head_of = lax.broadcasted_iota(jnp.int32, (QT, LANES), 1) // HD
+
+    def one_head(head, own, shared, allowed):
+        mine = head_of == head
+        query = jnp.where(mine, qs[own, :], 0).astype(bf16)
+        d_o = jnp.where(mine, ds[own, :], 0).astype(bf16)
         spans = [own] + ([pl.ds(0, shared)] if shared else [])
         raw = [matmul_nt(query, ks[s, :]) for s in spans]
         raw[0] = jnp.where(allowed, raw[0], neg_big)
@@ -118,16 +103,34 @@
             (w * (matmul_nt(d_o, vs[s, :]) - delta)).astype(bf16) for w, s in zip(weights, spans)
         ]
         d_query = functools.reduce(jnp.add, [matmul(d, ks[s, :]) for d, s in zip(d_scores, spans)])
+        d_keys = [matmul_tn(d, query) for d in d_scores]
+        d_values = [matmul_tn(w, d_o) for w in low]
+        return attended, d_query, d_keys, d_values
+
+    def tile(index, shared, allowed):
+        own = pl.ds(index * QT, QT)
+        found = [one_head(head, own, shared, allowed) for head in range(LANES // HD)]
+        attended, d_query = found[0][:2]
+        for head in range(1, LANES // HD):
+            mine = head_of == head
+            attended = jnp.where(mine, found[head][0], attended)
+            d_query = jnp.where(mine, found[head][1], d_query)
         d_query = d_query * HD ** (-0.5)
-        for s, d, w in zip(spans, d_scores, low):
-            d_key[s, :] += matmul_tn(d, query)
-            d_value[s, :] += matmul_tn(w, d_o)
+        d_keys, d_values = (
+            [functools.reduce(jnp.add, parts) for parts in zip(*(f[k] for f in found))]
+            for k in (2, 3)
+        )
+        d_key[own, :] = d_keys[0]
+        d_value[own, :] = d_values[0]
+        if shared:
+            d_key[:shared, :] += d_keys[1]
+            d_value[:shared, :] += d_values[1]
         for k in range(QT // BT):
             part = index * (QT // BT) + k
             rows = rows_of(part)
             piece = slice(k * BT, (k + 1) * BT)
-            put(out, rows, lanes[0], attended[piece, :].astype(bf16))
-            put(d_joint, rows, lanes[0], turned(d_query[piece, :], part, -1.0).astype(bf16))
+            out[rows, lanes[0]] = attended[piece, :].astype(bf16)
+            d_joint[rows, lanes[0]] = turned(d_query[piece, :], part, -1.0).astype(bf16)
 
     prompt_tiles = PB * BT // QT
     for index in range(BLK_GROUP * BT // QT):
@@ -138,8 +141,8 @@
     for part in range(BLK_GROUP):
         here = pl.ds(part * BT, BT)
         rows = rows_of(part)
-        put(d_joint, rows, lanes[1], turned(d_key[here, :], part, -1.0).astype(bf16))
-        put(d_joint, rows, lanes[2], d_value[here, :].astype(bf16))
+        d_joint[rows, lanes[1]] = turned(d_key[here, :], part, -1.0).astype(bf16)
+        d_joint[rows, lanes[2]] = d_value[here, :].astype(bf16)
 
 
 def attention(place, joint, d_out, tables):
@@ -150,7 +153,7 @@
         attention_kernel,
         grid_spec=pltpu.PrefetchScalarGridSpec(
             num_scalar_prefetch=1,
-            grid=(span // HD,),
+            grid=(span // LANES,),
             in_specs=[full(joint.shape), full(d_out.shape)] + [full(t.shape) for t in tables],
             out_specs=[full((count, span)), full((count, 3 * span))],
             scratch_shapes=scratch,
@@ -168,7 +171,7 @@
     return lax.optimization_barrier((values, earlier))[0]
 
 
-def gather_pieces(values):
+def gather_pieces(values, between):
     toks = lax.axis_size("tok")
     bits = toks.bit_length() - 1
     paths = values.shape[0] // BT
@@ -176,6 +179,8 @@
     held = list(jnp.split(values, paths))
     found = []
     for step in range(bits):
+        if step in between:
+            held = between[step](held)
         swaps = [[(i, i ^ (1 << orders[p % 2][step])) for i in range(toks)] for p in range(paths)]
         got = [lax.ppermute(h, "tok", s) for h, s in zip(held, swaps)]
         if step == bits - 1:
@@ -228,31 +233,49 @@
         out_specs=pl.BlockSpec((block, width), lambda i: (i, 0)),
         out_shape=jax.ShapeDtypeStruct((total, width), bf16),
         compiler_params=pltpu.CompilerParams(vmem_limit_bytes=48 * 2**20),
-        cost_estimate=no_cost,
+        cost_estimate=pl.CostEstimate(
+            flops=10 * total * width, transcendentals=0, bytes_accessed=8 * total * width
+        ),
     )(*pieces, *norm)
 
 
 def sum_kernel(count, transposed, *refs):
     product = matmul_nt if transposed else matmul
     terms = [product(refs[k][...], refs[count + k][...]) for k in range(count)]
-    refs[-1][...] = functools.reduce(jnp.add, terms).astype(bf16)
-
-
-def sum_of_products(lefts, rights, transposed):
+    total = functools.reduce(jnp.add, terms).astype(bf16)
+    outs = refs[2 * count :]
+    each = pl.num_programs(0) // len(outs)
+    for k, out in enumerate(outs):
+
+        @pl.when(pl.program_id(0) // each == k)
+        def _():
+            out[...] = total
+
+
+def sum_of_products(lefts, rights, transposed, paths):
     rows = lefts[0].shape[0]
     cols = rights[0].shape[0 if transposed else 1]
-    inner = sum(v.shape[1] for v in lefts)
-    block = QT
-    return pl.pallas_call(
+    outs = 2 * paths
+    each = rows // outs // QT
+
+    def left_block(i):
+        which = i // each
+        return (which % paths * 2 * each + (1 - which // paths) * each + i % each, 0)
+
+    def out_block(k):
+        return pl.BlockSpec((QT, cols), lambda i: (jnp.clip(i - k * each, 0, each - 1), 0))
+
+    found = pl.pallas_call(
         functools.partial(sum_kernel, len(lefts), transposed),
-        grid=(rows // block,),
-        in_specs=[pl.BlockSpec((block, v.shape[1]), lambda i: (i, 0)) for v in lefts]
+        grid=(rows // QT,),
+        in_specs=[pl.BlockSpec((QT, v.shape[1]), left_block) for v in lefts]
         + [pl.BlockSpec(v.shape, lambda i: (0, 0), pipeline_mode=pl.Buffered(1)) for v in rights],
-        out_specs=pl.BlockSpec((block, cols), lambda i: (i, 0)),
-        out_shape=jax.ShapeDtypeStruct((rows, cols), bf16),
+        out_specs=[out_block(k) for k in range(outs)],
+        out_shape=[jax.ShapeDtypeStruct((rows // outs, cols), bf16)] * outs,
         compiler_params=pltpu.CompilerParams(vmem_limit_bytes=48 * 2**20),
-        cost_estimate=no_cost,
+        cost_estimate=(pl.CostEstimate(flops=18*10**9, transcendentals=0, bytes_accessed=10**7) if transposed else no_cost),
     )(*lefts, *rights)
+    return list(zip(found[paths:], found[:paths]))
 
 
 def feed_kernel(hidden, d_result, up_weight, down_weight, act, d_both):
@@ -310,20 +333,53 @@
     )(left, right)
 
 
-def scatter_pieces(values, orders):
+def scatter_step(pairs, orders, step):
     toks = lax.axis_size("tok")
-    bits = toks.bit_length() - 1
-    held = list(jnp.split(values, len(orders)))
-    for step in range(bits - 1, -1, -1):
-        sent = [h[h.shape[0] // 2 :] for h in held]
-        swaps = [[(i, i ^ (1 << order[step])) for i in range(toks)] for order in orders]
-        got = [lax.ppermute(v, "tok", w) for v, w in zip(sent, swaps)]
-        held = [
-            h[: h.shape[0] // 2].astype(f32) + g.astype(f32) for h, g in zip(held, got)
-        ]
-        if step:
-            held = [h.astype(bf16) for h in held]
-    return jnp.concatenate(held)
+    held = []
+    for (kept, sent), order in zip(pairs, orders):
+        got = lax.ppermute(sent, "tok", [(i, i ^ (1 << order[step])) for i in range(toks)])
+        held.append(kept.astype(f32) + got.astype(f32))
+    if not step:
+        return held
+    tall = held[0].shape[0] // 2
+    return lax.optimization_barrier(
+        [(h[:tall].astype(bf16), h[tall:].astype(bf16)) for h in held]
+    )
+
+
+def head_terms_kernel(tall, hidden, d_joint, attended, d_result, out):
+    grps = pl.num_programs(0) // (tall // QT)
+    upper = pl.program_id(0) % grps % (LANES // HD) != 0
+    split = d_joint.shape[1]
+    out[:, :split] = matmul_tn(hidden[...], d_joint[...]).astype(bf16)
+    term = matmul_tn(attended[...], d_result[...])
+    term = jnp.where(upper, term[HD:], term[:HD]).astype(bf16)
+    wide = out.shape[1] - split
+    for k in range(QT // HD):
+        out[k * HD : (k + 1) * HD, split:] = term[:, k * wide : (k + 1) * wide]
+
+
+def head_terms(hidden, d_joint, attended, d_result, grps):
+    rows, width = hidden.shape
+    tall = width // grps
+    each = tall // QT
+    wide = HD * width // tall
+    return pl.pallas_call(
+        functools.partial(head_terms_kernel, tall),
+        grid=(each * grps,),
+        in_specs=[
+            pl.BlockSpec((rows, QT), lambda i: (0, i % grps * each + i // grps)),
+            pl.BlockSpec(d_joint.shape, lambda i: (0, 0), pipeline_mode=pl.Buffered(1)),
+            pl.BlockSpec((rows, LANES), lambda i: (0, i % grps // (LANES // HD))),
+            pl.BlockSpec((rows, width // each), lambda i: (0, i // grps)),
+        ],
+        out_specs=pl.BlockSpec(
+            (QT, d_joint.shape[1] + wide), lambda i: (i % grps * each + i // grps, 0)
+        ),
+        out_shape=jax.ShapeDtypeStruct((width, d_joint.shape[1] + wide), bf16),
+        compiler_params=pltpu.CompilerParams(vmem_limit_bytes=48 * 2**20),
+        cost_estimate=no_cost,
+    )(hidden, d_joint, attended, d_result)
 
 
 def gather_grp(values):
@@ -411,7 +467,8 @@
     gain = pair[:, 0].reshape(width).astype(f32)
     bias = pair[:, 1].reshape(width).astype(f32)
 
-    whole_heads = out_weight.shape[0] == HD
+    tall = width // grps
+    whole_heads = out_weight.shape[0] == HD and tall % QT == 0 and HD * grps % LANES == 0
     if whole_heads:
         first = gather_grp(jnp.concatenate([down_weight, out_weight]))
         first = first.reshape(grps, -1, width)
@@ -424,19 +481,35 @@
             out_w.reshape(own_heads, toks, HD, width), tok, 1, keepdims=False
         ).reshape(span, width)
     gate_up_own = swap_tok(split_columns([gate_weight, up_weight], grps, toks))
-    gate_up_w = gather_grp(after(gate_up_own.reshape(-1, 2 * wide), first))
-    pieces, orders = gather_pieces(after(tokens, gate_up_own))
+    gate_up_own = gate_up_own.reshape(-1, 2 * wide)
+    own_tokens, gate_up_own, gain, bias = lax.optimization_barrier(
+        (tokens, gate_up_own, gain, bias)
+    )
+    tables = rotary_tables()
+
+    def with_tables(held):
+        nonlocal tables
+        held, tables = lax.optimization_barrier((held, tables))
+        return held
+
+    def with_hidden(held):
+        nonlocal hidden
+        held, hidden = lax.optimization_barrier((held, hidden))
+        return held
+
+    pieces, orders = gather_pieces(own_tokens, {2: with_tables})
+    own_cotangent, pieces = lax.optimization_barrier((cotangent, pieces))
     hidden = assemble(pieces, gain[None], bias[None])
-    d_pieces, _ = gather_pieces(after(cotangent, *pieces))
-    dy = assemble(d_pieces)
     slots = jnp.argsort(block_table[0] % BLK_GROUP).astype(jnp.int32)
     halves = len(orders)
     spots = [(tok ^ apart) * halves + half for apart, half in order_of(orders)]
     place = jnp.argsort(jnp.stack(spots))[slots].astype(jnp.int32)
-    tables = rotary_tables()
+    d_pieces, _ = gather_pieces(own_cotangent, {2: with_hidden})
+    gate_up_w = gather_grp(after(gate_up_own, first))
+    dy = assemble(d_pieces)
     d_attended = matmul_nt(dy, out_w).astype(bf16)
     joint_own = split_columns(
-        [after(joint_weight, hidden, dy, d_attended, place, *tables)], 3 * own_heads, toks
+        [after(joint_weight, dy, d_attended, place)], 3 * own_heads, toks
     )
     joint_own = swap_tok(joint_own).reshape(-1, 3 * span)
     joint_w = gather_grp(after(joint_own, gate_up_w))
@@ -444,35 +517,46 @@
     activated, d_gate_up = feed_forward(hidden, dy, gate_up_w, down_w)
     gate_up_term = outer_product(hidden, d_gate_up)
     gate_up_grad = scatter_grp(after(gate_up_term, joint_w))
-    down_term = matmul_tn(after(activated, joint_w), dy).astype(bf16)
 
     joint = matmul(after(hidden, gate_up_term), joint_w)
-    attended, d_joint = attention(place, joint, after(d_attended, down_term), tables)
-    down_grad = scatter_grp(after(down_term, gate_up_grad, d_joint))
-    joint_term = matmul_tn(hidden, d_joint).astype(bf16)
-    out_term = matmul_tn(attended, dy).astype(bf16)
+    attended, d_joint = attention(place, joint, d_attended, tables)
+    last = toks.bit_length() - 2
     if whole_heads:
-        tall = width // grps
-        out_term = out_term.reshape(grps, -1, width).reshape(grps * tall, -1)
-        joined = jnp.concatenate([joint_term, out_term], axis=1)
-        joined = scatter_grp(after(joined, down_grad))
-        joint_grad = joined[:, : 3 * span]
-        out_grad = joined[:, 3 * span :].reshape(-1, width).astype(f32)
+        head_sums = head_terms(hidden, d_joint, attended, dy, grps)
     else:
-        joint_grad = scatter_grp(after(joint_term, down_grad))
+        head_sums = matmul_tn(hidden, d_joint).astype(bf16)
+    flat = lambda pairs: [v for pair in pairs for v in pair]
+    lefts = [after(attended, head_sums), activated]
+    sums = sum_of_products(lefts, [out_w, down_w], False, halves)
+    head_sums = scatter_grp(after(head_sums, gate_up_grad, *flat(sums)))
+    sums = scatter_step(sums, orders, last)
+    gate_up_rows = swap_tok(after(gate_up_grad, *flat(sums)).reshape(toks, -1, 2 * wide))
+    lefts = [after(d_joint, *flat(sums)), d_gate_up]
+    d_sums = sum_of_products(lefts, [joint_w, gate_up_w], True, halves)
+    sums = scatter_step(sums, orders, last - 1)
+    d_sums = scatter_step(d_sums, orders, last)
+    d_sums, sums, gate_up_rows = lax.optimization_barrier((d_sums, sums, gate_up_rows))
+    down_term = matmul_tn(after(activated, *flat(d_sums)), dy).astype(bf16)
+    d_sums = scatter_step(d_sums, orders, last - 1)
+    d_sums, sums, head_sums = lax.optimization_barrier((d_sums, sums, head_sums))
+    for step in range(last - 2, -1, -1):
+        d_sums = scatter_step(d_sums, orders, step)
+        sums = scatter_step(sums, orders, step)
+    down_grad = scatter_grp(after(down_term, head_sums))
+    d_hidden = jnp.concatenate(d_sums)
+    result = (tokens.astype(f32) + jnp.concatenate(sums)).astype(bf16)
+    if whole_heads:
+        joint_grad = head_sums[:, : 3 * span]
+        out_grad = head_sums[:, 3 * span :].reshape(tall // HD, HD, -1)
+        out_grad = out_grad.transpose(1, 0, 2).reshape(HD, width).astype(f32)
+    else:
+        joint_grad = head_sums
         spread = jnp.zeros((own_heads, toks, HD, width), bf16)
-        spread = lax.dynamic_update_index_in_dim(
-            spread, out_term.reshape(own_heads, 1, HD, width), tok, 1
-        )
+        out_term = matmul_tn(attended, dy).astype(bf16).reshape(own_heads, 1, HD, width)
+        spread = lax.dynamic_update_index_in_dim(spread, out_term, tok, 1)
         out_grad = lax.psum_scatter(
             spread.reshape(width, width), both, scatter_dimension=0, tiled=True
         ).astype(f32)
-    d_hidden = sum_of_products(
-        [after(d_joint, gate_up_grad, joint_term, out_term), d_gate_up], [joint_w, gate_up_w], True
-    )
-    branch = sum_of_products([after(attended, d_hidden), activated], [out_w, down_w], False)
-    d_hidden = scatter_pieces(d_hidden, orders)
-    result = (tokens.astype(f32) + scatter_pieces(branch, orders)).astype(bf16)
     tokens_wide = tokens.astype(f32)
     centred = tokens_wide - jnp.mean(tokens_wide, axis=-1, keepdims=True)
     inv_std = lax.rsqrt(jnp.mean(centred * centred, axis=-1, keepdims=True) + eps)
@@ -488,17 +572,16 @@
     sums = lax.all_to_all(sums.reshape(2, devices, -1).transpose(1, 0, 2), both, 0, 0)
     sums = jnp.sum(sums, axis=0)
 
-    def owned(grad, outer, count):
-        return join_columns(swap_tok(grad.reshape(toks, -1, grad.shape[1])), outer, count)
+    joint_rows = swap_tok(after(joint_grad, d_hidden, result).reshape(toks, -1, 3 * span))
 
     return (
         result,
         input_grad,
         sums[0],
         sums[1],
-        *owned(joint_grad, 3 * own_heads, 1),
+        *join_columns(joint_rows, 3 * own_heads, 1),
         out_grad,
-        *owned(gate_up_grad, grps, 2),
+        *join_columns(gate_up_rows, grps, 2),
         down_grad.astype(f32),
     )
 

time: 590 us -> 542 us (0.919)
  blocking collectives: 41.2 us -> 16.2 us
  local copies, waits for them, and re-layouts: 53.5 us -> 34.3 us
  matrix products: 46.6 us -> 28.6 us
  Pallas kernels: 176 us -> 194 us
  starting transfers between devices: 33.3 us -> 44.8 us
  waiting for transfers between devices: 172 us -> 161 us
    all_to_all x2 -> x3, waiting for transfers between devices: 7.68 us -> 39.8 us  [swap_tok(): return lax.all_to_all(values, 'tok', 0, 0)]
    all_to_all x2 -> x1, blocking collectives: 41.2 us -> 16.2 us  [swap_tok(): return lax.all_to_all(values, 'tok', 0, 0)]
    ppermute x12, waiting for transfers between devices: 48.5 us -> 29.9 us  [scatter_step(): lax.ppermute(sent, 'tok', [(i, i ^ 1 << order[step]) for i in range(toks)])]
    reduce_scatter x3, waiting for transfers between devices: 18.4 us -> 0.51 us  [scatter_grp(): lax.psum_scatter(values.astype(bf16), 'grp', scatter_dimension=0, tiled=T...]
    pallas_call x0 -> x1, Pallas kernels: none -> 17.7 us  [head_terms(): pl.pallas_call(functools.partial(head_terms_kernel, tall), grid=(each * g...]
    dot_general x3 -> x1, matrix products: 28 us -> 10.9 us  [matmul_tn(): lax.dot_general(left, right, (((0,), (0,)), ((), ())), preferred_element_...]
    ppermute x12, waiting for transfers between devices: 71.2 us -> 54.2 us  [gather_pieces(): got = [lax.ppermute(h, 'tok', s) for h, s in zip(held, swaps)]]
    convert_element_type x8 -> x0, other arithmetic: 15.2 us -> none  [the longest x6 14.5 us: scatter_pieces(): held = [h.astype(bf16) for h in held]]
  transfers between devices with their start and end apart: 34 -> 35, of which waited for: 17 -> 22; matrix products, arithmetic and copies ran while one was open for 23% -> 17% of each run, Pallas kernels for 30% -> 36%
where the time goes in v2:
time: 542 us; the launch traced here: 536 us
  Pallas kernels  194 us (36%)
  waiting for transfers between devices  161 us (30%)
  starting transfers between devices  44.8 us (8%)
  other arithmetic  42.6 us (8%)
  local copies, waits for them, and re-layouts  34.3 us (6%)
  matrix products  28.6 us (5%)
  blocking collectives  16.2 us (3%)
  between operations  15 us (3%)
    pallas_call x1, Pallas kernels, attention(): pl.pallas_call(attention_kernel, grid_spec=pltpu.PrefetchScalarGridSpec(n...  60 us
    ppermute x12, waiting for transfers between devices, gather_pieces(): got = [lax.ppermute(h, 'tok', s) for h, s in zip(held, swaps)]  54.2 us
    pallas_call x2, Pallas kernels, sum_of_products(): pl.pallas_call(functools.partial(sum_kernel, len(lefts), transposed), gri...  44.3 us
    all_to_all x3, waiting for transfers between devices, swap_tok(): return lax.all_to_all(values, 'tok', 0, 0)  39.8 us
    all_gather x3, waiting for transfers between devices, gather_grp(): return lax.all_gather(values, 'grp', axis=0, tiled=True)  30.1 us
    ppermute x12, waiting for transfers between devices, scatter_step(): lax.ppermute(sent, 'tok', [(i, i ^ 1 << order[step]) for i in range(toks)])  29.9 us
    pallas_call x1, Pallas kernels, feed_forward(): pl.pallas_call(feed_kernel, grid=(rows // QT,), in_specs=[pl.BlockSpec((Q...  28.2 us
    pallas_call x2, Pallas kernels, assemble(): pl.pallas_call(functools.partial(assemble_kernel, len(pieces), bool(norm)...  20.4 us
  transfers between devices with their start and end apart: 35, of which 22 were waited for; matrix products, arithmetic and copies ran while one was open for 17% of the time, Pallas kernels for 36%

profile of v2, /device:TPU:0, one launch (start us, length us, event | category | flops | bytes accessed | tf_op | source)
XLA Modules:
  0.0 536.2 jit_solution(7593639903100314480)
XLA Ops:
  10.3 7.3 %all-to-all-start.1 = ((bf16[32,2,64]{2,1,0:T(2,128)(2,1)}), bf16[32,2,64]{2,1,0:T(2,128)(2,1)S(1)}, u32[]{:S(2)}, u32[]{:S(2)}) async-start(bf16[32,2,64]{2,1,0:T(2,128)(2,1)} %broadcast_in_dim.13), calls=%async_computation.1 | async-start | bytes 32768 | tf_op jit(solution)/shard_map/all_to_all | solution.py:466
  28.5 19.3 %all-to-all-done = bf16[8,64,1408]{2,1,0:T(8,128)(2,1)S(1)} async-done(((bf16[8,64,1408]{2,1,0:T(8,128)(2,1)}), bf16[8,64,1408]{2,1,0:T(8,128)(2,1)S(1)}, u32[]{:S(2)}, u32[]{:S(2)}) %all-to-all-start) | async-done | bytes 1441824 | tf_op jit(solution)/shard_map/all_to_all | solution.py:394
  49.1 9.9 %collective-permute-done.2 = bf16[128,2048]{1,0:T(8,128)(2,1)S(1)} collective-permute-done((bf16[128,2048]{1,0:T(8,128)(2,1)S(1)}, bf16[128,2048]{1,0:T(8,128)(2,1)S(1)}, u32[]{:S(2)}, u32[]{:S(2)}) %collective-permute-start.2) | collective-permute-done | bytes 524320 | tf_op jit(solution)/shard_map/ppermute | solution.py:185
  73.1 13.6 %collective-permute-done.3 = bf16[256,2048]{1,0:T(8,128)(2,1)} collective-permute-done((bf16[256,2048]{1,0:T(8,128)(2,1)}, bf16[256,2048]{1,0:T(8,128)(2,1)}, u32[]{:S(2)}, u32[]{:S(2)}) %collective-permute-start.3) | collective-permute-done | bytes 1048608 | tf_op jit(solution)/shard_map/ppermute | solution.py:185
  101.9 11.0 %collective-permute-done.8 = bf16[128,2048]{1,0:T(8,128)(2,1)S(1)} collective-permute-done((bf16[128,2048]{1,0:T(8,128)(2,1)S(1)}, bf16[128,2048]{1,0:T(8,128)(2,1)S(1)}, u32[]{:S(2)}, u32[]{:S(2)}) %collective-permute-start.8) | collective-permute-done | bytes 524320 | tf_op jit(solution)/shard_map/ppermute | solution.py:185
  116.3 10.6 %shard_map.170.hidden.left = bf16[2048,2048]{1,0:T(8,128)(2,1)} custom-call(bf16[512,2048]{1,0:T(8,128)(2,1)S(1)} %pad_maximum_fusion.refs_0_, bf16[512,2048]{1,0:T(8,128)(2,1)S(1)} %collective-permute-done.4.refs_1_, bf16[512,2048]{1,0:T(8,128)(2,1)} %copy-done.13, bf16[512,2048]{1,0:T(8,128)(2,1)} %copy-done.24, f32[1,2048]{1,0:T(1,128)S(1)} %bitcast.51, ...), custom_call_target="tpu_custom_call" | custom-call | flops 41943040 | bytes 33554432 | tf_op jit(solution)/shard_map/pallas_call | solution.py:228
  126.8 10.8 %collective-permute-done.9 = bf16[256,2048]{1,0:T(8,128)(2,1)S(1)} collective-permute-done((bf16[256,2048]{1,0:T(8,128)(2,1)S(1)}, bf16[256,2048]{1,0:T(8,128)(2,1)S(1)}, u32[]{:S(2)}, u32[]{:S(2)}) %collective-permute-start.9) | collective-permute-done | bytes 1048608 | tf_op jit(solution)/shard_map/ppermute | solution.py:185
  146.9 9.8 %shard_map.171.d_result = bf16[2048,2048]{1,0:T(8,128)(2,1)} custom-call(bf16[512,2048]{1,0:T(8,128)(2,1)S(1)} %pad_maximum_fusion.2.refs_0_, bf16[512,2048]{1,0:T(8,128)(2,1)} %collective-permute-done.10.refs_1_, bf16[512,2048]{1,0:T(8,128)(2,1)} %pad_maximum_fusion.3.refs_2_, bf16[512,2048]{1,0:T(8,128)(2,1)} %collective-permute-done.11.refs_3_), custom_call_target="tpu_custom_call" | custom-call | flops 41943040 | bytes 33554432 | tf_op jit(solution)/shard_map/pallas_call | solution.py:228
  162.9 16.2 %all_to_all.30 = bf16[8,64,768]{2,1,0:T(8,128)(2,1)} all-to-all(bf16[8,64,768]{2,1,0:T(8,128)(2,1)S(1)} %shard_map.174), channel_id=1, replica_groups=mesh['grp'=4,'tok'=8] {'tok'}, dimensions={0} | all-to-all | bytes 1572864 | tf_op jit(solution)/shard_map/all_to_all | solution.py:394
  179.0 17.8 %all-gather.6.cloned.1.call-done.up_weight.refs_3_ = bf16[2048,1408]{1,0:T(8,128)(2,1)} async-done(((bf16[512,1408]{1,0:T(8,128)(2,1)}), bf16[2048,1408]{1,0:T(8,128)(2,1)}) %all-gather.6.cloned.1.call-update) | async-done | bytes 5767184 | tf_op jit(solution)/shard_map/all_gather | solution.py:386
  199.1 28.2 %shard_map.172 = (bf16[2048,704]{1,0:T(8,128)(2,1)S(1)}, bf16[2048,1408]{1,0:T(8,128)(2,1)}) custom-call(bf16[2048,2048]{1,0:T(8,128)(2,1)} %shard_map.170.hidden.left, bf16[2048,2048]{1,0:T(8,128)(2,1)} %shard_map.171.d_result, bf16[2048,1408]{1,0:T(8,128)(2,1)} %all-gather.6.cloned.1.call-done.up_weight.refs_3_, bf16[704,2048]{1,0:T(8,128)(2,1)S(1)} %bitcast.47), custom_call_target="tpu_custom_call" | custom-call | tf_op jit(solution)/shard_map/pallas_call | solution.py:297
  228.9 17.7 %shard_map.173 = bf16[2048,1408]{1,0:T(8,128)(2,1)S(1)} custom-call(bf16[2048,2048]{1,0:T(8,128)(2,1)} %shard_map.170.hidden.left, bf16[2048,1408]{1,0:T(8,128)(2,1)} %get-tuple-element.105.right.refs_1_), custom_call_target="tpu_custom_call" | custom-call | tf_op jit(solution)/shard_map/pallas_call | solution.py:322
  249.1 11.2 %all-gather.8.cloned.1.call-done.refs_2_ = bf16[2048,768]{1,0:T(8,128)(2,1)} async-done(((bf16[512,768]{1,0:T(8,128)(2,1)}), bf16[2048,768]{1,0:T(8,128)(2,1)}) %all-gather.8.cloned.1.call-update) | async-done | bytes 3145744 | tf_op jit(solution)/shard_map/all_gather | solution.py:386
  260.3 11.8 %fusion.29.joint = f32[2048,768]{1,0:T(8,128)} fusion(bf16[2048,2048]{1,0:T(8,128)(2,1)} %shard_map.170.hidden.left, bf16[2048,768]{1,0:T(8,128)(2,1)} %all-gather.8.cloned.1.call-done.refs_2_), kind=kOutput, calls=%fused_computation.78 | convolution fusion | flops 6442450944 | bytes 17825792 | tf_op jit(solution)/shard_map/dot_general | solution.py:27
  272.1 60.0 %shard_map.175 = (bf16[2048,256]{1,0:T(8,128)(2,1)S(1)}, bf16[2048,768]{1,0:T(8,128)(2,1)}) custom-call(s32[16]{0:T(128)S(1)} %gather_fusion, f32[2048,768]{1,0:T(8,128)} %fusion.29.joint, bf16[2048,256]{1,0:T(8,128)(2,1)S(1)} %convolution_convert_fusion.1.d_out, f32[1152,128]{1,0:T(8,128)S(1)} %copy-done.6, f32[1152,128]{1,0:T(8,128)S(1)} %copy-done.5, ...), custom_call_target="tpu_custom_call" | custom-call | tf_op jit(solution)/shard_map/pallas_call | solution.py:152
  334.0 17.7 %shard_map.176 = bf16[2048,1024]{1,0:T(8,128)(2,1)} custom-call(bf16[2048,2048]{1,0:T(8,128)(2,1)} %shard_map.170.hidden.left, bf16[2048,768]{1,0:T(8,128)(2,1)S(1)} %copy-done.2, bf16[2048,256]{1,0:T(8,128)(2,1)S(1)} %get-tuple-element.114.attended.refs_0_, bf16[2048,2048]{1,0:T(8,128)(2,1)} %shard_map.171.d_result), custom_call_target="tpu_custom_call" | custom-call | tf_op jit(solution)/shard_map/pallas_call | solution.py:367
  351.7 15.2 %shard_map.177 = (bf16[512,2048]{1,0:T(8,128)(2,1)S(1)}, bf16[512,2048]{1,0:T(8,128)(2,1)}, bf16[512,2048]{1,0:T(8,128)(2,1)}, bf16[512,2048]{1,0:T(8,128)(2,1)}) custom-call(bf16[2048,256]{1,0:T(8,128)(2,1)S(1)} %get-tuple-element.114.attended.refs_0_, bf16[2048,704]{1,0:T(8,128)(2,1)} %copy-done.3, bf16[256,2048]{1,0:T(8,128)(2,1)S(1)} %bitcast.50, ...), custom_call_target="tpu_custom_call" | custom-call | tf_op jit(solution)/shard_map/pallas_call | solution.py:268
  367.5 6.6 %collective-permute-done.12 = bf16[512,2048]{1,0:T(8,128)(2,1)S(1)} collective-permute-done((bf16[512,2048]{1,0:T(8,128)(2,1)S(1)}, bf16[512,2048]{1,0:T(8,128)(2,1)S(1)}, u32[]{:S(2)}, u32[]{:S(2)}) %collective-permute-start.12) | collective-permute-done | bytes 2097184 | tf_op jit(solution)/shard_map/ppermute | solution.py:340
  383.4 29.1 %shard_map.178 = (bf16[512,2048]{1,0:T(8,128)(2,1)S(1)}, bf16[512,2048]{1,0:T(8,128)(2,1)}, bf16[512,2048]{1,0:T(8,128)(2,1)}, bf16[512,2048]{1,0:T(8,128)(2,1)}) custom-call(bf16[2048,768]{1,0:T(8,128)(2,1)} %get-tuple-element.124.d_joint.refs_0_, bf16[2048,1408]{1,0:T(8,128)(2,1)} %get-tuple-element.105.right.refs_1_, ...), custom_call_target="tpu_custom_call" | custom-call | flops 17999998976 | bytes 10000000 | tf_op jit(solution)/shard_map/pallas_call | solution.py:268
  429.5 13.6 %all-to-all-done.3.source = bf16[8,64,1408]{2,1,0:T(8,128)(2,1)S(1)} async-done(((bf16[8,64,1408]{2,1,0:T(8,128)(2,1)}), bf16[8,64,1408]{2,1,0:T(8,128)(2,1)S(1)}, u32[]{:S(2)}, u32[]{:S(2)}) %all-to-all-start.3) | async-done | bytes 1441824 | tf_op jit(solution)/shard_map/all_to_all | solution.py:394
  444.2 10.9 %convolution_convert_fusion = bf16[704,2048]{1,0:T(8,128)(2,1)} fusion(bf16[2048,704]{1,0:T(8,128)(2,1)} %copy-done.3, bf16[2048,2048]{1,0:T(8,128)(2,1)} %shard_map.171.d_result), kind=kOutput, calls=%fused_computation.5 | convolution fusion | flops 5907021824 | bytes 14155776 | tf_op jit(solution)/shard_map/dot_general | solution.py:35
  455.1 10.5 %collective-permute-done.18 = bf16[256,2048]{1,0:T(8,128)(2,1)} collective-permute-done((bf16[256,2048]{1,0:T(8,128)(2,1)}, bf16[256,2048]{1,0:T(8,128)(2,1)}, u32[]{:S(2)}, u32[]{:S(2)}) %collective-permute-start.18) | collective-permute-done | bytes 1048608 | tf_op jit(solution)/shard_map/ppermute | solution.py:340
  479.3 9.0 %collective-permute-done.22 = bf16[128,2048]{1,0:T(8,128)(2,1)S(1)} collective-permute-done((bf16[128,2048]{1,0:T(8,128)(2,1)}, bf16[128,2048]{1,0:T(8,128)(2,1)S(1)}, u32[]{:S(2)}, u32[]{:S(2)}) %collective-permute-start.22) | collective-permute-done | bytes 524320 | tf_op jit(solution)/shard_map/ppermute | solution.py:340
  517.9 7.0 %all-to-all-done.5.source = bf16[8,64,768]{2,1,0:T(8,128)(2,1)S(1)} async-done(((bf16[8,64,768]{2,1,0:T(8,128)(2,1)}), bf16[8,64,768]{2,1,0:T(8,128)(2,1)S(1)}, u32[]{:S(2)}, u32[]{:S(2)}) %all-to-all-start.5) | async-done | bytes 786464 | tf_op jit(solution)/shard_map/all_to_all | solution.py:394
  (223 shorter events, 146.7 us)
Async XLA Ops:
  7.2 82.2 %all-gather.4.cloned.1.call-start = ((), (), s32[]{:S(2)}) async-start(), calls=%async_computation.9 | async-start | bytes 4915200 | tf_op jit(solution)/shard_map/all_gather | solution.py:386
  10.3 14.4 %all-to-all-start.1 = ((bf16[32,2,64]{2,1,0:T(2,128)(2,1)}), bf16[32,2,64]{2,1,0:T(2,128)(2,1)S(1)}, u32[]{:S(2)}, u32[]{:S(2)}) async-start(bf16[32,2,64]{2,1,0:T(2,128)(2,1)} %broadcast_in_dim.13), calls=%async_computation.1 | async-start | bytes 32768 | tf_op jit(solution)/shard_map/all_to_all | solution.py:466
  24.7 23.2 %all-to-all-start = ((bf16[8,64,1408]{2,1,0:T(8,128)(2,1)}), bf16[8,64,1408]{2,1,0:T(8,128)(2,1)S(1)}, u32[]{:S(2)}, u32[]{:S(2)}) async-start(bf16[8,64,1408]{2,1,0:T(8,128)(2,1)} %shard_map.169), calls=%async_computation | async-start | bytes 2883584 | tf_op jit(solution)/shard_map/all_to_all | solution.py:394
  28.2 168.6 %all-gather.6.cloned.1.call-start = ((), (), s32[]{:S(2)}) async-start(), calls=%async_computation.10 | async-start | bytes 7208960 | tf_op jit(solution)/shard_map/all_gather | solution.py:386
  48.5 15.1 %collective-permute-start = (bf16[128,2048]{1,0:T(8,128)(2,1)S(1)}, bf16[128,2048]{1,0:T(8,128)(2,1)S(1)}, u32[]{:S(2)}, u32[]{:S(2)}) collective-permute-start(bf16[128,2048]{1,0:T(8,128)(2,1)S(1)} %get-tuple-element.197), channel_id=1, source_target_pairs={{0,2},{1,3},{2,0},{3,1},{4,6},{5,7},{6,4},{7,5},{8,10},{9,11},{10,... | collective-permute-start | bytes 1572872 | tf_op jit(solution)/shard_map/ppermute | solution.py:185
  60.1 26.6 %collective-permute-start.3 = (bf16[256,2048]{1,0:T(8,128)(2,1)}, bf16[256,2048]{1,0:T(8,128)(2,1)}, u32[]{:S(2)}, u32[]{:S(2)}) collective-permute-start(bf16[256,2048]{1,0:T(8,128)(2,1)} %pad_maximum_fusion.6), channel_id=1, source_target_pairs={{0,2},{1,3},{2,0},{3,1},{4,6},{5,7},{6,4},{7,5},{8,10},{9,11},{10,... | collective-permute-start | bytes 3145736 | tf_op jit(solution)/shard_map/ppermute | solution.py:185
  64.8 25.1 %collective-permute-start.1 = (bf16[256,2048]{1,0:T(8,128)(2,1)}, bf16[256,2048]{1,0:T(8,128)(2,1)}, u32[]{:S(2)}, u32[]{:S(2)}) collective-permute-start(bf16[256,2048]{1,0:T(8,128)(2,1)} %pad_maximum_fusion.5), channel_id=1, source_target_pairs={{0,4},{1,5},{2,6},{3,7},{4,0},{5,1},{6,2},{7,3},{8,12},{9,13},{10,... | collective-permute-start | bytes 3145736 | tf_op jit(solution)/shard_map/ppermute | solution.py:185
  89.4 170.8 %all-gather.8.cloned.1.call-start = ((), (), s32[]{:S(2)}) async-start(), calls=%async_computation.11 | async-start | bytes 3932160 | tf_op jit(solution)/shard_map/all_gather | solution.py:386
  100.5 14.1 %collective-permute-start.6 = (bf16[128,2048]{1,0:T(8,128)(2,1)S(1)}, bf16[128,2048]{1,0:T(8,128)(2,1)S(1)}, u32[]{:S(2)}, u32[]{:S(2)}) collective-permute-start(bf16[128,2048]{1,0:T(8,128)(2,1)S(1)} %get-tuple-element.195), channel_id=1, source_target_pairs={{0,2},{1,3},{2,0},{3,1},{4,6},{5,7},{6,4},{7,5},{8,10},{9,11},{10,... | collective-permute-start | bytes 1572872 | tf_op jit(solution)/shard_map/ppermute | solution.py:185
  113.0 24.5 %collective-permute-start.9 = (bf16[256,2048]{1,0:T(8,128)(2,1)S(1)}, bf16[256,2048]{1,0:T(8,128)(2,1)S(1)}, u32[]{:S(2)}, u32[]{:S(2)}) collective-permute-start(bf16[256,2048]{1,0:T(8,128)(2,1)S(1)} %pad_maximum_fusion.8), channel_id=1, source_target_pairs={{0,2},{1,3},{2,0},{3,1},{4,6},{5,7},{6,4},{7,5},{8,10},{9,11},{10,... | collective-permute-start | bytes 3145736 | tf_op jit(solution)/shard_map/ppermute | solution.py:185
  114.7 24.4 %collective-permute-start.7 = (bf16[256,2048]{1,0:T(8,128)(2,1)S(1)}, bf16[256,2048]{1,0:T(8,128)(2,1)S(1)}, u32[]{:S(2)}, u32[]{:S(2)}) collective-permute-start(bf16[256,2048]{1,0:T(8,128)(2,1)S(1)} %pad_maximum_fusion.7), channel_id=1, source_target_pairs={{0,4},{1,5},{2,6},{3,7},{4,0},{5,1},{6,2},{7,3},{8,12},{9,13},{10,... | collective-permute-start | bytes 3145736 | tf_op jit(solution)/shard_map/ppermute | solution.py:185
  196.9 186.5 %reduce-scatter.4.cloned.1.call-start = ((), (), s32[]{:S(2)}) async-start(), calls=%async_computation.12 | async-start | bytes 7208960 | tf_op jit(solution)/shard_map/reduce_scatter | solution.py:390
  260.3 210.7 %reduce-scatter.6.cloned.1.call-start = ((), (), s32[]{:S(2)}) async-start(), calls=%async_computation.13 | async-start | bytes 5242880 | tf_op jit(solution)/shard_map/reduce_scatter | solution.py:390
  380.4 32.6 %collective-permute-start.16 = (bf16[256,2048]{1,0:T(8,128)(2,1)}, bf16[256,2048]{1,0:T(8,128)(2,1)}, u32[]{:S(2)}, u32[]{:S(2)}) collective-permute-start(bf16[256,2048]{1,0:T(8,128)(2,1)} %get-tuple-element.121), channel_id=1, source_target_pairs={{0,4},{1,5},{2,6},{3,7},{4,0},{5,1},{6,2},{7,3},{8,12},{9,13},{10,... | collective-permute-start | bytes 3145736 | tf_op jit(solution)/shard_map/ppermute | solution.py:340
  381.9 32.7 %collective-permute-start.17 = (bf16[256,2048]{1,0:T(8,128)(2,1)}, bf16[256,2048]{1,0:T(8,128)(2,1)S(1)}, u32[]{:S(2)}, u32[]{:S(2)}) collective-permute-start(bf16[256,2048]{1,0:T(8,128)(2,1)} %get-tuple-element.123), channel_id=1, source_target_pairs={{0,2},{1,3},{2,0},{3,1},{4,6},{5,7},{6,4},{7,5},{8,10},{9,11},{10,... | collective-permute-start | bytes 3145736 | tf_op jit(solution)/shard_map/ppermute | solution.py:340
  419.9 23.2 %all-to-all-start.3 = ((bf16[8,64,1408]{2,1,0:T(8,128)(2,1)}), bf16[8,64,1408]{2,1,0:T(8,128)(2,1)S(1)}, u32[]{:S(2)}, u32[]{:S(2)}) async-start(bf16[8,64,1408]{2,1,0:T(8,128)(2,1)} %bitcast.58), calls=%async_computation.4 | async-start | bytes 2883584 | tf_op jit(solution)/shard_map/all_to_all | solution.py:394
  423.5 103.3 %reduce-scatter.8.cloned.1.call-start = ((), (), s32[]{:S(2)}) async-start(), calls=%async_computation.14 | async-start | bytes 3604480 | tf_op jit(solution)/shard_map/reduce_scatter | solution.py:390
  443.0 22.6 %collective-permute-start.18 = (bf16[256,2048]{1,0:T(8,128)(2,1)}, bf16[256,2048]{1,0:T(8,128)(2,1)}, u32[]{:S(2)}, u32[]{:S(2)}) collective-permute-start(bf16[256,2048]{1,0:T(8,128)(2,1)} %get-tuple-element.140), channel_id=1, source_target_pairs={{0,4},{1,5},{2,6},{3,7},{4,0},{5,1},{6,2},{7,3},{8,12},{9,13},{10,... | collective-permute-start | bytes 3145736 | tf_op jit(solution)/shard_map/ppermute | solution.py:340
  443.6 24.7 %collective-permute-start.19 = (bf16[256,2048]{1,0:T(8,128)(2,1)}, bf16[256,2048]{1,0:T(8,128)(2,1)}, u32[]{:S(2)}, u32[]{:S(2)}) collective-permute-start(bf16[256,2048]{1,0:T(8,128)(2,1)} %get-tuple-element.142), channel_id=1, source_target_pairs={{0,2},{1,3},{2,0},{3,1},{4,6},{5,7},{6,4},{7,5},{8,10},{9,11},{10,... | collective-permute-start | bytes 3145736 | tf_op jit(solution)/shard_map/ppermute | solution.py:340
  471.7 16.6 %collective-permute-start.22 = (bf16[128,2048]{1,0:T(8,128)(2,1)}, bf16[128,2048]{1,0:T(8,128)(2,1)S(1)}, u32[]{:S(2)}, u32[]{:S(2)}) collective-permute-start(bf16[128,2048]{1,0:T(8,128)(2,1)} %get-tuple-element.157), channel_id=1, source_target_pairs={{0,2},{1,3},{2,0},{3,1},{4,6},{5,7},{6,4},{7,5},{8,10},{9,11},{10,... | collective-permute-start | bytes 1572872 | tf_op jit(solution)/shard_map/ppermute | solution.py:340
  475.3 15.1 %collective-permute-start.23 = (bf16[128,2048]{1,0:T(8,128)(2,1)}, bf16[128,2048]{1,0:T(8,128)(2,1)S(1)}, u32[]{:S(2)}, u32[]{:S(2)}) collective-permute-start(bf16[128,2048]{1,0:T(8,128)(2,1)} %get-tuple-element.159), channel_id=1, source_target_pairs={{0,4},{1,5},{2,6},{3,7},{4,0},{5,1},{6,2},{7,3},{8,12},{9,13},{10,... | collective-permute-start | bytes 1572872 | tf_op jit(solution)/shard_map/ppermute | solution.py:340
  477.7 24.7 %collective-permute-start.20 = (bf16[128,2048]{1,0:T(8,128)(2,1)}, bf16[128,2048]{1,0:T(8,128)(2,1)}, u32[]{:S(2)}, u32[]{:S(2)}) collective-permute-start(bf16[128,2048]{1,0:T(8,128)(2,1)} %get-tuple-element.153), channel_id=1, source_target_pairs={{0,2},{1,3},{2,0},{3,1},{4,6},{5,7},{6,4},{7,5},{8,10},{9,11},{10,... | collective-permute-start | bytes 1572872 | tf_op jit(solution)/shard_map/ppermute | solution.py:340
  477.7 26.2 %collective-permute-start.21 = (bf16[128,2048]{1,0:T(8,128)(2,1)}, bf16[128,2048]{1,0:T(8,128)(2,1)}, u32[]{:S(2)}, u32[]{:S(2)}) collective-permute-start(bf16[128,2048]{1,0:T(8,128)(2,1)} %get-tuple-element.155), channel_id=1, source_target_pairs={{0,4},{1,5},{2,6},{3,7},{4,0},{5,1},{6,2},{7,3},{8,12},{9,13},{10,... | collective-permute-start | bytes 1572872 | tf_op jit(solution)/shard_map/ppermute | solution.py:340
  508.8 16.1 %all-to-all-start.5 = ((bf16[8,64,768]{2,1,0:T(8,128)(2,1)}), bf16[8,64,768]{2,1,0:T(8,128)(2,1)S(1)}, u32[]{:S(2)}, u32[]{:S(2)}) async-start(bf16[8,64,768]{2,1,0:T(8,128)(2,1)} %bitcast.56), calls=%async_computation.7 | async-start | bytes 1572864 | tf_op jit(solution)/shard_map/all_to_all | solution.py:394
  (50 other events, 443.6 us)
Sparse Core Ops, SparseCore 0:
  10.2 79.1 all-gather.3
  91.5 105.2 all-gather.5
  198.4 61.7 all-gather.7
  262.4 100.8 reduce-scatter.3
  383.5 73.7 reduce-scatter.5
  471.1 55.6 reduce-scatter.7

commit v3 on v2

--- a/solution.py
+++ b/solution.py
@@ -528,29 +528,35 @@
     flat = lambda pairs: [v for pair in pairs for v in pair]
     lefts = [after(attended, head_sums), activated]
     sums = sum_of_products(lefts, [out_w, down_w], False, halves)
-    head_sums = scatter_grp(after(head_sums, gate_up_grad, *flat(sums)))
+    head_sums = scatter_grp(after(head_sums, gate_up_grad))
     sums = scatter_step(sums, orders, last)
     gate_up_rows = swap_tok(after(gate_up_grad, *flat(sums)).reshape(toks, -1, 2 * wide))
     lefts = [after(d_joint, *flat(sums)), d_gate_up]
     d_sums = sum_of_products(lefts, [joint_w, gate_up_w], True, halves)
+    d_sums, gate_up_rows = lax.optimization_barrier((d_sums, gate_up_rows))
     sums = scatter_step(sums, orders, last - 1)
     d_sums = scatter_step(d_sums, orders, last)
-    d_sums, sums, gate_up_rows = lax.optimization_barrier((d_sums, sums, gate_up_rows))
+    d_sums, sums = lax.optimization_barrier((d_sums, sums))
     down_term = matmul_tn(after(activated, *flat(d_sums)), dy).astype(bf16)
+    for step in range(last - 2, -1, -1):
+        sums = scatter_step(sums, orders, step)
+    kept, head_sums = lax.optimization_barrier(([pair[0] for pair in d_sums], head_sums))
+    d_sums = [(k, pair[1]) for k, pair in zip(kept, d_sums)]
     d_sums = scatter_step(d_sums, orders, last - 1)
-    d_sums, sums, head_sums = lax.optimization_barrier((d_sums, sums, head_sums))
+    sums, d_sums = lax.optimization_barrier((sums, d_sums))
+    head_rows = after(head_sums[:, : 3 * span], *flat(d_sums))
+    head_rows = swap_tok(head_rows.reshape(toks, -1, 3 * span))
+    kept, head_rows = lax.optimization_barrier(([pair[0] for pair in d_sums], head_rows))
+    d_sums = [(k, pair[1]) for k, pair in zip(kept, d_sums)]
     for step in range(last - 2, -1, -1):
         d_sums = scatter_step(d_sums, orders, step)
-        sums = scatter_step(sums, orders, step)
     down_grad = scatter_grp(after(down_term, head_sums))
     d_hidden = jnp.concatenate(d_sums)
     result = (tokens.astype(f32) + jnp.concatenate(sums)).astype(bf16)
     if whole_heads:
-        joint_grad = head_sums[:, : 3 * span]
         out_grad = head_sums[:, 3 * span :].reshape(tall // HD, HD, -1)
         out_grad = out_grad.transpose(1, 0, 2).reshape(HD, width).astype(f32)
     else:
-        joint_grad = head_sums
         spread = jnp.zeros((own_heads, toks, HD, width), bf16)
         out_term = matmul_tn(attended, dy).astype(bf16).reshape(own_heads, 1, HD, width)
         spread = lax.dynamic_update_index_in_dim(spread, out_term, tok, 1)
@@ -572,14 +578,12 @@
     sums = lax.all_to_all(sums.reshape(2, devices, -1).transpose(1, 0, 2), both, 0, 0)
     sums = jnp.sum(sums, axis=0)
 
-    joint_rows = swap_tok(after(joint_grad, d_hidden, result).reshape(toks, -1, 3 * span))
-
     return (
         result,
         input_grad,
         sums[0],
         sums[1],
-        *join_columns(joint_rows, 3 * own_heads, 1),
+        *join_columns(head_rows, 3 * own_heads, 1),
         out_grad,
         *join_columns(gate_up_rows, grps, 2),
         down_grad.astype(f32),

time: 542 us -> 532 us (0.982)
  Pallas kernels: 194 us -> 180 us
    pallas_call x1, Pallas kernels: 60 us -> 46.9 us  [attention(): pl.pallas_call(attention_kernel, grid_spec=pltpu.PrefetchScalarGridSpec(n...]
    all_to_all x3, waiting for transfers between devices: 39.8 us -> 31.6 us  [swap_tok(): return lax.all_to_all(values, 'tok', 0, 0)]
    reduce_scatter x3, waiting for transfers between devices: 0.51 us -> 7.87 us  [scatter_grp(): lax.psum_scatter(values.astype(bf16), 'grp', scatter_dimension=0, tiled=T...]
    another operation x8 -> x7, other arithmetic: 11.7 us -> 12.5 us
  transfers between devices with their start and end apart: 35 -> 35, of which waited for: 22 -> 20; matrix products, arithmetic and copies ran while one was open for 17% -> 17% of each run, Pallas kernels for 36% -> 34%
where the time goes in v3:
time: 532 us; the launch traced here: 526 us
  Pallas kernels  180 us (34%)
  waiting for transfers between devices  164 us (31%)
  other arithmetic  45.8 us (9%)
  starting transfers between devices  45.1 us (8%)
  local copies, waits for them, and re-layouts  33 us (6%)
  matrix products  26.3 us (5%)
  blocking collectives  16.1 us (3%)
  between operations  15 us (3%)
    ppermute x12, waiting for transfers between devices, gather_pieces(): got = [lax.ppermute(h, 'tok', s) for h, s in zip(held, swaps)]  54.2 us
    pallas_call x1, Pallas kernels, attention(): pl.pallas_call(attention_kernel, grid_spec=pltpu.PrefetchScalarGridSpec(n...  46.9 us
    pallas_call x2, Pallas kernels, sum_of_products(): pl.pallas_call(functools.partial(sum_kernel, len(lefts), transposed), gri...  43.4 us
    ppermute x12, waiting for transfers between devices, scatter_step(): lax.ppermute(sent, 'tok', [(i, i ^ 1 << order[step]) for i in range(toks)])  34.7 us
    all_to_all x3, waiting for transfers between devices, swap_tok(): return lax.all_to_all(values, 'tok', 0, 0)  31.6 us
    all_gather x3, waiting for transfers between devices, gather_grp(): return lax.all_gather(values, 'grp', axis=0, tiled=True)  29 us
    pallas_call x1, Pallas kernels, feed_forward(): pl.pallas_call(feed_kernel, grid=(rows // QT,), in_specs=[pl.BlockSpec((Q...  28.2 us
    pallas_call x2, Pallas kernels, assemble(): pl.pallas_call(functools.partial(assemble_kernel, len(pieces), bool(norm)...  20.4 us
  transfers between devices with their start and end apart: 35, of which 20 were waited for; matrix products, arithmetic and copies ran while one was open for 17% of the time, Pallas kernels for 34%

profile of v3, /device:TPU:0, one launch (start us, length us, event | category | flops | bytes accessed | tf_op | source)
XLA Modules:
  0.0 525.6 jit_solution(6152856514819243212)
XLA Ops:
  10.3 7.3 %all-to-all-start.1 = ((bf16[32,2,64]{2,1,0:T(2,128)(2,1)}), bf16[32,2,64]{2,1,0:T(2,128)(2,1)S(1)}, u32[]{:S(2)}, u32[]{:S(2)}) async-start(bf16[32,2,64]{2,1,0:T(2,128)(2,1)} %broadcast_in_dim.13), calls=%async_computation.1 | async-start | bytes 32768 | tf_op jit(solution)/shard_map/all_to_all | solution.py:466
  28.5 19.3 %all-to-all-done = bf16[8,64,1408]{2,1,0:T(8,128)(2,1)S(1)} async-done(((bf16[8,64,1408]{2,1,0:T(8,128)(2,1)}), bf16[8,64,1408]{2,1,0:T(8,128)(2,1)S(1)}, u32[]{:S(2)}, u32[]{:S(2)}) %all-to-all-start) | async-done | bytes 1441824 | tf_op jit(solution)/shard_map/all_to_all | solution.py:394
  49.1 9.9 %collective-permute-done.2 = bf16[128,2048]{1,0:T(8,128)(2,1)S(1)} collective-permute-done((bf16[128,2048]{1,0:T(8,128)(2,1)S(1)}, bf16[128,2048]{1,0:T(8,128)(2,1)S(1)}, u32[]{:S(2)}, u32[]{:S(2)}) %collective-permute-start.2) | collective-permute-done | bytes 524320 | tf_op jit(solution)/shard_map/ppermute | solution.py:185
  73.1 13.6 %collective-permute-done.3 = bf16[256,2048]{1,0:T(8,128)(2,1)} collective-permute-done((bf16[256,2048]{1,0:T(8,128)(2,1)}, bf16[256,2048]{1,0:T(8,128)(2,1)}, u32[]{:S(2)}, u32[]{:S(2)}) %collective-permute-start.3) | collective-permute-done | bytes 1048608 | tf_op jit(solution)/shard_map/ppermute | solution.py:185
  102.0 11.0 %collective-permute-done.8 = bf16[128,2048]{1,0:T(8,128)(2,1)S(1)} collective-permute-done((bf16[128,2048]{1,0:T(8,128)(2,1)S(1)}, bf16[128,2048]{1,0:T(8,128)(2,1)S(1)}, u32[]{:S(2)}, u32[]{:S(2)}) %collective-permute-start.8) | collective-permute-done | bytes 524320 | tf_op jit(solution)/shard_map/ppermute | solution.py:185
  116.4 10.6 %shard_map.170.hidden.left = bf16[2048,2048]{1,0:T(8,128)(2,1)} custom-call(bf16[512,2048]{1,0:T(8,128)(2,1)S(1)} %pad_maximum_fusion.refs_0_, bf16[512,2048]{1,0:T(8,128)(2,1)S(1)} %collective-permute-done.4.refs_1_, bf16[512,2048]{1,0:T(8,128)(2,1)} %copy-done.16, bf16[512,2048]{1,0:T(8,128)(2,1)} %copy-done.28, f32[1,2048]{1,0:T(1,128)S(1)} %bitcast.51, ...), custom_call_target="tpu_custom_call" | custom-call | flops 41943040 | bytes 33554432 | tf_op jit(solution)/shard_map/pallas_call | solution.py:228
  126.9 10.7 %collective-permute-done.9 = bf16[256,2048]{1,0:T(8,128)(2,1)S(1)} collective-permute-done((bf16[256,2048]{1,0:T(8,128)(2,1)S(1)}, bf16[256,2048]{1,0:T(8,128)(2,1)S(1)}, u32[]{:S(2)}, u32[]{:S(2)}) %collective-permute-start.9) | collective-permute-done | bytes 1048608 | tf_op jit(solution)/shard_map/ppermute | solution.py:185
  146.9 9.8 %shard_map.171.d_result = bf16[2048,2048]{1,0:T(8,128)(2,1)} custom-call(bf16[512,2048]{1,0:T(8,128)(2,1)S(1)} %pad_maximum_fusion.2.refs_0_, bf16[512,2048]{1,0:T(8,128)(2,1)} %collective-permute-done.10.refs_1_, bf16[512,2048]{1,0:T(8,128)(2,1)} %pad_maximum_fusion.3.refs_2_, bf16[512,2048]{1,0:T(8,128)(2,1)} %collective-permute-done.11.refs_3_), custom_call_target="tpu_custom_call" | custom-call | flops 41943040 | bytes 33554432 | tf_op jit(solution)/shard_map/pallas_call | solution.py:228
  156.8 6.9 %convolution_convert_fusion.1.d_out = bf16[2048,256]{1,0:T(8,128)(2,1)} fusion(bf16[2048,2048]{1,0:T(8,128)(2,1)} %shard_map.171.d_result, bf16[256,2048]{1,0:T(8,128)(2,1)S(1)} %bitcast.49), kind=kOutput, calls=%fused_computation.9 | convolution fusion | flops 2148007936 | bytes 10485760 | tf_op jit(solution)/shard_map/dot_general | solution.py:31
  163.9 16.1 %all_to_all.30 = bf16[8,64,768]{2,1,0:T(8,128)(2,1)} all-to-all(bf16[8,64,768]{2,1,0:T(8,128)(2,1)S(1)} %shard_map.174), channel_id=1, replica_groups=mesh['grp'=4,'tok'=8] {'tok'}, dimensions={0} | all-to-all | bytes 1572864 | tf_op jit(solution)/shard_map/all_to_all | solution.py:394
  180.1 16.8 %all-gather.6.cloned.1.call-done.up_weight.refs_3_ = bf16[2048,1408]{1,0:T(8,128)(2,1)} async-done(((bf16[512,1408]{1,0:T(8,128)(2,1)}), bf16[2048,1408]{1,0:T(8,128)(2,1)}) %all-gather.6.cloned.1.call-update) | async-done | bytes 5767184 | tf_op jit(solution)/shard_map/all_gather | solution.py:386
  199.1 28.2 %shard_map.172 = (bf16[2048,704]{1,0:T(8,128)(2,1)S(1)}, bf16[2048,1408]{1,0:T(8,128)(2,1)}) custom-call(bf16[2048,2048]{1,0:T(8,128)(2,1)} %shard_map.170.hidden.left, bf16[2048,2048]{1,0:T(8,128)(2,1)} %shard_map.171.d_result, bf16[2048,1408]{1,0:T(8,128)(2,1)} %all-gather.6.cloned.1.call-done.up_weight.refs_3_, bf16[704,2048]{1,0:T(8,128)(2,1)S(1)} %bitcast.47), custom_call_target="tpu_custom_call" | custom-call | tf_op jit(solution)/shard_map/pallas_call | solution.py:297
  229.0 17.7 %shard_map.173 = bf16[2048,1408]{1,0:T(8,128)(2,1)S(1)} custom-call(bf16[2048,2048]{1,0:T(8,128)(2,1)} %shard_map.170.hidden.left, bf16[2048,1408]{1,0:T(8,128)(2,1)} %get-tuple-element.112.right.refs_1_), custom_call_target="tpu_custom_call" | custom-call | tf_op jit(solution)/shard_map/pallas_call | solution.py:322
  249.1 11.2 %all-gather.8.cloned.1.call-done.refs_2_ = bf16[2048,768]{1,0:T(8,128)(2,1)} async-done(((bf16[512,768]{1,0:T(8,128)(2,1)}), bf16[2048,768]{1,0:T(8,128)(2,1)}) %all-gather.8.cloned.1.call-update) | async-done | bytes 3145744 | tf_op jit(solution)/shard_map/all_gather | solution.py:386
  260.4 11.8 %fusion.29.joint = f32[2048,768]{1,0:T(8,128)} fusion(bf16[2048,2048]{1,0:T(8,128)(2,1)} %shard_map.170.hidden.left, bf16[2048,768]{1,0:T(8,128)(2,1)} %all-gather.8.cloned.1.call-done.refs_2_), kind=kOutput, calls=%fused_computation.78 | convolution fusion | flops 6442450944 | bytes 17825792 | tf_op jit(solution)/shard_map/dot_general | solution.py:27
  272.2 46.9 %shard_map.175 = (bf16[2048,256]{1,0:T(8,128)(2,1)S(1)}, bf16[2048,768]{1,0:T(8,128)(2,1)}) custom-call(s32[16]{0:T(128)S(1)} %gather_fusion, f32[2048,768]{1,0:T(8,128)} %fusion.29.joint, bf16[2048,256]{1,0:T(8,128)(2,1)S(1)} %copy-done.8, f32[1152,128]{1,0:T(8,128)S(1)} %copy-done.7, f32[1152,128]{1,0:T(8,128)S(1)} %copy-done.6, f32[1152,128]{1,0:T(8,128)S(1)} %copy-done.5), custom_call_target="tpu_custom_call" | custom-call | tf_op jit(solution)/shard_map/pallas_call | solution.py:152
  321.0 18.1 %shard_map.176 = bf16[2048,1024]{1,0:T(8,128)(2,1)} custom-call(bf16[2048,2048]{1,0:T(8,128)(2,1)} %shard_map.170.hidden.left, bf16[2048,768]{1,0:T(8,128)(2,1)S(1)} %copy-done.2, bf16[2048,256]{1,0:T(8,128)(2,1)S(1)} %get-tuple-element.121.attended.refs_0_, bf16[2048,2048]{1,0:T(8,128)(2,1)} %shard_map.171.d_result), custom_call_target="tpu_custom_call" | custom-call | tf_op jit(solution)/shard_map/pallas_call | solution.py:367
  339.1 15.3 %shard_map.177 = (bf16[512,2048]{1,0:T(8,128)(2,1)S(1)}, bf16[512,2048]{1,0:T(8,128)(2,1)}, bf16[512,2048]{1,0:T(8,128)(2,1)}, bf16[512,2048]{1,0:T(8,128)(2,1)}) custom-call(bf16[2048,256]{1,0:T(8,128)(2,1)S(1)} %get-tuple-element.121.attended.refs_0_, bf16[2048,704]{1,0:T(8,128)(2,1)} %copy-done.3, bf16[256,2048]{1,0:T(8,128)(2,1)S(1)} %bitcast.50, ...), custom_call_target="tpu_custom_call" | custom-call | tf_op jit(solution)/shard_map/pallas_call | solution.py:268
  354.9 6.6 %collective-permute-done.12 = bf16[512,2048]{1,0:T(8,128)(2,1)S(1)} collective-permute-done((bf16[512,2048]{1,0:T(8,128)(2,1)S(1)}, bf16[512,2048]{1,0:T(8,128)(2,1)S(1)}, u32[]{:S(2)}, u32[]{:S(2)}) %collective-permute-start.12) | collective-permute-done | bytes 2097184 | tf_op jit(solution)/shard_map/ppermute | solution.py:340
  376.7 28.0 %shard_map.178 = (bf16[512,2048]{1,0:T(8,128)(2,1)S(1)}, bf16[512,2048]{1,0:T(8,128)(2,1)S(1)}, bf16[512,2048]{1,0:T(8,128)(2,1)}, bf16[512,2048]{1,0:T(8,128)(2,1)}) custom-call(bf16[2048,768]{1,0:T(8,128)(2,1)} %get-tuple-element.131.d_joint.refs_0_, bf16[2048,1408]{1,0:T(8,128)(2,1)} %get-tuple-element.112.right.refs_1_, ...), custom_call_target="tpu_custom_call" | custom-call | flops 17999998976 | bytes 10000000 | tf_op jit(solution)/shard_map/pallas_call | solution.py:268
  426.7 7.6 %convolution_convert_fusion = bf16[704,2048]{1,0:T(8,128)(2,1)} fusion(bf16[2048,704]{1,0:T(8,128)(2,1)S(1)} %copy-done.4, bf16[2048,2048]{1,0:T(8,128)(2,1)S(1)} %bitcast.54), kind=kOutput, calls=%fused_computation.5 | convolution fusion | flops 5907021824 | bytes 14155776 | tf_op jit(solution)/shard_map/dot_general | solution.py:35
  434.9 7.9 %reduce-scatter.6.cloned.1.call-done = bf16[512,1024]{1,0:T(8,128)(2,1)} async-done(((bf16[2048,1024]{1,0:T(8,128)(2,1)}), bf16[512,1024]{1,0:T(8,128)(2,1)}) %reduce-scatter.6.cloned.1.call-update) | async-done | bytes 1048592 | tf_op jit(solution)/shard_map/reduce_scatter | solution.py:390
  443.1 18.1 %collective-permute-done.18 = bf16[128,2048]{1,0:T(8,128)(2,1)} collective-permute-done((bf16[128,2048]{1,0:T(8,128)(2,1)}, bf16[128,2048]{1,0:T(8,128)(2,1)}, u32[]{:S(2)}, u32[]{:S(2)}) %collective-permute-start.18) | collective-permute-done | bytes 524320 | tf_op jit(solution)/shard_map/ppermute | solution.py:340
  487.9 9.9 %collective-permute-done.22 = bf16[128,2048]{1,0:T(8,128)(2,1)} collective-permute-done((bf16[128,2048]{1,0:T(8,128)(2,1)}, bf16[128,2048]{1,0:T(8,128)(2,1)}, u32[]{:S(2)}, u32[]{:S(2)}) %collective-permute-start.22) | collective-permute-done | bytes 524320 | tf_op jit(solution)/shard_map/ppermute | solution.py:340
  (226 shorter events, 151.3 us)
Async XLA Ops:
  7.2 82.2 %all-gather.4.cloned.1.call-start = ((), (), s32[]{:S(2)}) async-start(), calls=%async_computation.9 | async-start | bytes 4915200 | tf_op jit(solution)/shard_map/all_gather | solution.py:386
  10.3 14.4 %all-to-all-start.1 = ((bf16[32,2,64]{2,1,0:T(2,128)(2,1)}), bf16[32,2,64]{2,1,0:T(2,128)(2,1)S(1)}, u32[]{:S(2)}, u32[]{:S(2)}) async-start(bf16[32,2,64]{2,1,0:T(2,128)(2,1)} %broadcast_in_dim.13), calls=%async_computation.1 | async-start | bytes 32768 | tf_op jit(solution)/shard_map/all_to_all | solution.py:466
  24.7 23.2 %all-to-all-start = ((bf16[8,64,1408]{2,1,0:T(8,128)(2,1)}), bf16[8,64,1408]{2,1,0:T(8,128)(2,1)S(1)}, u32[]{:S(2)}, u32[]{:S(2)}) async-start(bf16[8,64,1408]{2,1,0:T(8,128)(2,1)} %shard_map.169), calls=%async_computation | async-start | bytes 2883584 | tf_op jit(solution)/shard_map/all_to_all | solution.py:394
  28.2 168.6 %all-gather.6.cloned.1.call-start = ((), (), s32[]{:S(2)}) async-start(), calls=%async_computation.10 | async-start | bytes 7208960 | tf_op jit(solution)/shard_map/all_gather | solution.py:386
  48.5 15.1 %collective-permute-start = (bf16[128,2048]{1,0:T(8,128)(2,1)S(1)}, bf16[128,2048]{1,0:T(8,128)(2,1)S(1)}, u32[]{:S(2)}, u32[]{:S(2)}) collective-permute-start(bf16[128,2048]{1,0:T(8,128)(2,1)S(1)} %get-tuple-element.211), channel_id=1, source_target_pairs={{0,2},{1,3},{2,0},{3,1},{4,6},{5,7},{6,4},{7,5},{8,10},{9,11},{10,... | collective-permute-start | bytes 1572872 | tf_op jit(solution)/shard_map/ppermute | solution.py:185
  60.2 26.6 %collective-permute-start.3 = (bf16[256,2048]{1,0:T(8,128)(2,1)}, bf16[256,2048]{1,0:T(8,128)(2,1)}, u32[]{:S(2)}, u32[]{:S(2)}) collective-permute-start(bf16[256,2048]{1,0:T(8,128)(2,1)} %pad_maximum_fusion.6), channel_id=1, source_target_pairs={{0,2},{1,3},{2,0},{3,1},{4,6},{5,7},{6,4},{7,5},{8,10},{9,11},{10,... | collective-permute-start | bytes 3145736 | tf_op jit(solution)/shard_map/ppermute | solution.py:185
  64.8 25.1 %collective-permute-start.1 = (bf16[256,2048]{1,0:T(8,128)(2,1)}, bf16[256,2048]{1,0:T(8,128)(2,1)}, u32[]{:S(2)}, u32[]{:S(2)}) collective-permute-start(bf16[256,2048]{1,0:T(8,128)(2,1)} %pad_maximum_fusion.5), channel_id=1, source_target_pairs={{0,4},{1,5},{2,6},{3,7},{4,0},{5,1},{6,2},{7,3},{8,12},{9,13},{10,... | collective-permute-start | bytes 3145736 | tf_op jit(solution)/shard_map/ppermute | solution.py:185
  89.4 170.8 %all-gather.8.cloned.1.call-start = ((), (), s32[]{:S(2)}) async-start(), calls=%async_computation.11 | async-start | bytes 3932160 | tf_op jit(solution)/shard_map/all_gather | solution.py:386
  100.6 14.1 %collective-permute-start.6 = (bf16[128,2048]{1,0:T(8,128)(2,1)S(1)}, bf16[128,2048]{1,0:T(8,128)(2,1)S(1)}, u32[]{:S(2)}, u32[]{:S(2)}) collective-permute-start(bf16[128,2048]{1,0:T(8,128)(2,1)S(1)} %get-tuple-element.209), channel_id=1, source_target_pairs={{0,2},{1,3},{2,0},{3,1},{4,6},{5,7},{6,4},{7,5},{8,10},{9,11},{10,... | collective-permute-start | bytes 1572872 | tf_op jit(solution)/shard_map/ppermute | solution.py:185
  113.1 24.5 %collective-permute-start.9 = (bf16[256,2048]{1,0:T(8,128)(2,1)S(1)}, bf16[256,2048]{1,0:T(8,128)(2,1)S(1)}, u32[]{:S(2)}, u32[]{:S(2)}) collective-permute-start(bf16[256,2048]{1,0:T(8,128)(2,1)S(1)} %pad_maximum_fusion.8), channel_id=1, source_target_pairs={{0,2},{1,3},{2,0},{3,1},{4,6},{5,7},{6,4},{7,5},{8,10},{9,11},{10,... | collective-permute-start | bytes 3145736 | tf_op jit(solution)/shard_map/ppermute | solution.py:185
  114.8 24.4 %collective-permute-start.7 = (bf16[256,2048]{1,0:T(8,128)(2,1)S(1)}, bf16[256,2048]{1,0:T(8,128)(2,1)S(1)}, u32[]{:S(2)}, u32[]{:S(2)}) collective-permute-start(bf16[256,2048]{1,0:T(8,128)(2,1)S(1)} %pad_maximum_fusion.7), channel_id=1, source_target_pairs={{0,4},{1,5},{2,6},{3,7},{4,0},{5,1},{6,2},{7,3},{8,12},{9,13},{10,... | collective-permute-start | bytes 3145736 | tf_op jit(solution)/shard_map/ppermute | solution.py:185
  196.9 169.5 %reduce-scatter.4.cloned.1.call-start = ((), (), s32[]{:S(2)}) async-start(), calls=%async_computation.12 | async-start | bytes 7208960 | tf_op jit(solution)/shard_map/reduce_scatter | solution.py:390
  260.3 182.5 %reduce-scatter.6.cloned.1.call-start = ((), (), s32[]{:S(2)}) async-start(), calls=%async_computation.13 | async-start | bytes 5242880 | tf_op jit(solution)/shard_map/reduce_scatter | solution.py:390
  370.1 42.1 %collective-permute-start.16 = (bf16[256,2048]{1,0:T(8,128)(2,1)}, bf16[256,2048]{1,0:T(8,128)(2,1)}, u32[]{:S(2)}, u32[]{:S(2)}) collective-permute-start(bf16[256,2048]{1,0:T(8,128)(2,1)} %get-tuple-element.128), channel_id=1, source_target_pairs={{0,4},{1,5},{2,6},{3,7},{4,0},{5,1},{6,2},{7,3},{8,12},{9,13},{10,... | collective-permute-start | bytes 3145736 | tf_op jit(solution)/shard_map/ppermute | solution.py:340
  371.6 42.7 %collective-permute-start.17 = (bf16[256,2048]{1,0:T(8,128)(2,1)}, bf16[256,2048]{1,0:T(8,128)(2,1)}, u32[]{:S(2)}, u32[]{:S(2)}) collective-permute-start(bf16[256,2048]{1,0:T(8,128)(2,1)} %get-tuple-element.130), channel_id=1, source_target_pairs={{0,2},{1,3},{2,0},{3,1},{4,6},{5,7},{6,4},{7,5},{8,10},{9,11},{10,... | collective-permute-start | bytes 3145736 | tf_op jit(solution)/shard_map/ppermute | solution.py:340
  373.1 39.2 %all-to-all-start.3 = ((bf16[8,64,1408]{2,1,0:T(8,128)(2,1)}), bf16[8,64,1408]{2,1,0:T(8,128)(2,1)S(1)}, u32[]{:S(2)}, u32[]{:S(2)}) async-start(bf16[8,64,1408]{2,1,0:T(8,128)(2,1)} %bitcast.26), calls=%async_computation.4 | async-start | bytes 2883584 | tf_op jit(solution)/shard_map/all_to_all | solution.py:394
  376.7 139.5 %reduce-scatter.8.cloned.1.call-start = ((), (), s32[]{:S(2)}) async-start(), calls=%async_computation.14 | async-start | bytes 3604480 | tf_op jit(solution)/shard_map/reduce_scatter | solution.py:390
  423.2 43.5 %collective-permute-start.20 = (bf16[256,2048]{1,0:T(8,128)(2,1)}, bf16[256,2048]{1,0:T(8,128)(2,1)}, u32[]{:S(2)}, u32[]{:S(2)}) collective-permute-start(bf16[256,2048]{1,0:T(8,128)(2,1)} %get-tuple-element.158), channel_id=1, source_target_pairs={{0,4},{1,5},{2,6},{3,7},{4,0},{5,1},{6,2},{7,3},{8,12},{9,13},{10,... | collective-permute-start | bytes 3145736 | tf_op jit(solution)/shard_map/ppermute | solution.py:340
  424.7 42.1 %collective-permute-start.21 = (bf16[256,2048]{1,0:T(8,128)(2,1)}, bf16[256,2048]{1,0:T(8,128)(2,1)}, u32[]{:S(2)}, u32[]{:S(2)}) collective-permute-start(bf16[256,2048]{1,0:T(8,128)(2,1)} %get-tuple-element.160), channel_id=1, source_target_pairs={{0,2},{1,3},{2,0},{3,1},{4,6},{5,7},{6,4},{7,5},{8,10},{9,11},{10,... | collective-permute-start | bytes 3145736 | tf_op jit(solution)/shard_map/ppermute | solution.py:340
  425.3 35.8 %collective-permute-start.18 = (bf16[128,2048]{1,0:T(8,128)(2,1)}, bf16[128,2048]{1,0:T(8,128)(2,1)}, u32[]{:S(2)}, u32[]{:S(2)}) collective-permute-start(bf16[128,2048]{1,0:T(8,128)(2,1)} %get-tuple-element.151), channel_id=1, source_target_pairs={{0,2},{1,3},{2,0},{3,1},{4,6},{5,7},{6,4},{7,5},{8,10},{9,11},{10,... | collective-permute-start | bytes 1572872 | tf_op jit(solution)/shard_map/ppermute | solution.py:340
  434.4 29.1 %collective-permute-start.19 = (bf16[128,2048]{1,0:T(8,128)(2,1)}, bf16[128,2048]{1,0:T(8,128)(2,1)}, u32[]{:S(2)}, u32[]{:S(2)}) collective-permute-start(bf16[128,2048]{1,0:T(8,128)(2,1)} %get-tuple-element.153), channel_id=1, source_target_pairs={{0,4},{1,5},{2,6},{3,7},{4,0},{5,1},{6,2},{7,3},{8,12},{9,13},{10,... | collective-permute-start | bytes 1572872 | tf_op jit(solution)/shard_map/ppermute | solution.py:340
  471.2 16.7 %all-to-all-start.4 = ((bf16[8,64,768]{2,1,0:T(8,128)(2,1)}), bf16[8,64,768]{2,1,0:T(8,128)(2,1)S(1)}, u32[]{:S(2)}, u32[]{:S(2)}) async-start(bf16[8,64,768]{2,1,0:T(8,128)(2,1)} %bitcast.58), calls=%async_computation.6 | async-start | bytes 1572864 | tf_op jit(solution)/shard_map/all_to_all | solution.py:394
  474.9 23.0 %collective-permute-start.22 = (bf16[128,2048]{1,0:T(8,128)(2,1)}, bf16[128,2048]{1,0:T(8,128)(2,1)}, u32[]{:S(2)}, u32[]{:S(2)}) collective-permute-start(bf16[128,2048]{1,0:T(8,128)(2,1)} %get-tuple-element.170), channel_id=1, source_target_pairs={{0,2},{1,3},{2,0},{3,1},{4,6},{5,7},{6,4},{7,5},{8,10},{9,11},{10,... | collective-permute-start | bytes 1572872 | tf_op jit(solution)/shard_map/ppermute | solution.py:340
  477.2 22.0 %collective-permute-start.23 = (bf16[128,2048]{1,0:T(8,128)(2,1)}, bf16[128,2048]{1,0:T(8,128)(2,1)}, u32[]{:S(2)}, u32[]{:S(2)}) collective-permute-start(bf16[128,2048]{1,0:T(8,128)(2,1)} %get-tuple-element.171), channel_id=1, source_target_pairs={{0,4},{1,5},{2,6},{3,7},{4,0},{5,1},{6,2},{7,3},{8,12},{9,13},{10,... | collective-permute-start | bytes 1572872 | tf_op jit(solution)/shard_map/ppermute | solution.py:340
  (51 other events, 445.6 us)
Sparse Core Ops, SparseCore 0:
  10.2 79.1 all-gather.3
  91.5 105.2 all-gather.5
  198.4 61.7 all-gather.7
  262.4 100.8 reduce-scatter.3
  366.5 76.2 reduce-scatter.5
  445.1 56.6 reduce-scatter.7

commit v4 on v3

--- a/solution.py
+++ b/solution.py
@@ -273,7 +273,7 @@
         out_specs=[out_block(k) for k in range(outs)],
         out_shape=[jax.ShapeDtypeStruct((rows // outs, cols), bf16)] * outs,
         compiler_params=pltpu.CompilerParams(vmem_limit_bytes=48 * 2**20),
-        cost_estimate=(pl.CostEstimate(flops=18*10**9, transcendentals=0, bytes_accessed=10**7) if transposed else no_cost),
+        cost_estimate=no_cost,
     )(*lefts, *rights)
     return list(zip(found[paths:], found[:paths]))
 
@@ -378,7 +378,9 @@
         ),
         out_shape=jax.ShapeDtypeStruct((width, d_joint.shape[1] + wide), bf16),
         compiler_params=pltpu.CompilerParams(vmem_limit_bytes=48 * 2**20),
-        cost_estimate=no_cost,
+        cost_estimate=pl.CostEstimate(
+            flops=10**10, transcendentals=0, bytes_accessed=10**7
+        ),
     )(hidden, d_joint, attended, d_result)
 
 
@@ -521,35 +523,35 @@
     joint = matmul(after(hidden, gate_up_term), joint_w)
     attended, d_joint = attention(place, joint, d_attended, tables)
     last = toks.bit_length() - 2
+    flat = lambda pairs: [v for pair in pairs for v in pair]
+    sums = sum_of_products([attended, activated], [out_w, down_w], False, halves)
+    sums = scatter_step(sums, orders, last)
+    d_joint_next = after(d_joint, *flat(sums))
     if whole_heads:
-        head_sums = head_terms(hidden, d_joint, attended, dy, grps)
+        head_term = head_terms(hidden, d_joint_next, attended, dy, grps)
     else:
-        head_sums = matmul_tn(hidden, d_joint).astype(bf16)
-    flat = lambda pairs: [v for pair in pairs for v in pair]
-    lefts = [after(attended, head_sums), activated]
-    sums = sum_of_products(lefts, [out_w, down_w], False, halves)
-    head_sums = scatter_grp(after(head_sums, gate_up_grad))
-    sums = scatter_step(sums, orders, last)
-    gate_up_rows = swap_tok(after(gate_up_grad, *flat(sums)).reshape(toks, -1, 2 * wide))
-    lefts = [after(d_joint, *flat(sums)), d_gate_up]
+        head_term = matmul_tn(hidden, d_joint_next).astype(bf16)
+    head_sums = scatter_grp(after(head_term, gate_up_grad))
+    gate_up_rows = swap_tok(after(gate_up_grad, head_term).reshape(toks, -1, 2 * wide))
+    kept, gate_up_grad = lax.optimization_barrier(([pair[0] for pair in sums], gate_up_grad))
+    sums = [(k, pair[1]) for k, pair in zip(kept, sums)]
+    sums = scatter_step(sums, orders, last - 1)
+    lefts = [after(d_joint, head_term, gate_up_grad, *flat(sums)), d_gate_up]
     d_sums = sum_of_products(lefts, [joint_w, gate_up_w], True, halves)
     d_sums, gate_up_rows = lax.optimization_barrier((d_sums, gate_up_rows))
-    sums = scatter_step(sums, orders, last - 1)
     d_sums = scatter_step(d_sums, orders, last)
-    d_sums, sums = lax.optimization_barrier((d_sums, sums))
     down_term = matmul_tn(after(activated, *flat(d_sums)), dy).astype(bf16)
-    for step in range(last - 2, -1, -1):
-        sums = scatter_step(sums, orders, step)
-    kept, head_sums = lax.optimization_barrier(([pair[0] for pair in d_sums], head_sums))
-    d_sums = [(k, pair[1]) for k, pair in zip(kept, d_sums)]
     d_sums = scatter_step(d_sums, orders, last - 1)
-    sums, d_sums = lax.optimization_barrier((sums, d_sums))
-    head_rows = after(head_sums[:, : 3 * span], *flat(d_sums))
+    d_sums, head_sums = lax.optimization_barrier((d_sums, head_sums))
+    head_rows = head_sums[:, : 3 * span]
     head_rows = swap_tok(head_rows.reshape(toks, -1, 3 * span))
     kept, head_rows = lax.optimization_barrier(([pair[0] for pair in d_sums], head_rows))
     d_sums = [(k, pair[1]) for k, pair in zip(kept, d_sums)]
     for step in range(last - 2, -1, -1):
         d_sums = scatter_step(d_sums, orders, step)
+    sums, head_rows = lax.optimization_barrier((sums, head_rows))
+    for step in range(last - 2, -1, -1):
+        sums = scatter_step(sums, orders, step)
     down_grad = scatter_grp(after(down_term, head_sums))
     d_hidden = jnp.concatenate(d_sums)
     result = (tokens.astype(f32) + jnp.concatenate(sums)).astype(bf16)
@@ -576,6 +578,7 @@
     input_grad = (cotangent.astype(f32) + d_inputs).astype(bf16)
     sums = jnp.stack([jnp.sum(d_hidden * normed, axis=0), jnp.sum(d_hidden, axis=0)])
     sums = lax.all_to_all(sums.reshape(2, devices, -1).transpose(1, 0, 2), both, 0, 0)
+    sums, down_grad = lax.optimization_barrier((sums, down_grad.astype(f32)))
     sums = jnp.sum(sums, axis=0)
 
     return (
@@ -586,7 +589,7 @@
         *join_columns(head_rows, 3 * own_heads, 1),
         out_grad,
         *join_columns(gate_up_rows, grps, 2),
-        down_grad.astype(f32),
+        down_grad,
     )
 
 

time: 532 us -> 530 us (level)
    reduce_scatter x3, waiting for transfers between devices: 7.87 us -> 0.01 us  [scatter_grp(): lax.psum_scatter(values.astype(bf16), 'grp', scatter_dimension=0, tiled=T...]
    all_to_all x3, waiting for transfers between devices: 31.6 us -> 25.4 us  [swap_tok(): return lax.all_to_all(values, 'tok', 0, 0)]
    ppermute x12, waiting for transfers between devices: 34.7 us -> 40.7 us  [scatter_step(): lax.ppermute(sent, 'tok', [(i, i ^ 1 << order[step]) for i in range(toks)])]
    all_to_all x1, waiting for transfers between devices: 1.11 us -> 6.71 us  [body(): lax.all_to_all(sums.reshape(2, devices, -1).transpose(1, 0, 2), both, 0, 0)]
  transfers between devices with their start and end apart: 35 -> 35, of which waited for: 20 -> 22; matrix products, arithmetic and copies ran while one was open for 17% -> 17% of each run, Pallas kernels for 34% -> 34%
where the time goes in v4:
time: 530 us; the launch traced here: 524 us
  Pallas kernels  180 us (34%)
  waiting for transfers between devices  163 us (31%)
  starting transfers between devices  46.9 us (9%)
  other arithmetic  42 us (8%)
  local copies, waits for them, and re-layouts  33.2 us (6%)
  matrix products  27.5 us (5%)
  blocking collectives  16.1 us (3%)
  between operations  15 us (3%)
    ppermute x12, waiting for transfers between devices, gather_pieces(): got = [lax.ppermute(h, 'tok', s) for h, s in zip(held, swaps)]  54.2 us
    pallas_call x1, Pallas kernels, attention(): pl.pallas_call(attention_kernel, grid_spec=pltpu.PrefetchScalarGridSpec(n...  47 us
    pallas_call x2, Pallas kernels, sum_of_products(): pl.pallas_call(functools.partial(sum_kernel, len(lefts), transposed), gri...  43.7 us
    ppermute x12, waiting for transfers between devices, scatter_step(): lax.ppermute(sent, 'tok', [(i, i ^ 1 << order[step]) for i in range(toks)])  40.7 us
    all_gather x3, waiting for transfers between devices, gather_grp(): return lax.all_gather(values, 'grp', axis=0, tiled=True)  30.1 us
    pallas_call x1, Pallas kernels, feed_forward(): pl.pallas_call(feed_kernel, grid=(rows // QT,), in_specs=[pl.BlockSpec((Q...  28.2 us
    all_to_all x3, waiting for transfers between devices, swap_tok(): return lax.all_to_all(values, 'tok', 0, 0)  25.4 us
    pallas_call x2, Pallas kernels, assemble(): pl.pallas_call(functools.partial(assemble_kernel, len(pieces), bool(norm)...  20.4 us
  transfers between devices with their start and end apart: 35, of which 22 were waited for; matrix products, arithmetic and copies ran while one was open for 17% of the time, Pallas kernels for 34%

profile of v4, /device:TPU:0, one launch (start us, length us, event | category | flops | bytes accessed | tf_op | source)
XLA Modules:
  0.0 523.8 jit_solution(8948907155749182674)
XLA Ops:
  10.3 7.3 %all-to-all-start.1 = ((bf16[32,2,64]{2,1,0:T(2,128)(2,1)}), bf16[32,2,64]{2,1,0:T(2,128)(2,1)S(1)}, u32[]{:S(2)}, u32[]{:S(2)}) async-start(bf16[32,2,64]{2,1,0:T(2,128)(2,1)} %broadcast_in_dim.13), calls=%async_computation.1 | async-start | bytes 32768 | tf_op jit(solution)/shard_map/all_to_all | solution.py:468
  28.5 19.3 %all-to-all-done = bf16[8,64,1408]{2,1,0:T(8,128)(2,1)S(1)} async-done(((bf16[8,64,1408]{2,1,0:T(8,128)(2,1)}), bf16[8,64,1408]{2,1,0:T(8,128)(2,1)S(1)}, u32[]{:S(2)}, u32[]{:S(2)}) %all-to-all-start) | async-done | bytes 1441824 | tf_op jit(solution)/shard_map/all_to_all | solution.py:396
  49.1 9.9 %collective-permute-done.2 = bf16[128,2048]{1,0:T(8,128)(2,1)S(1)} collective-permute-done((bf16[128,2048]{1,0:T(8,128)(2,1)S(1)}, bf16[128,2048]{1,0:T(8,128)(2,1)S(1)}, u32[]{:S(2)}, u32[]{:S(2)}) %collective-permute-start.2) | collective-permute-done | bytes 524320 | tf_op jit(solution)/shard_map/ppermute | solution.py:185
  73.1 13.6 %collective-permute-done.3 = bf16[256,2048]{1,0:T(8,128)(2,1)} collective-permute-done((bf16[256,2048]{1,0:T(8,128)(2,1)}, bf16[256,2048]{1,0:T(8,128)(2,1)}, u32[]{:S(2)}, u32[]{:S(2)}) %collective-permute-start.3) | collective-permute-done | bytes 1048608 | tf_op jit(solution)/shard_map/ppermute | solution.py:185
  102.0 11.0 %collective-permute-done.8 = bf16[128,2048]{1,0:T(8,128)(2,1)S(1)} collective-permute-done((bf16[128,2048]{1,0:T(8,128)(2,1)S(1)}, bf16[128,2048]{1,0:T(8,128)(2,1)S(1)}, u32[]{:S(2)}, u32[]{:S(2)}) %collective-permute-start.8) | collective-permute-done | bytes 524320 | tf_op jit(solution)/shard_map/ppermute | solution.py:185
  116.4 10.6 %shard_map.170.hidden.left = bf16[2048,2048]{1,0:T(8,128)(2,1)} custom-call(bf16[512,2048]{1,0:T(8,128)(2,1)S(1)} %pad_maximum_fusion.refs_0_, bf16[512,2048]{1,0:T(8,128)(2,1)S(1)} %collective-permute-done.4.refs_1_, bf16[512,2048]{1,0:T(8,128)(2,1)} %copy-done.15, bf16[512,2048]{1,0:T(8,128)(2,1)} %copy-done.24, f32[1,2048]{1,0:T(1,128)S(1)} %bitcast.51, ...), custom_call_target="tpu_custom_call" | custom-call | flops 41943040 | bytes 33554432 | tf_op jit(solution)/shard_map/pallas_call | solution.py:228
  127.0 10.7 %collective-permute-done.9 = bf16[256,2048]{1,0:T(8,128)(2,1)S(1)} collective-permute-done((bf16[256,2048]{1,0:T(8,128)(2,1)S(1)}, bf16[256,2048]{1,0:T(8,128)(2,1)S(1)}, u32[]{:S(2)}, u32[]{:S(2)}) %collective-permute-start.9) | collective-permute-done | bytes 1048608 | tf_op jit(solution)/shard_map/ppermute | solution.py:185
  147.0 9.7 %shard_map.171.d_result = bf16[2048,2048]{1,0:T(8,128)(2,1)} custom-call(bf16[512,2048]{1,0:T(8,128)(2,1)S(1)} %pad_maximum_fusion.2.refs_0_, bf16[512,2048]{1,0:T(8,128)(2,1)} %collective-permute-done.10.refs_1_, bf16[512,2048]{1,0:T(8,128)(2,1)} %pad_maximum_fusion.3.refs_2_, bf16[512,2048]{1,0:T(8,128)(2,1)} %collective-permute-done.11.refs_3_), custom_call_target="tpu_custom_call" | custom-call | flops 41943040 | bytes 33554432 | tf_op jit(solution)/shard_map/pallas_call | solution.py:228
  162.9 16.1 %all_to_all.30 = bf16[8,64,768]{2,1,0:T(8,128)(2,1)} all-to-all(bf16[8,64,768]{2,1,0:T(8,128)(2,1)S(1)} %shard_map.174), channel_id=1, replica_groups=mesh['grp'=4,'tok'=8] {'tok'}, dimensions={0} | all-to-all | bytes 1572864 | tf_op jit(solution)/shard_map/all_to_all | solution.py:396
  179.0 17.8 %all-gather.6.cloned.1.call-done.up_weight.refs_3_ = bf16[2048,1408]{1,0:T(8,128)(2,1)} async-done(((bf16[512,1408]{1,0:T(8,128)(2,1)}), bf16[2048,1408]{1,0:T(8,128)(2,1)}) %all-gather.6.cloned.1.call-update) | async-done | bytes 5767184 | tf_op jit(solution)/shard_map/all_gather | solution.py:388
  199.1 28.2 %shard_map.172 = (bf16[2048,704]{1,0:T(8,128)(2,1)S(1)}, bf16[2048,1408]{1,0:T(8,128)(2,1)}) custom-call(bf16[2048,2048]{1,0:T(8,128)(2,1)} %shard_map.170.hidden.left, bf16[2048,2048]{1,0:T(8,128)(2,1)} %shard_map.171.d_result, bf16[2048,1408]{1,0:T(8,128)(2,1)} %all-gather.6.cloned.1.call-done.up_weight.refs_3_, bf16[704,2048]{1,0:T(8,128)(2,1)S(1)} %bitcast.47), custom_call_target="tpu_custom_call" | custom-call | tf_op jit(solution)/shard_map/pallas_call | solution.py:297
  229.0 17.7 %shard_map.173 = bf16[2048,1408]{1,0:T(8,128)(2,1)S(1)} custom-call(bf16[2048,2048]{1,0:T(8,128)(2,1)} %shard_map.170.hidden.left, bf16[2048,1408]{1,0:T(8,128)(2,1)} %get-tuple-element.108.right.refs_1_), custom_call_target="tpu_custom_call" | custom-call | tf_op jit(solution)/shard_map/pallas_call | solution.py:322
  249.1 11.2 %all-gather.8.cloned.1.call-done.refs_2_ = bf16[2048,768]{1,0:T(8,128)(2,1)} async-done(((bf16[512,768]{1,0:T(8,128)(2,1)}), bf16[2048,768]{1,0:T(8,128)(2,1)}) %all-gather.8.cloned.1.call-update) | async-done | bytes 3145744 | tf_op jit(solution)/shard_map/all_gather | solution.py:388
  260.3 11.8 %fusion.29.joint = f32[2048,768]{1,0:T(8,128)} fusion(bf16[2048,2048]{1,0:T(8,128)(2,1)} %shard_map.170.hidden.left, bf16[2048,768]{1,0:T(8,128)(2,1)} %all-gather.8.cloned.1.call-done.refs_2_), kind=kOutput, calls=%fused_computation.78 | convolution fusion | flops 6442450944 | bytes 17825792 | tf_op jit(solution)/shard_map/dot_general | solution.py:27
  272.1 47.0 %shard_map.175 = (bf16[2048,256]{1,0:T(8,128)(2,1)S(1)}, bf16[2048,768]{1,0:T(8,128)(2,1)}) custom-call(s32[16]{0:T(128)S(1)} %gather_fusion, f32[2048,768]{1,0:T(8,128)} %fusion.29.joint, bf16[2048,256]{1,0:T(8,128)(2,1)S(1)} %convolution_convert_fusion.1.d_out, f32[1152,128]{1,0:T(8,128)S(1)} %copy-done.7, f32[1152,128]{1,0:T(8,128)S(1)} %copy-done.5, ...), custom_call_target="tpu_custom_call" | custom-call | tf_op jit(solution)/shard_map/pallas_call | solution.py:152
  319.1 15.2 %shard_map.176 = (bf16[512,2048]{1,0:T(8,128)(2,1)S(1)}, bf16[512,2048]{1,0:T(8,128)(2,1)}, bf16[512,2048]{1,0:T(8,128)(2,1)}, bf16[512,2048]{1,0:T(8,128)(2,1)}) custom-call(bf16[2048,256]{1,0:T(8,128)(2,1)S(1)} %get-tuple-element.115.refs_0_.attended, bf16[2048,704]{1,0:T(8,128)(2,1)} %copy-done.2, bf16[256,2048]{1,0:T(8,128)(2,1)S(1)} %bitcast.50, ...), custom_call_target="tpu_custom_call" | custom-call | tf_op jit(solution)/shard_map/pallas_call | solution.py:268
  334.8 6.8 %collective-permute-done.13 = bf16[512,2048]{1,0:T(8,128)(2,1)S(1)} collective-permute-done((bf16[512,2048]{1,0:T(8,128)(2,1)}, bf16[512,2048]{1,0:T(8,128)(2,1)S(1)}, u32[]{:S(2)}, u32[]{:S(2)}) %collective-permute-start.13) | collective-permute-done | bytes 2097184 | tf_op jit(solution)/shard_map/ppermute | solution.py:340
  351.5 17.7 %shard_map.177 = bf16[2048,1024]{1,0:T(8,128)(2,1)} custom-call(bf16[2048,2048]{1,0:T(8,128)(2,1)} %shard_map.170.hidden.left, bf16[2048,768]{1,0:T(8,128)(2,1)S(1)} %copy-done.4, bf16[2048,256]{1,0:T(8,128)(2,1)S(1)} %get-tuple-element.115.refs_0_.attended, bf16[2048,2048]{1,0:T(8,128)(2,1)} %shard_map.171.d_result), custom_call_target="tpu_custom_call" | custom-call | flops 10000000000 | bytes 10000000 | tf_op jit(solution)/shard_map/pallas_call | solution.py:367
  380.1 28.5 %shard_map.178 = (bf16[512,2048]{1,0:T(8,128)(2,1)S(1)}, bf16[512,2048]{1,0:T(8,128)(2,1)S(1)}, bf16[512,2048]{1,0:T(8,128)(2,1)}, bf16[512,2048]{1,0:T(8,128)(2,1)}) custom-call(bf16[2048,768]{1,0:T(8,128)(2,1)} %get-tuple-element.134.d_joint.refs_0_, bf16[2048,1408]{1,0:T(8,128)(2,1)} %get-tuple-element.108.right.refs_1_, ...), custom_call_target="tpu_custom_call" | custom-call | tf_op jit(solution)/shard_map/pallas_call | solution.py:268
  410.4 6.8 %collective-permute-done.17 = bf16[512,2048]{1,0:T(8,128)(2,1)S(1)} collective-permute-done((bf16[512,2048]{1,0:T(8,128)(2,1)}, bf16[512,2048]{1,0:T(8,128)(2,1)S(1)}, u32[]{:S(2)}, u32[]{:S(2)}) %collective-permute-start.17) | collective-permute-done | bytes 2097184 | tf_op jit(solution)/shard_map/ppermute | solution.py:340
  426.3 9.8 %convolution_convert_fusion = bf16[704,2048]{1,0:T(8,128)(2,1)} fusion(bf16[2048,704]{1,0:T(8,128)(2,1)S(1)} %copy-done.3, bf16[2048,2048]{1,0:T(8,128)(2,1)} %shard_map.171.d_result), kind=kOutput, calls=%fused_computation.5 | convolution fusion | flops 5907021824 | bytes 14155776 | tf_op jit(solution)/shard_map/dot_general | solution.py:35
  436.2 13.4 %collective-permute-done.19 = bf16[256,2048]{1,0:T(8,128)(2,1)} collective-permute-done((bf16[256,2048]{1,0:T(8,128)(2,1)}, bf16[256,2048]{1,0:T(8,128)(2,1)}, u32[]{:S(2)}, u32[]{:S(2)}) %collective-permute-start.19) | collective-permute-done | bytes 1048608 | tf_op jit(solution)/shard_map/ppermute | solution.py:340
  474.5 9.9 %collective-permute-done.22 = bf16[128,2048]{1,0:T(8,128)(2,1)} collective-permute-done((bf16[128,2048]{1,0:T(8,128)(2,1)}, bf16[128,2048]{1,0:T(8,128)(2,1)}, u32[]{:S(2)}, u32[]{:S(2)}) %collective-permute-start.22) | collective-permute-done | bytes 524320 | tf_op jit(solution)/shard_map/ppermute | solution.py:340
  498.7 6.7 %all-to-all-done.5 = f32[32,1,128]{2,1,0:T(1,128)S(1)} async-done(((f32[32,1,128]{2,1,0:T(1,128)}), f32[32,1,128]{2,1,0:T(1,128)S(1)}, u32[]{:S(2)}, u32[]{:S(2)}) %all-to-all-start.5) | async-done | bytes 16416 | tf_op jit(solution)/shard_map/all_to_all | solution.py:580
  (211 shorter events, 152.1 us)
Async XLA Ops:
  7.2 82.2 %all-gather.4.cloned.1.call-start = ((), (), s32[]{:S(2)}) async-start(), calls=%async_computation.9 | async-start | bytes 4915200 | tf_op jit(solution)/shard_map/all_gather | solution.py:388
  10.3 14.4 %all-to-all-start.1 = ((bf16[32,2,64]{2,1,0:T(2,128)(2,1)}), bf16[32,2,64]{2,1,0:T(2,128)(2,1)S(1)}, u32[]{:S(2)}, u32[]{:S(2)}) async-start(bf16[32,2,64]{2,1,0:T(2,128)(2,1)} %broadcast_in_dim.13), calls=%async_computation.1 | async-start | bytes 32768 | tf_op jit(solution)/shard_map/all_to_all | solution.py:468
  24.7 23.2 %all-to-all-start = ((bf16[8,64,1408]{2,1,0:T(8,128)(2,1)}), bf16[8,64,1408]{2,1,0:T(8,128)(2,1)S(1)}, u32[]{:S(2)}, u32[]{:S(2)}) async-start(bf16[8,64,1408]{2,1,0:T(8,128)(2,1)} %shard_map.169), calls=%async_computation | async-start | bytes 2883584 | tf_op jit(solution)/shard_map/all_to_all | solution.py:396
  28.2 168.6 %all-gather.6.cloned.1.call-start = ((), (), s32[]{:S(2)}) async-start(), calls=%async_computation.10 | async-start | bytes 7208960 | tf_op jit(solution)/shard_map/all_gather | solution.py:388
  48.5 15.1 %collective-permute-start = (bf16[128,2048]{1,0:T(8,128)(2,1)S(1)}, bf16[128,2048]{1,0:T(8,128)(2,1)S(1)}, u32[]{:S(2)}, u32[]{:S(2)}) collective-permute-start(bf16[128,2048]{1,0:T(8,128)(2,1)S(1)} %get-tuple-element.203), channel_id=1, source_target_pairs={{0,2},{1,3},{2,0},{3,1},{4,6},{5,7},{6,4},{7,5},{8,10},{9,11},{10,... | collective-permute-start | bytes 1572872 | tf_op jit(solution)/shard_map/ppermute | solution.py:185
  60.1 26.6 %collective-permute-start.3 = (bf16[256,2048]{1,0:T(8,128)(2,1)}, bf16[256,2048]{1,0:T(8,128)(2,1)}, u32[]{:S(2)}, u32[]{:S(2)}) collective-permute-start(bf16[256,2048]{1,0:T(8,128)(2,1)} %pad_maximum_fusion.6), channel_id=1, source_target_pairs={{0,2},{1,3},{2,0},{3,1},{4,6},{5,7},{6,4},{7,5},{8,10},{9,11},{10,... | collective-permute-start | bytes 3145736 | tf_op jit(solution)/shard_map/ppermute | solution.py:185
  64.8 25.2 %collective-permute-start.1 = (bf16[256,2048]{1,0:T(8,128)(2,1)}, bf16[256,2048]{1,0:T(8,128)(2,1)}, u32[]{:S(2)}, u32[]{:S(2)}) collective-permute-start(bf16[256,2048]{1,0:T(8,128)(2,1)} %pad_maximum_fusion.5), channel_id=1, source_target_pairs={{0,4},{1,5},{2,6},{3,7},{4,0},{5,1},{6,2},{7,3},{8,12},{9,13},{10,... | collective-permute-start | bytes 3145736 | tf_op jit(solution)/shard_map/ppermute | solution.py:185
  89.4 170.8 %all-gather.8.cloned.1.call-start = ((), (), s32[]{:S(2)}) async-start(), calls=%async_computation.11 | async-start | bytes 3932160 | tf_op jit(solution)/shard_map/all_gather | solution.py:388
  100.6 14.1 %collective-permute-start.6 = (bf16[128,2048]{1,0:T(8,128)(2,1)S(1)}, bf16[128,2048]{1,0:T(8,128)(2,1)S(1)}, u32[]{:S(2)}, u32[]{:S(2)}) collective-permute-start(bf16[128,2048]{1,0:T(8,128)(2,1)S(1)} %get-tuple-element.201), channel_id=1, source_target_pairs={{0,2},{1,3},{2,0},{3,1},{4,6},{5,7},{6,4},{7,5},{8,10},{9,11},{10,... | collective-permute-start | bytes 1572872 | tf_op jit(solution)/shard_map/ppermute | solution.py:185
  113.1 24.5 %collective-permute-start.9 = (bf16[256,2048]{1,0:T(8,128)(2,1)S(1)}, bf16[256,2048]{1,0:T(8,128)(2,1)S(1)}, u32[]{:S(2)}, u32[]{:S(2)}) collective-permute-start(bf16[256,2048]{1,0:T(8,128)(2,1)S(1)} %pad_maximum_fusion.8), channel_id=1, source_target_pairs={{0,2},{1,3},{2,0},{3,1},{4,6},{5,7},{6,4},{7,5},{8,10},{9,11},{10,... | collective-permute-start | bytes 3145736 | tf_op jit(solution)/shard_map/ppermute | solution.py:185
  114.8 24.5 %collective-permute-start.7 = (bf16[256,2048]{1,0:T(8,128)(2,1)S(1)}, bf16[256,2048]{1,0:T(8,128)(2,1)S(1)}, u32[]{:S(2)}, u32[]{:S(2)}) collective-permute-start(bf16[256,2048]{1,0:T(8,128)(2,1)S(1)} %pad_maximum_fusion.7), channel_id=1, source_target_pairs={{0,4},{1,5},{2,6},{3,7},{4,0},{5,1},{6,2},{7,3},{8,12},{9,13},{10,... | collective-permute-start | bytes 3145736 | tf_op jit(solution)/shard_map/ppermute | solution.py:185
  196.9 172.3 %reduce-scatter.4.cloned.1.call-start = ((), (), s32[]{:S(2)}) async-start(), calls=%async_computation.12 | async-start | bytes 7208960 | tf_op jit(solution)/shard_map/reduce_scatter | solution.py:392
  348.5 25.5 %collective-permute-start.14 = (bf16[256,2048]{1,0:T(8,128)(2,1)}, bf16[256,2048]{1,0:T(8,128)(2,1)}, u32[]{:S(2)}, u32[]{:S(2)}) collective-permute-start(bf16[256,2048]{1,0:T(8,128)(2,1)} %get-tuple-element.125), channel_id=1, source_target_pairs={{0,4},{1,5},{2,6},{3,7},{4,0},{5,1},{6,2},{7,3},{8,12},{9,13},{10,... | collective-permute-start | bytes 3145736 | tf_op jit(solution)/shard_map/ppermute | solution.py:340
  350.0 25.2 %collective-permute-start.15 = (bf16[256,2048]{1,0:T(8,128)(2,1)}, bf16[256,2048]{1,0:T(8,128)(2,1)}, u32[]{:S(2)}, u32[]{:S(2)}) collective-permute-start(bf16[256,2048]{1,0:T(8,128)(2,1)} %get-tuple-element.127), channel_id=1, source_target_pairs={{0,2},{1,3},{2,0},{3,1},{4,6},{5,7},{6,4},{7,5},{8,10},{9,11},{10,... | collective-permute-start | bytes 3145736 | tf_op jit(solution)/shard_map/ppermute | solution.py:340
  369.2 40.7 %all-to-all-start.3 = ((bf16[8,64,1408]{2,1,0:T(8,128)(2,1)}), bf16[8,64,1408]{2,1,0:T(8,128)(2,1)S(1)}, u32[]{:S(2)}, u32[]{:S(2)}) async-start(bf16[8,64,1408]{2,1,0:T(8,128)(2,1)} %bitcast.58), calls=%async_computation.4 | async-start | bytes 2883584 | tf_op jit(solution)/shard_map/all_to_all | solution.py:396
  372.8 82.2 %reduce-scatter.6.cloned.1.call-start = ((), (), s32[]{:S(2)}) async-start(), calls=%async_computation.13 | async-start | bytes 5242880 | tf_op jit(solution)/shard_map/reduce_scatter | solution.py:392
  373.3 140.5 %reduce-scatter.8.cloned.1.call-start = ((), (), s32[]{:S(2)}) async-start(), calls=%async_computation.14 | async-start | bytes 3604480 | tf_op jit(solution)/shard_map/reduce_scatter | solution.py:392
  424.0 25.6 %collective-permute-start.19 = (bf16[256,2048]{1,0:T(8,128)(2,1)}, bf16[256,2048]{1,0:T(8,128)(2,1)}, u32[]{:S(2)}, u32[]{:S(2)}) collective-permute-start(bf16[256,2048]{1,0:T(8,128)(2,1)} %get-tuple-element.147), channel_id=1, source_target_pairs={{0,2},{1,3},{2,0},{3,1},{4,6},{5,7},{6,4},{7,5},{8,10},{9,11},{10,... | collective-permute-start | bytes 3145736 | tf_op jit(solution)/shard_map/ppermute | solution.py:340
  425.8 26.4 %collective-permute-start.18 = (bf16[256,2048]{1,0:T(8,128)(2,1)}, bf16[256,2048]{1,0:T(8,128)(2,1)}, u32[]{:S(2)}, u32[]{:S(2)}) collective-permute-start(bf16[256,2048]{1,0:T(8,128)(2,1)} %get-tuple-element.145), channel_id=1, source_target_pairs={{0,4},{1,5},{2,6},{3,7},{4,0},{5,1},{6,2},{7,3},{8,12},{9,13},{10,... | collective-permute-start | bytes 3145736 | tf_op jit(solution)/shard_map/ppermute | solution.py:340
  457.8 16.8 %all-to-all-start.4 = ((bf16[8,64,768]{2,1,0:T(8,128)(2,1)}), bf16[8,64,768]{2,1,0:T(8,128)(2,1)S(1)}, u32[]{:S(2)}, u32[]{:S(2)}) async-start(bf16[8,64,768]{2,1,0:T(8,128)(2,1)} %bitcast.56), calls=%async_computation.6 | async-start | bytes 1572864 | tf_op jit(solution)/shard_map/all_to_all | solution.py:396
  461.5 23.0 %collective-permute-start.22 = (bf16[128,2048]{1,0:T(8,128)(2,1)}, bf16[128,2048]{1,0:T(8,128)(2,1)}, u32[]{:S(2)}, u32[]{:S(2)}) collective-permute-start(bf16[128,2048]{1,0:T(8,128)(2,1)} %get-tuple-element.162), channel_id=1, source_target_pairs={{0,2},{1,3},{2,0},{3,1},{4,6},{5,7},{6,4},{7,5},{8,10},{9,11},{10,... | collective-permute-start | bytes 1572872 | tf_op jit(solution)/shard_map/ppermute | solution.py:340
  463.8 22.0 %collective-permute-start.23 = (bf16[128,2048]{1,0:T(8,128)(2,1)}, bf16[128,2048]{1,0:T(8,128)(2,1)}, u32[]{:S(2)}, u32[]{:S(2)}) collective-permute-start(bf16[128,2048]{1,0:T(8,128)(2,1)} %get-tuple-element.164), channel_id=1, source_target_pairs={{0,4},{1,5},{2,6},{3,7},{4,0},{5,1},{6,2},{7,3},{8,12},{9,13},{10,... | collective-permute-start | bytes 1572872 | tf_op jit(solution)/shard_map/ppermute | solution.py:340
  490.5 16.2 %collective-permute-start.20 = (bf16[128,2048]{1,0:T(8,128)(2,1)}, bf16[128,2048]{1,0:T(8,128)(2,1)}, u32[]{:S(2)}, u32[]{:S(2)}) collective-permute-start(bf16[128,2048]{1,0:T(8,128)(2,1)} %get-tuple-element.158), channel_id=1, source_target_pairs={{0,2},{1,3},{2,0},{3,1},{4,6},{5,7},{6,4},{7,5},{8,10},{9,11},{10,... | collective-permute-start | bytes 1572872 | tf_op jit(solution)/shard_map/ppermute | solution.py:340
  495.4 14.6 %collective-permute-start.21 = (bf16[128,2048]{1,0:T(8,128)(2,1)}, bf16[128,2048]{1,0:T(8,128)(2,1)}, u32[]{:S(2)}, u32[]{:S(2)}) collective-permute-start(bf16[128,2048]{1,0:T(8,128)(2,1)} %get-tuple-element.160), channel_id=1, source_target_pairs={{0,4},{1,5},{2,6},{3,7},{4,0},{5,1},{6,2},{7,3},{8,12},{9,13},{10,... | collective-permute-start | bytes 1572872 | tf_op jit(solution)/shard_map/ppermute | solution.py:340
  (44 other events, 403.3 us)
Sparse Core Ops, SparseCore 0:
  10.2 79.1 all-gather.3
  91.5 105.2 all-gather.5
  198.4 61.7 all-gather.7
  262.4 100.8 reduce-scatter.3
  375.6 75.8 reduce-scatter.5
  455.1 55.6 reduce-scatter.7

commit v5 on v3

--- a/solution.py
+++ b/solution.py
@@ -538,18 +538,18 @@
     d_sums = scatter_step(d_sums, orders, last)
     d_sums, sums = lax.optimization_barrier((d_sums, sums))
     down_term = matmul_tn(after(activated, *flat(d_sums)), dy).astype(bf16)
-    for step in range(last - 2, -1, -1):
-        sums = scatter_step(sums, orders, step)
     kept, head_sums = lax.optimization_barrier(([pair[0] for pair in d_sums], head_sums))
     d_sums = [(k, pair[1]) for k, pair in zip(kept, d_sums)]
     d_sums = scatter_step(d_sums, orders, last - 1)
-    sums, d_sums = lax.optimization_barrier((sums, d_sums))
     head_rows = after(head_sums[:, : 3 * span], *flat(d_sums))
     head_rows = swap_tok(head_rows.reshape(toks, -1, 3 * span))
     kept, head_rows = lax.optimization_barrier(([pair[0] for pair in d_sums], head_rows))
     d_sums = [(k, pair[1]) for k, pair in zip(kept, d_sums)]
     for step in range(last - 2, -1, -1):
         d_sums = scatter_step(d_sums, orders, step)
+    sums, head_rows = lax.optimization_barrier((sums, head_rows))
+    for step in range(last - 2, -1, -1):
+        sums = scatter_step(sums, orders, step)
     down_grad = scatter_grp(after(down_term, head_sums))
     d_hidden = jnp.concatenate(d_sums)
     result = (tokens.astype(f32) + jnp.concatenate(sums)).astype(bf16)

time: 532 us -> 522 us (0.981)
  waiting for transfers between devices: 164 us -> 157 us
    ppermute x12, waiting for transfers between devices: 34.7 us -> 21 us  [scatter_step(): lax.ppermute(sent, 'tok', [(i, i ^ 1 << order[step]) for i in range(toks)])]
  transfers between devices with their start and end apart: 35 -> 35, of which waited for: 20 -> 21; matrix products, arithmetic and copies ran while one was open for 17% -> 18% of each run, Pallas kernels for 34% -> 35%
where the time goes in v5:
time: 522 us; the launch traced here: 516 us
  Pallas kernels  180 us (34%)
  waiting for transfers between devices  157 us (30%)
  starting transfers between devices  44.3 us (8%)
  other arithmetic  43.3 us (8%)
  local copies, waits for them, and re-layouts  34.3 us (7%)
  matrix products  26.3 us (5%)
  blocking collectives  16.1 us (3%)
  between operations  15 us (3%)
    ppermute x12, waiting for transfers between devices, gather_pieces(): got = [lax.ppermute(h, 'tok', s) for h, s in zip(held, swaps)]  54.2 us
    pallas_call x1, Pallas kernels, attention(): pl.pallas_call(attention_kernel, grid_spec=pltpu.PrefetchScalarGridSpec(n...  46.9 us
    pallas_call x2, Pallas kernels, sum_of_products(): pl.pallas_call(functools.partial(sum_kernel, len(lefts), transposed), gri...  43.4 us
    all_to_all x3, waiting for transfers between devices, swap_tok(): return lax.all_to_all(values, 'tok', 0, 0)  31.6 us
    all_gather x3, waiting for transfers between devices, gather_grp(): return lax.all_gather(values, 'grp', axis=0, tiled=True)  29 us
    pallas_call x1, Pallas kernels, feed_forward(): pl.pallas_call(feed_kernel, grid=(rows // QT,), in_specs=[pl.BlockSpec((Q...  28.2 us
    ppermute x12, waiting for transfers between devices, scatter_step(): lax.ppermute(sent, 'tok', [(i, i ^ 1 << order[step]) for i in range(toks)])  21 us
    pallas_call x2, Pallas kernels, assemble(): pl.pallas_call(functools.partial(assemble_kernel, len(pieces), bool(norm)...  20.4 us
  transfers between devices with their start and end apart: 35, of which 21 were waited for; matrix products, arithmetic and copies ran while one was open for 18% of the time, Pallas kernels for 35%

profile of v5, /device:TPU:0, one launch (start us, length us, event | category | flops | bytes accessed | tf_op | source)
XLA Modules:
  0.0 516.2 jit_solution(10804149028384257688)
XLA Ops:
  10.3 7.3 %all-to-all-start.1 = ((bf16[32,2,64]{2,1,0:T(2,128)(2,1)}), bf16[32,2,64]{2,1,0:T(2,128)(2,1)S(1)}, u32[]{:S(2)}, u32[]{:S(2)}) async-start(bf16[32,2,64]{2,1,0:T(2,128)(2,1)} %broadcast_in_dim.13), calls=%async_computation.1 | async-start | bytes 32768 | tf_op jit(solution)/shard_map/all_to_all | solution.py:466
  28.5 19.3 %all-to-all-done = bf16[8,64,1408]{2,1,0:T(8,128)(2,1)S(1)} async-done(((bf16[8,64,1408]{2,1,0:T(8,128)(2,1)}), bf16[8,64,1408]{2,1,0:T(8,128)(2,1)S(1)}, u32[]{:S(2)}, u32[]{:S(2)}) %all-to-all-start) | async-done | bytes 1441824 | tf_op jit(solution)/shard_map/all_to_all | solution.py:394
  49.1 9.9 %collective-permute-done.2 = bf16[128,2048]{1,0:T(8,128)(2,1)S(1)} collective-permute-done((bf16[128,2048]{1,0:T(8,128)(2,1)S(1)}, bf16[128,2048]{1,0:T(8,128)(2,1)S(1)}, u32[]{:S(2)}, u32[]{:S(2)}) %collective-permute-start.2) | collective-permute-done | bytes 524320 | tf_op jit(solution)/shard_map/ppermute | solution.py:185
  73.1 13.6 %collective-permute-done.3 = bf16[256,2048]{1,0:T(8,128)(2,1)} collective-permute-done((bf16[256,2048]{1,0:T(8,128)(2,1)}, bf16[256,2048]{1,0:T(8,128)(2,1)}, u32[]{:S(2)}, u32[]{:S(2)}) %collective-permute-start.3) | collective-permute-done | bytes 1048608 | tf_op jit(solution)/shard_map/ppermute | solution.py:185
  102.0 11.0 %collective-permute-done.8 = bf16[128,2048]{1,0:T(8,128)(2,1)S(1)} collective-permute-done((bf16[128,2048]{1,0:T(8,128)(2,1)S(1)}, bf16[128,2048]{1,0:T(8,128)(2,1)S(1)}, u32[]{:S(2)}, u32[]{:S(2)}) %collective-permute-start.8) | collective-permute-done | bytes 524320 | tf_op jit(solution)/shard_map/ppermute | solution.py:185
  116.4 10.6 %shard_map.170.hidden.left = bf16[2048,2048]{1,0:T(8,128)(2,1)} custom-call(bf16[512,2048]{1,0:T(8,128)(2,1)S(1)} %pad_maximum_fusion.refs_0_, bf16[512,2048]{1,0:T(8,128)(2,1)S(1)} %collective-permute-done.4.refs_1_, bf16[512,2048]{1,0:T(8,128)(2,1)} %copy-done.17, bf16[512,2048]{1,0:T(8,128)(2,1)} %copy-done.29, f32[1,2048]{1,0:T(1,128)S(1)} %bitcast.51, ...), custom_call_target="tpu_custom_call" | custom-call | flops 41943040 | bytes 33554432 | tf_op jit(solution)/shard_map/pallas_call | solution.py:228
  126.9 10.7 %collective-permute-done.9 = bf16[256,2048]{1,0:T(8,128)(2,1)S(1)} collective-permute-done((bf16[256,2048]{1,0:T(8,128)(2,1)S(1)}, bf16[256,2048]{1,0:T(8,128)(2,1)S(1)}, u32[]{:S(2)}, u32[]{:S(2)}) %collective-permute-start.9) | collective-permute-done | bytes 1048608 | tf_op jit(solution)/shard_map/ppermute | solution.py:185
  146.9 9.8 %shard_map.171.d_result = bf16[2048,2048]{1,0:T(8,128)(2,1)} custom-call(bf16[512,2048]{1,0:T(8,128)(2,1)S(1)} %pad_maximum_fusion.2.refs_0_, bf16[512,2048]{1,0:T(8,128)(2,1)} %collective-permute-done.10.refs_1_, bf16[512,2048]{1,0:T(8,128)(2,1)} %pad_maximum_fusion.3.refs_2_, bf16[512,2048]{1,0:T(8,128)(2,1)} %collective-permute-done.11.refs_3_), custom_call_target="tpu_custom_call" | custom-call | flops 41943040 | bytes 33554432 | tf_op jit(solution)/shard_map/pallas_call | solution.py:228
  156.8 6.9 %convolution_convert_fusion.1.d_out = bf16[2048,256]{1,0:T(8,128)(2,1)} fusion(bf16[2048,2048]{1,0:T(8,128)(2,1)} %shard_map.171.d_result, bf16[256,2048]{1,0:T(8,128)(2,1)S(1)} %bitcast.49), kind=kOutput, calls=%fused_computation.9 | convolution fusion | flops 2148007936 | bytes 10485760 | tf_op jit(solution)/shard_map/dot_general | solution.py:31
  163.9 16.1 %all_to_all.30 = bf16[8,64,768]{2,1,0:T(8,128)(2,1)} all-to-all(bf16[8,64,768]{2,1,0:T(8,128)(2,1)S(1)} %shard_map.174), channel_id=1, replica_groups=mesh['grp'=4,'tok'=8] {'tok'}, dimensions={0} | all-to-all | bytes 1572864 | tf_op jit(solution)/shard_map/all_to_all | solution.py:394
  180.1 16.7 %all-gather.6.cloned.1.call-done.up_weight.refs_3_ = bf16[2048,1408]{1,0:T(8,128)(2,1)} async-done(((bf16[512,1408]{1,0:T(8,128)(2,1)}), bf16[2048,1408]{1,0:T(8,128)(2,1)}) %all-gather.6.cloned.1.call-update) | async-done | bytes 5767184 | tf_op jit(solution)/shard_map/all_gather | solution.py:386
  199.1 28.2 %shard_map.172 = (bf16[2048,704]{1,0:T(8,128)(2,1)S(1)}, bf16[2048,1408]{1,0:T(8,128)(2,1)}) custom-call(bf16[2048,2048]{1,0:T(8,128)(2,1)} %shard_map.170.hidden.left, bf16[2048,2048]{1,0:T(8,128)(2,1)} %shard_map.171.d_result, bf16[2048,1408]{1,0:T(8,128)(2,1)} %all-gather.6.cloned.1.call-done.up_weight.refs_3_, bf16[704,2048]{1,0:T(8,128)(2,1)S(1)} %bitcast.47), custom_call_target="tpu_custom_call" | custom-call | tf_op jit(solution)/shard_map/pallas_call | solution.py:297
  229.0 17.7 %shard_map.173 = bf16[2048,1408]{1,0:T(8,128)(2,1)S(1)} custom-call(bf16[2048,2048]{1,0:T(8,128)(2,1)} %shard_map.170.hidden.left, bf16[2048,1408]{1,0:T(8,128)(2,1)} %get-tuple-element.111.right.refs_1_), custom_call_target="tpu_custom_call" | custom-call | tf_op jit(solution)/shard_map/pallas_call | solution.py:322
  249.1 11.2 %all-gather.8.cloned.1.call-done.refs_2_ = bf16[2048,768]{1,0:T(8,128)(2,1)} async-done(((bf16[512,768]{1,0:T(8,128)(2,1)}), bf16[2048,768]{1,0:T(8,128)(2,1)}) %all-gather.8.cloned.1.call-update) | async-done | bytes 3145744 | tf_op jit(solution)/shard_map/all_gather | solution.py:386
  260.4 11.8 %fusion.29.joint = f32[2048,768]{1,0:T(8,128)} fusion(bf16[2048,2048]{1,0:T(8,128)(2,1)} %shard_map.170.hidden.left, bf16[2048,768]{1,0:T(8,128)(2,1)} %all-gather.8.cloned.1.call-done.refs_2_), kind=kOutput, calls=%fused_computation.78 | convolution fusion | flops 6442450944 | bytes 17825792 | tf_op jit(solution)/shard_map/dot_general | solution.py:27
  272.2 46.9 %shard_map.175 = (bf16[2048,256]{1,0:T(8,128)(2,1)S(1)}, bf16[2048,768]{1,0:T(8,128)(2,1)}) custom-call(s32[16]{0:T(128)S(1)} %gather_fusion, f32[2048,768]{1,0:T(8,128)} %fusion.29.joint, bf16[2048,256]{1,0:T(8,128)(2,1)S(1)} %copy-done.8, f32[1152,128]{1,0:T(8,128)S(1)} %copy-done.7, f32[1152,128]{1,0:T(8,128)S(1)} %copy-done.6, f32[1152,128]{1,0:T(8,128)S(1)} %copy-done.5), custom_call_target="tpu_custom_call" | custom-call | tf_op jit(solution)/shard_map/pallas_call | solution.py:152
  321.0 18.0 %shard_map.176 = bf16[2048,1024]{1,0:T(8,128)(2,1)} custom-call(bf16[2048,2048]{1,0:T(8,128)(2,1)} %shard_map.170.hidden.left, bf16[2048,768]{1,0:T(8,128)(2,1)S(1)} %copy-done.2, bf16[2048,256]{1,0:T(8,128)(2,1)S(1)} %get-tuple-element.120.attended.refs_0_, bf16[2048,2048]{1,0:T(8,128)(2,1)} %shard_map.171.d_result), custom_call_target="tpu_custom_call" | custom-call | tf_op jit(solution)/shard_map/pallas_call | solution.py:367
  339.1 15.4 %shard_map.177 = (bf16[512,2048]{1,0:T(8,128)(2,1)S(1)}, bf16[512,2048]{1,0:T(8,128)(2,1)}, bf16[512,2048]{1,0:T(8,128)(2,1)}, bf16[512,2048]{1,0:T(8,128)(2,1)}) custom-call(bf16[2048,256]{1,0:T(8,128)(2,1)S(1)} %get-tuple-element.120.attended.refs_0_, bf16[2048,704]{1,0:T(8,128)(2,1)} %copy-done.3, bf16[256,2048]{1,0:T(8,128)(2,1)S(1)} %bitcast.50, ...), custom_call_target="tpu_custom_call" | custom-call | tf_op jit(solution)/shard_map/pallas_call | solution.py:268
  354.9 6.6 %collective-permute-done.12 = bf16[512,2048]{1,0:T(8,128)(2,1)S(1)} collective-permute-done((bf16[512,2048]{1,0:T(8,128)(2,1)S(1)}, bf16[512,2048]{1,0:T(8,128)(2,1)S(1)}, u32[]{:S(2)}, u32[]{:S(2)}) %collective-permute-start.12) | collective-permute-done | bytes 2097184 | tf_op jit(solution)/shard_map/ppermute | solution.py:340
  376.7 28.0 %shard_map.178 = (bf16[512,2048]{1,0:T(8,128)(2,1)S(1)}, bf16[512,2048]{1,0:T(8,128)(2,1)S(1)}, bf16[512,2048]{1,0:T(8,128)(2,1)}, bf16[512,2048]{1,0:T(8,128)(2,1)}) custom-call(bf16[2048,768]{1,0:T(8,128)(2,1)} %get-tuple-element.130.d_joint.refs_0_, bf16[2048,1408]{1,0:T(8,128)(2,1)} %get-tuple-element.111.right.refs_1_, ...), custom_call_target="tpu_custom_call" | custom-call | flops 17999998976 | bytes 10000000 | tf_op jit(solution)/shard_map/pallas_call | solution.py:268
  406.0 6.2 %all-to-all-done.3.source = bf16[8,64,1408]{2,1,0:T(8,128)(2,1)S(1)} async-done(((bf16[8,64,1408]{2,1,0:T(8,128)(2,1)}), bf16[8,64,1408]{2,1,0:T(8,128)(2,1)S(1)}, u32[]{:S(2)}, u32[]{:S(2)}) %all-to-all-start.3) | async-done | bytes 1441824 | tf_op jit(solution)/shard_map/all_to_all | solution.py:394
  425.5 7.7 %convolution_convert_fusion = bf16[704,2048]{1,0:T(8,128)(2,1)} fusion(bf16[2048,704]{1,0:T(8,128)(2,1)S(1)} %copy-done.4, bf16[2048,2048]{1,0:T(8,128)(2,1)S(1)} %bitcast.54), kind=kOutput, calls=%fused_computation.5 | convolution fusion | flops 5907021824 | bytes 14155776 | tf_op jit(solution)/shard_map/dot_general | solution.py:35
  433.2 9.6 %reduce-scatter.6.cloned.1.call-done = bf16[512,1024]{1,0:T(8,128)(2,1)} async-done(((bf16[2048,1024]{1,0:T(8,128)(2,1)}), bf16[512,1024]{1,0:T(8,128)(2,1)}) %reduce-scatter.6.cloned.1.call-update) | async-done | bytes 1048592 | tf_op jit(solution)/shard_map/reduce_scatter | solution.py:390
  473.7 9.3 %collective-permute-done.22 = bf16[128,2048]{1,0:T(8,128)(2,1)} collective-permute-done((bf16[128,2048]{1,0:T(8,128)(2,1)}, bf16[128,2048]{1,0:T(8,128)(2,1)}, u32[]{:S(2)}, u32[]{:S(2)}) %collective-permute-start.22) | collective-permute-done | bytes 524320 | tf_op jit(solution)/shard_map/ppermute | solution.py:340
  (224 shorter events, 152.6 us)
Async XLA Ops:
  7.2 82.2 %all-gather.4.cloned.1.call-start = ((), (), s32[]{:S(2)}) async-start(), calls=%async_computation.9 | async-start | bytes 4915200 | tf_op jit(solution)/shard_map/all_gather | solution.py:386
  10.3 14.4 %all-to-all-start.1 = ((bf16[32,2,64]{2,1,0:T(2,128)(2,1)}), bf16[32,2,64]{2,1,0:T(2,128)(2,1)S(1)}, u32[]{:S(2)}, u32[]{:S(2)}) async-start(bf16[32,2,64]{2,1,0:T(2,128)(2,1)} %broadcast_in_dim.13), calls=%async_computation.1 | async-start | bytes 32768 | tf_op jit(solution)/shard_map/all_to_all | solution.py:466
  24.7 23.2 %all-to-all-start = ((bf16[8,64,1408]{2,1,0:T(8,128)(2,1)}), bf16[8,64,1408]{2,1,0:T(8,128)(2,1)S(1)}, u32[]{:S(2)}, u32[]{:S(2)}) async-start(bf16[8,64,1408]{2,1,0:T(8,128)(2,1)} %shard_map.169), calls=%async_computation | async-start | bytes 2883584 | tf_op jit(solution)/shard_map/all_to_all | solution.py:394
  28.2 168.6 %all-gather.6.cloned.1.call-start = ((), (), s32[]{:S(2)}) async-start(), calls=%async_computation.10 | async-start | bytes 7208960 | tf_op jit(solution)/shard_map/all_gather | solution.py:386
  48.5 15.1 %collective-permute-start = (bf16[128,2048]{1,0:T(8,128)(2,1)S(1)}, bf16[128,2048]{1,0:T(8,128)(2,1)S(1)}, u32[]{:S(2)}, u32[]{:S(2)}) collective-permute-start(bf16[128,2048]{1,0:T(8,128)(2,1)S(1)} %get-tuple-element.209), channel_id=1, source_target_pairs={{0,2},{1,3},{2,0},{3,1},{4,6},{5,7},{6,4},{7,5},{8,10},{9,11},{10,... | collective-permute-start | bytes 1572872 | tf_op jit(solution)/shard_map/ppermute | solution.py:185
  60.2 26.6 %collective-permute-start.3 = (bf16[256,2048]{1,0:T(8,128)(2,1)}, bf16[256,2048]{1,0:T(8,128)(2,1)}, u32[]{:S(2)}, u32[]{:S(2)}) collective-permute-start(bf16[256,2048]{1,0:T(8,128)(2,1)} %pad_maximum_fusion.6), channel_id=1, source_target_pairs={{0,2},{1,3},{2,0},{3,1},{4,6},{5,7},{6,4},{7,5},{8,10},{9,11},{10,... | collective-permute-start | bytes 3145736 | tf_op jit(solution)/shard_map/ppermute | solution.py:185
  64.8 25.1 %collective-permute-start.1 = (bf16[256,2048]{1,0:T(8,128)(2,1)}, bf16[256,2048]{1,0:T(8,128)(2,1)}, u32[]{:S(2)}, u32[]{:S(2)}) collective-permute-start(bf16[256,2048]{1,0:T(8,128)(2,1)} %pad_maximum_fusion.5), channel_id=1, source_target_pairs={{0,4},{1,5},{2,6},{3,7},{4,0},{5,1},{6,2},{7,3},{8,12},{9,13},{10,... | collective-permute-start | bytes 3145736 | tf_op jit(solution)/shard_map/ppermute | solution.py:185
  89.4 170.8 %all-gather.8.cloned.1.call-start = ((), (), s32[]{:S(2)}) async-start(), calls=%async_computation.11 | async-start | bytes 3932160 | tf_op jit(solution)/shard_map/all_gather | solution.py:386
  100.6 14.1 %collective-permute-start.6 = (bf16[128,2048]{1,0:T(8,128)(2,1)S(1)}, bf16[128,2048]{1,0:T(8,128)(2,1)S(1)}, u32[]{:S(2)}, u32[]{:S(2)}) collective-permute-start(bf16[128,2048]{1,0:T(8,128)(2,1)S(1)} %get-tuple-element.207), channel_id=1, source_target_pairs={{0,2},{1,3},{2,0},{3,1},{4,6},{5,7},{6,4},{7,5},{8,10},{9,11},{10,... | collective-permute-start | bytes 1572872 | tf_op jit(solution)/shard_map/ppermute | solution.py:185
  113.1 24.5 %collective-permute-start.9 = (bf16[256,2048]{1,0:T(8,128)(2,1)S(1)}, bf16[256,2048]{1,0:T(8,128)(2,1)S(1)}, u32[]{:S(2)}, u32[]{:S(2)}) collective-permute-start(bf16[256,2048]{1,0:T(8,128)(2,1)S(1)} %pad_maximum_fusion.8), channel_id=1, source_target_pairs={{0,2},{1,3},{2,0},{3,1},{4,6},{5,7},{6,4},{7,5},{8,10},{9,11},{10,... | collective-permute-start | bytes 3145736 | tf_op jit(solution)/shard_map/ppermute | solution.py:185
  114.8 24.4 %collective-permute-start.7 = (bf16[256,2048]{1,0:T(8,128)(2,1)S(1)}, bf16[256,2048]{1,0:T(8,128)(2,1)S(1)}, u32[]{:S(2)}, u32[]{:S(2)}) collective-permute-start(bf16[256,2048]{1,0:T(8,128)(2,1)S(1)} %pad_maximum_fusion.7), channel_id=1, source_target_pairs={{0,4},{1,5},{2,6},{3,7},{4,0},{5,1},{6,2},{7,3},{8,12},{9,13},{10,... | collective-permute-start | bytes 3145736 | tf_op jit(solution)/shard_map/ppermute | solution.py:185
  196.9 169.4 %reduce-scatter.4.cloned.1.call-start = ((), (), s32[]{:S(2)}) async-start(), calls=%async_computation.12 | async-start | bytes 7208960 | tf_op jit(solution)/shard_map/reduce_scatter | solution.py:390
  260.3 182.5 %reduce-scatter.6.cloned.1.call-start = ((), (), s32[]{:S(2)}) async-start(), calls=%async_computation.13 | async-start | bytes 5242880 | tf_op jit(solution)/shard_map/reduce_scatter | solution.py:390
  370.1 42.1 %collective-permute-start.16 = (bf16[256,2048]{1,0:T(8,128)(2,1)}, bf16[256,2048]{1,0:T(8,128)(2,1)}, u32[]{:S(2)}, u32[]{:S(2)}) collective-permute-start(bf16[256,2048]{1,0:T(8,128)(2,1)} %get-tuple-element.127), channel_id=1, source_target_pairs={{0,4},{1,5},{2,6},{3,7},{4,0},{5,1},{6,2},{7,3},{8,12},{9,13},{10,... | collective-permute-start | bytes 3145736 | tf_op jit(solution)/shard_map/ppermute | solution.py:340
  371.6 42.7 %collective-permute-start.17 = (bf16[256,2048]{1,0:T(8,128)(2,1)}, bf16[256,2048]{1,0:T(8,128)(2,1)}, u32[]{:S(2)}, u32[]{:S(2)}) collective-permute-start(bf16[256,2048]{1,0:T(8,128)(2,1)} %get-tuple-element.129), channel_id=1, source_target_pairs={{0,2},{1,3},{2,0},{3,1},{4,6},{5,7},{6,4},{7,5},{8,10},{9,11},{10,... | collective-permute-start | bytes 3145736 | tf_op jit(solution)/shard_map/ppermute | solution.py:340
  373.1 39.2 %all-to-all-start.3 = ((bf16[8,64,1408]{2,1,0:T(8,128)(2,1)}), bf16[8,64,1408]{2,1,0:T(8,128)(2,1)S(1)}, u32[]{:S(2)}, u32[]{:S(2)}) async-start(bf16[8,64,1408]{2,1,0:T(8,128)(2,1)} %bitcast.26), calls=%async_computation.4 | async-start | bytes 2883584 | tf_op jit(solution)/shard_map/all_to_all | solution.py:394
  376.6 130.1 %reduce-scatter.8.cloned.1.call-start = ((), (), s32[]{:S(2)}) async-start(), calls=%async_computation.14 | async-start | bytes 3604480 | tf_op jit(solution)/shard_map/reduce_scatter | solution.py:390
  423.4 25.5 %collective-permute-start.18 = (bf16[256,2048]{1,0:T(8,128)(2,1)}, bf16[256,2048]{1,0:T(8,128)(2,1)}, u32[]{:S(2)}, u32[]{:S(2)}) collective-permute-start(bf16[256,2048]{1,0:T(8,128)(2,1)} %get-tuple-element.157), channel_id=1, source_target_pairs={{0,4},{1,5},{2,6},{3,7},{4,0},{5,1},{6,2},{7,3},{8,12},{9,13},{10,... | collective-permute-start | bytes 3145736 | tf_op jit(solution)/shard_map/ppermute | solution.py:340
  424.9 25.2 %collective-permute-start.19 = (bf16[256,2048]{1,0:T(8,128)(2,1)}, bf16[256,2048]{1,0:T(8,128)(2,1)}, u32[]{:S(2)}, u32[]{:S(2)}) collective-permute-start(bf16[256,2048]{1,0:T(8,128)(2,1)} %get-tuple-element.159), channel_id=1, source_target_pairs={{0,2},{1,3},{2,0},{3,1},{4,6},{5,7},{6,4},{7,5},{8,10},{9,11},{10,... | collective-permute-start | bytes 3145736 | tf_op jit(solution)/shard_map/ppermute | solution.py:340
  455.9 16.7 %all-to-all-start.4 = ((bf16[8,64,768]{2,1,0:T(8,128)(2,1)}), bf16[8,64,768]{2,1,0:T(8,128)(2,1)S(1)}, u32[]{:S(2)}, u32[]{:S(2)}) async-start(bf16[8,64,768]{2,1,0:T(8,128)(2,1)} %bitcast.58), calls=%async_computation.6 | async-start | bytes 1572864 | tf_op jit(solution)/shard_map/all_to_all | solution.py:394
  459.6 23.5 %collective-permute-start.22 = (bf16[128,2048]{1,0:T(8,128)(2,1)}, bf16[128,2048]{1,0:T(8,128)(2,1)}, u32[]{:S(2)}, u32[]{:S(2)}) collective-permute-start(bf16[128,2048]{1,0:T(8,128)(2,1)} %get-tuple-element.163), channel_id=1, source_target_pairs={{0,2},{1,3},{2,0},{3,1},{4,6},{5,7},{6,4},{7,5},{8,10},{9,11},{10,... | collective-permute-start | bytes 1572872 | tf_op jit(solution)/shard_map/ppermute | solution.py:340
  461.9 22.5 %collective-permute-start.23 = (bf16[128,2048]{1,0:T(8,128)(2,1)}, bf16[128,2048]{1,0:T(8,128)(2,1)}, u32[]{:S(2)}, u32[]{:S(2)}) collective-permute-start(bf16[128,2048]{1,0:T(8,128)(2,1)} %get-tuple-element.164), channel_id=1, source_target_pairs={{0,4},{1,5},{2,6},{3,7},{4,0},{5,1},{6,2},{7,3},{8,12},{9,13},{10,... | collective-permute-start | bytes 1572872 | tf_op jit(solution)/shard_map/ppermute | solution.py:340
  472.6 28.9 %collective-permute-start.20 = (bf16[128,2048]{1,0:T(8,128)(2,1)}, bf16[128,2048]{1,0:T(8,128)(2,1)}, u32[]{:S(2)}, u32[]{:S(2)}) collective-permute-start(bf16[128,2048]{1,0:T(8,128)(2,1)} %get-tuple-element.168), channel_id=1, source_target_pairs={{0,2},{1,3},{2,0},{3,1},{4,6},{5,7},{6,4},{7,5},{8,10},{9,11},{10,... | collective-permute-start | bytes 1572872 | tf_op jit(solution)/shard_map/ppermute | solution.py:340
  472.6 30.4 %collective-permute-start.21 = (bf16[128,2048]{1,0:T(8,128)(2,1)}, bf16[128,2048]{1,0:T(8,128)(2,1)}, u32[]{:S(2)}, u32[]{:S(2)}) collective-permute-start(bf16[128,2048]{1,0:T(8,128)(2,1)} %get-tuple-element.170), channel_id=1, source_target_pairs={{0,4},{1,5},{2,6},{3,7},{4,0},{5,1},{6,2},{7,3},{8,12},{9,13},{10,... | collective-permute-start | bytes 1572872 | tf_op jit(solution)/shard_map/ppermute | solution.py:340
  (50 other events, 402.8 us)
Sparse Core Ops, SparseCore 0:
  10.2 79.1 all-gather.3
  91.5 105.2 all-gather.5
  198.4 61.7 all-gather.7
  262.4 100.8 reduce-scatter.3
  366.4 76.3 reduce-scatter.5
  445.0 56.9 reduce-scatter.7
